TPU v7x, 32 devices: a whole 2x2x4 slice. The times are simulated.
32 devices in a mesh: qr: 4 (over z), qc: 4 (over x, core), grp: 2 (over y).
Axes of the slice: x: 2, y: 2, z: 4, core: 2. Of those that a mesh axis runs over, the one named last changes fastest.
Arguments:
- kohn_sham: bfloat16 [1536, 1536], P('qr', 'qc'), may hold values from -1 to 1, as said below
- pattern: int32 [24, 24], P('qr', 'qc'), may hold values from 0 to 1, as said below
- basis_centers: float32 [3, 1536], P(None, 'qr'), may hold values from 0 to 6.8
- occupations: float32 [1536], P('qr'), may hold values from 0.05 to 0.5
- atoms: float32 [4, 4, 4, 2, 1024], P(None, 'qr', 'qc', 'grp'), may hold values from -1.2 to 3.4, as said below
- neighbours: int32 [4, 4, 2, 2, 64, 1024], P('qr', 'qc', 'grp'), may hold values from 0 to 1023, as said below
- emb_atom: int32 [8192], P(('qr', 'qc', 'grp')), may hold values from 0 to 1023
- emb_dest: int32 [8192, 1], P(('qr', 'qc', 'grp')), may hold values from 0 to 3; in each aligned block of 256 rows (0 to 255, 256 to 511, ...) at most 96 rows name the same one
- emb_block: int32 [8192], P(('qr', 'qc', 'grp')), may hold values from 0 to 5
Outputs:
- sign_step: bfloat16 [1536, 1536], P(('qr', 'grp'), 'qc')
- forces: float32 [3, 4, 4, 2, 1024], P(None, 'qr', 'qc', 'grp')
Inputs may be any that keep to these rules, and one draw needn't show every extreme that they name: `kohn_sham`: zero outside the blocks that pattern marks. `pattern`: 1 on every diagonal block. `atoms`: rows 0 to 2 lie in the domain's box of edge 3.4; row 3 holds charges. `neighbours`: entry 0 of the fourth dimension is a slot, 0 to 26; entry 1 an atom of that domain. `emb_dest`: among the 256 records of one domain at most 96 name the same tile row.
All inputs are finite; a program needn't handle non-finite values.
Results may differ from a plain program's by a relative error of at most 0.012.
Values may be sent and summed in bfloat16 or wider, within the bound.
No kernel may reach another device: no remote copies, remote signals or barrier semaphores. Data moves between devices by JAX's collectives and lax.ppermute only.
A program may use at most 128 MiB of HBM per device.

v0:
```python
import functools

import jax
import jax.numpy as jnp
from jax import lax
from jax.experimental import pallas as pl
from jax.experimental.pallas import tpu as pltpu
from jax.sharding import PartitionSpec as P


BLOCK = 64
SUB, LANES = 8, 128

coulomb = 138.935
hartree_nm = 0.0529177
soften = 0.01
domain_edge = 3.4

ALL = ("qr", "qc", "grp")
VMEM = pltpu.MemorySpace.VMEM
GRANT = 16 << 20
SMEM = pltpu.MemorySpace.SMEM

LANE_PICK = lax.GatherDimensionNumbers(
    offset_dims=(),
    collapsed_slice_dims=(1,),
    start_index_map=(1,),
    operand_batching_dims=(0,),
    start_indices_batching_dims=(0,),
)


def pick_lanes(row, lane):
    return lax.gather(
        row, lane[..., None], LANE_PICK, (1, 1), mode=lax.GatherScatterMode.PROMISE_IN_BOUNDS
    )


def everyone(value, axes):
    count = 1
    for axis in (axes,) if isinstance(axes, str) else axes:
        count *= lax.axis_size(axis)
    copies = jnp.broadcast_to(value[None], (count,) + value.shape)
    return lax.all_to_all(copies, axes, split_axis=0, concat_axis=0, tiled=True)


def rotated(value, axis):
    count = lax.axis_size(axis)
    return [value] + [
        lax.ppermute(value, axis, [(i, (i + k) % count) for i in range(count)])
        for k in range(1, count)
    ]


def in_place(*values):
    return [pltpu.with_memory_space_constraint(value, pltpu.MemorySpace.HBM) for value in values]


def thirds(value):
    high = value.astype(jnp.bfloat16)
    rest = value - high.astype(jnp.float32)
    middle = rest.astype(jnp.bfloat16)
    low = (rest - middle.astype(jnp.float32)).astype(jnp.bfloat16)
    return high, middle, low


def prepare_kernel(
    matrix_ref,
    atoms_ref,
    centers_ref,
    weights_ref,
    left_ref,
    right_ref,
    packet_ref,
    matrix_buf,
    centers_buf,
    weights_buf,
    sems,
):
    order, width = left_ref.shape
    layer = lax.axis_index("grp")
    copies = [
        pltpu.make_async_copy(matrix_ref, matrix_buf, sems.at[0]),
        pltpu.make_async_copy(atoms_ref, packet_ref.at[0:4], sems.at[1]),
        pltpu.make_async_copy(centers_ref, centers_buf, sems.at[2]),
        pltpu.make_async_copy(weights_ref, weights_buf, sems.at[3]),
    ]
    for copy in copies:
        copy.start()
    copies[2].wait()
    copies[3].wait()
    lines = order // LANES
    rows = [
        centers_buf[c : c + 1, n * LANES : (n + 1) * LANES] for c in range(3) for n in range(lines)
    ]
    rows = rows + [weights_buf[n * LANES : (n + 1) * LANES].reshape(1, LANES) for n in range(lines)]
    planes = packet_ref.shape[0] - 4
    rows = rows + [jnp.zeros((1, LANES), jnp.float32)] * (planes * SUB - len(rows))
    for n in range(planes):
        packet_ref[4 + n] = jnp.concatenate(rows[n * SUB : (n + 1) * SUB], axis=0)
    copies[0].wait()
    right_ref[...] = matrix_buf[pl.ds(pl.multiple_of(layer * width, width), width), :]
    for i in range(order // width):

        @pl.when(layer == i)
        def _():
            left_ref[...] = matrix_buf[:, i * width : (i + 1) * width]

    copies[1].wait()


def prepare(width, matrix, atoms, centers, weights):
    order = matrix.shape[0]
    planes = -(-4 * (order // LANES) // SUB)
    return pl.pallas_call(
        prepare_kernel,
        out_shape=(
            jax.ShapeDtypeStruct((order, width), matrix.dtype),
            jax.ShapeDtypeStruct((width, order), matrix.dtype),
            jax.ShapeDtypeStruct((4 + planes, SUB, LANES), jnp.float32),
        ),
        in_specs=[pl.BlockSpec(memory_space=pltpu.MemorySpace.HBM)] * 4,
        out_specs=(pl.BlockSpec(memory_space=VMEM),) * 3,
        scratch_shapes=[
            pltpu.VMEM(matrix.shape, matrix.dtype),
            pltpu.VMEM(centers.shape, centers.dtype),
            pltpu.VMEM(weights.shape, weights.dtype),
            pltpu.SemaphoreType.DMA((4,)),
        ],
        cost_estimate=pl.CostEstimate(flops=10**6, bytes_accessed=10**6, transcendentals=0),
        compiler_params=pltpu.CompilerParams(vmem_limit_bytes=GRANT),
        name="prepare",
    )(*in_place(matrix, atoms, centers, weights))


def records_kernel(extent, lines, *refs):
    packet_refs = refs[:extent]
    pick_ref, dest_ref, block_ref, field_ref, force_ref = refs[extent:]
    count = pick_ref.shape[1]
    here = [lax.axis_index(axis) for axis in ALL]
    anchor = [place.astype(jnp.float32) * domain_edge for place in here]
    pick, dest, block = pick_ref[...], dest_ref[...], block_ref[...]
    lane, group = pick & (LANES - 1), pick >> 7
    behind = here[0] - dest
    behind = jnp.where(behind < 0, behind + extent, behind)
    iota = functools.partial(lax.broadcasted_iota, jnp.int32)
    one_lane = (iota((LANES, count), 0) == lane).astype(jnp.bfloat16)
    in_group = iota((SUB, count), 0) == group
    half = block >> 1
    odd = (block & 1) == 1
    one_line = (iota((extent * lines, count), 0) == behind * lines + half).astype(jnp.bfloat16)
    one_out = (iota((extent * lines, count), 0) == dest * lines + half).astype(jnp.bfloat16)

    def exact(product, value):
        high, middle, low = thirds(value)
        return product(high) + product(middle) + product(low)

    def dot(contract):
        return lambda other: lambda value: lax.dot_general(
            value, other, (contract, ((), ())), preferred_element_type=jnp.float32
        )

    own = packet_refs[0]
    atoms = jnp.concatenate([own[c] for c in range(4)], axis=0)
    spread = exact(dot(((1,), (0,)))(one_lane), atoms)
    taken = [
        jnp.sum(jnp.where(in_group, spread[c * SUB : (c + 1) * SUB], 0.0), axis=0, keepdims=True)
        for c in range(4)
    ]

    def line(k, n):
        return packet_refs[k][4 + n // SUB, n % SUB : n % SUB + 1, :]

    def chosen(c):
        table = jnp.concatenate(
            [line(k, c * lines + n) for k in range(extent) for n in range(lines)], axis=0
        )
        both = exact(dot(((0,), (0,)))(one_line), table)
        return jnp.where(odd, both[BLOCK:], both[:BLOCK])

    charge = taken[3]
    offset = [taken[c] + anchor[c] - chosen(c) for c in range(3)]
    weight = chosen(3)
    distance = offset[0] * offset[0] + offset[1] * offset[1] + offset[2] * offset[2] + soften
    inverse = lax.rsqrt(distance)
    terms = hartree_nm * charge * inverse
    terms = jnp.concatenate([jnp.where(odd, 0.0, terms), jnp.where(odd, terms, 0.0)], axis=0)
    high, middle, low = thirds(terms)
    field_ref[...] = sum(
        lax.dot_general(one_out, piece, (((1,), (1,)), ((), ())), preferred_element_type=jnp.float32)
        for piece in (high, middle, low)
    )
    strength = weight * (inverse * inverse * inverse)
    pushes = [
        coulomb * charge * jnp.sum(strength * offset[c], axis=0, keepdims=True) for c in range(3)
    ]
    pushes = jnp.concatenate([jnp.where(in_group, push, 0.0) for push in pushes], axis=0)
    total = exact(dot(((1,), (1,)))(one_lane), pushes)
    for c in range(3):
        force_ref[c] = total[c * SUB : (c + 1) * SUB]


def embedding(order, packets, pick, dest, block):
    extent, lines = len(packets), order // LANES
    return pl.pallas_call(
        functools.partial(records_kernel, extent, lines),
        out_shape=(
            jax.ShapeDtypeStruct((extent * lines, LANES), jnp.float32),
            jax.ShapeDtypeStruct((3, SUB, LANES), jnp.float32),
        ),
        in_specs=[pl.BlockSpec(memory_space=VMEM)] * (extent + 3),
        out_specs=(pl.BlockSpec(memory_space=VMEM),) * 2,
        cost_estimate=pl.CostEstimate(flops=10**7, bytes_accessed=5 * 10**6, transcendentals=0),
        compiler_params=pltpu.CompilerParams(vmem_limit_bytes=GRANT),
        name="embedding",
    )(*packets, pick, dest, block)


def field_kernel(parts_ref, rows_ref, columns_ref):
    total = parts_ref[0]
    for k in range(1, parts_ref.shape[0]):
        total = total + parts_ref[k]
    rows_ref[...] = total
    for n in range(total.shape[0]):
        columns_ref[n * LANES : (n + 1) * LANES, :] = jnp.broadcast_to(
            total[n : n + 1], (LANES, LANES)
        ).T


def whole_field(parts):
    lines = parts.shape[1]
    return pl.pallas_call(
        field_kernel,
        out_shape=(
            jax.ShapeDtypeStruct((lines, LANES), jnp.float32),
            jax.ShapeDtypeStruct((lines * LANES, LANES), jnp.float32),
        ),
        in_specs=[pl.BlockSpec(memory_space=VMEM)],
        out_specs=(pl.BlockSpec(memory_space=VMEM),) * 2,
        cost_estimate=pl.CostEstimate(flops=10**6, bytes_accessed=3 * 10**6, transcendentals=0),
        compiler_params=pltpu.CompilerParams(vmem_limit_bytes=GRANT),
        name="field",
    )(parts)


def modulo(value, count):
    return jnp.where(value < 0, value + count, value)


def keep_pattern(keep_ref, value):
    return jnp.where(keep_ref[...].astype(jnp.float32) > 0.5, value, 0.0)


def part_outputs(layers, value, hold_ref, mine_ref, send_ref):
    width = mine_ref.shape[0]
    layer = lax.axis_index("grp")
    hold_ref[...] = value
    mine_ref[...] = hold_ref[pl.ds(pl.multiple_of(layer * width, width), width), :]
    if layers == 2:
        send_ref[...] = hold_ref[
            pl.ds(pl.multiple_of((1 - layer) * width, width), width), :
        ].astype(send_ref.dtype)
    else:
        send_ref[...] = value.astype(send_ref.dtype)


def product_kernel(places, keep_ref, *refs):
    extent = len(refs) - 4 - len(places)
    left_refs, right_refs = refs[: len(places)], refs[len(places) : len(places) + extent]
    mine_ref, send_ref, table_ref, hold_ref = refs[len(places) + extent :]
    row, column = lax.axis_index("qr"), lax.axis_index("qc")
    for left_ref, place in zip(left_refs, places):
        table_ref[place(column)] = left_ref[...]
    total = jnp.zeros(hold_ref.shape, jnp.float32)
    for k in range(extent):
        total = total + jnp.dot(
            table_ref[modulo(row - k, extent)],
            right_refs[k][...],
            preferred_element_type=jnp.float32,
        )
    part_outputs(
        hold_ref.shape[0] // mine_ref.shape[0],
        keep_pattern(keep_ref, total),
        hold_ref,
        mine_ref,
        send_ref,
    )


def part_shapes(order, width):
    rows = width if order == 2 * width else order
    return (
        jax.ShapeDtypeStruct((width, order), jnp.float32),
        jax.ShapeDtypeStruct((rows, order), jnp.bfloat16),
    )


def product_part(keep, lefts, places, rights):
    order, width = lefts[0].shape
    inputs = len(lefts) + len(rights)
    return pl.pallas_call(
        functools.partial(product_kernel, places),
        out_shape=part_shapes(order, width)
        + (jax.ShapeDtypeStruct((len(lefts), order, width), jnp.bfloat16),),
        in_specs=[pl.BlockSpec(memory_space=VMEM)] * (inputs + 1),
        out_specs=(pl.BlockSpec(memory_space=VMEM),) * 3,
        scratch_shapes=[pltpu.VMEM((order, order), jnp.float32)],
        cost_estimate=pl.CostEstimate(
            flops=2 * order * order * width * len(rights),
            bytes_accessed=3 * 10**6,
            transcendentals=0,
        ),
        compiler_params=pltpu.CompilerParams(vmem_limit_bytes=GRANT),
        name="product",
    )(keep, *lefts, *rights)


def cube_kernel(keep_ref, table_ref, rows_ref, columns_ref, *refs):
    extent = (len(refs) - 3) // 2
    product_refs, right_refs = refs[:extent], refs[extent : 2 * extent]
    mine_ref, send_ref, hold_ref = refs[2 * extent :]
    width, order = mine_ref.shape
    lines = order // LANES
    row, column, layer = (lax.axis_index(axis) for axis in ALL)
    first = layer * width
    iota = functools.partial(lax.broadcasted_iota, jnp.int32)
    total = jnp.zeros((order, order), jnp.float32)
    for k in range(extent):
        tile = modulo(row - k, extent)
        down = columns_ref[pl.ds(pl.multiple_of(tile * order + first, width), width), :]
        pieces = []
        for n in range(lines):
            spot = slice(n * LANES, (n + 1) * LANES)
            across = rows_ref[pl.ds(column * lines + n, 1), :]
            matrix = right_refs[k][:, spot].astype(jnp.float32)
            on_diagonal = iota((width, LANES), 0) + first == iota((width, LANES), 1) + n * LANES
            corner = jnp.where(on_diagonal & (tile == column), down * down, 0.0)
            piece = product_refs[k][:, spot].astype(jnp.float32) + matrix * (down + across) + corner
            pieces.append(piece.astype(jnp.bfloat16))
        square = jnp.concatenate(pieces, axis=1)
        operand = table_ref[tile]
        if k == 0:
            own = columns_ref[pl.ds(pl.multiple_of(row * order, order), order), :]
            parts = []
            for start in range(0, width, LANES):
                size = min(LANES, width - start)
                shape = (order, size)
                on_diagonal = iota(shape, 0) == iota(shape, 1) + (first + start)
                parts.append(jnp.where(on_diagonal, own[:, :size], 0.0))
            added = parts[0] if len(parts) == 1 else jnp.concatenate(parts, axis=1)
            operand = (operand.astype(jnp.float32) + added).astype(jnp.bfloat16)
        total = total + jnp.dot(operand, square, preferred_element_type=jnp.float32)
    part_outputs(
        order // width, keep_pattern(keep_ref, total), hold_ref, mine_ref, send_ref
    )


def cube_part(keep, table, rows, columns, products, rights):
    _, order, width = table.shape
    inputs = 3 + len(products) + len(rights)
    return pl.pallas_call(
        cube_kernel,
        out_shape=part_shapes(order, width),
        in_specs=[pl.BlockSpec(memory_space=VMEM)] * (inputs + 1),
        out_specs=(pl.BlockSpec(memory_space=VMEM),) * 2,
        scratch_shapes=[pltpu.VMEM((order, order), jnp.float32)],
        cost_estimate=pl.CostEstimate(
            flops=2 * order * order * width * len(rights),
            bytes_accessed=3 * 10**6,
            transcendentals=0,
        ),
        compiler_params=pltpu.CompilerParams(vmem_limit_bytes=GRANT),
        name="cube",
    )(keep, table, rows, columns, *products, *rights)


def final_kernel(mine_ref, got_ref, right_ref, columns_ref, out_ref):
    width, order = mine_ref.shape
    row, column, layer = (lax.axis_index(axis) for axis in ALL)
    first = layer * width
    down = columns_ref[pl.ds(pl.multiple_of(row * order + first, width), width), :]
    iota = functools.partial(lax.broadcasted_iota, jnp.int32)
    for n in range(order // LANES):
        spot = slice(n * LANES, (n + 1) * LANES)
        on_diagonal = iota((width, LANES), 0) + first == iota((width, LANES), 1) + n * LANES
        added = jnp.where(on_diagonal & (row == column), down, 0.0)
        shifted = (right_ref[:, spot].astype(jnp.float32) + added).astype(jnp.bfloat16)
        cube = mine_ref[:, spot] + got_ref[:, spot].astype(jnp.float32)
        out_ref[:, spot] = (0.5 * (3.0 * shifted.astype(jnp.float32) - cube)).astype(jnp.bfloat16)


def final_step(mine, got, right, columns):
    return pl.pallas_call(
        final_kernel,
        out_shape=jax.ShapeDtypeStruct(mine.shape, jnp.bfloat16),
        in_specs=[pl.BlockSpec(memory_space=VMEM)] * 4,
        out_specs=pl.BlockSpec(memory_space=VMEM),
        cost_estimate=pl.CostEstimate(flops=10**6, bytes_accessed=10**6, transcendentals=0),
        compiler_params=pltpu.CompilerParams(vmem_limit_bytes=GRANT),
        name="final",
    )(mine, got, right, columns)


KEY_BITS = 8
GROUP_BITS = 3
BATCH = 8
CHUNK = 24


def packing_kernel(inner, *refs):
    *near_refs, packed_ref, scale_ref = refs
    picks = [(near_ref, i) for i in range(inner) for near_ref in near_refs]
    domains = len(picks)

    def entry(d, c):
        near_ref, i = picks[d]
        return near_ref[i, c]

    low = [entry(0, c) for c in range(4)]
    high = list(low)
    for d in range(1, domains):
        for c in range(4):
            value = entry(d, c)
            low[c] = jnp.minimum(low[c], value)
            high[c] = jnp.maximum(high[c], value)
    steps = 65535.0
    base, back = [], []
    for c in range(4):
        least = jnp.min(low[c], axis=(0, 1), keepdims=True)
        width = jnp.maximum(jnp.max(high[c], axis=(0, 1), keepdims=True) - least, 1e-30)
        base.append(jnp.broadcast_to(least, (SUB, LANES)))
        back.append(jnp.broadcast_to(steps / width, (SUB, LANES)))
        scale_ref[c] = base[c]
        scale_ref[4 + c] = jnp.broadcast_to(width * (1.0 / steps), (SUB, LANES))
    for d in range(domains):
        code = [
            jnp.clip((entry(d, c) - base[c]) * back[c] + 0.5, 0.0, steps).astype(jnp.int32)
            for c in range(4)
        ]
        start = (SUB - 1) * domains + d * SUB
        packed_ref[0, start : start + SUB, :] = code[0] | (code[1] << 16)
        packed_ref[1, start : start + SUB, :] = code[2] | (code[3] << 16)
    front, size = (SUB - 1) * domains, domains * SUB
    for w in range(2):
        packed_ref[w, :front, :] = jnp.zeros((front, LANES), jnp.int32)
        packed_ref[w, front + size :, :] = jnp.zeros((front + CHUNK, LANES), jnp.int32)


def packing(near):
    domains = len(near) * near[0].shape[0]
    rows = domains * SUB + 2 * (SUB - 1) * domains + CHUNK
    return pl.pallas_call(
        functools.partial(packing_kernel, near[0].shape[0]),
        out_shape=(
            jax.ShapeDtypeStruct((2, rows, LANES), jnp.int32),
            jax.ShapeDtypeStruct((8, SUB, LANES), jnp.float32),
        ),
        in_specs=[pl.BlockSpec(memory_space=VMEM)] * len(near),
        out_specs=(pl.BlockSpec(memory_space=VMEM),) * 2,
        cost_estimate=pl.CostEstimate(flops=10**7, bytes_accessed=5 * 10**6, transcendentals=0),
        compiler_params=pltpu.CompilerParams(vmem_limit_bytes=GRANT),
        name="packing",
    )(*near)


def compact(place, count):
    if count >= 3:
        return place
    if count == 2:
        return jnp.where(place == 1, 0, 1)
    return jnp.zeros_like(place)


def places_of(slot):
    p = (slot * 57) >> 9
    rest = slot - 9 * p
    q = (rest * 11) >> 5
    return p, q, rest - 3 * q


def network(count):
    pairs = []
    p = 1
    while p < count:
        k = p
        while k >= 1:
            for j in range(k % p, count - k, 2 * k):
                for i in range(min(k, count - j - k)):
                    if (i + j) // (2 * p) == (i + j + k) // (2 * p):
                        pairs.append((i + j, i + j + k))
            k //= 2
        p *= 2
    return pairs


def sorting_kernel(
    counts,
    lists_hbm,
    pattern_hbm,
    pick_hbm,
    dest_hbm,
    block_hbm,
    keys_ref,
    range_ref,
    keep_ref,
    pick_ref,
    dest_ref,
    block_ref,
    spread_ref,
    lists_ref,
    pattern_ref,
    sems,
):
    moves = [
        (lists_hbm, lists_ref),
        (pattern_hbm, pattern_ref),
        (pick_hbm, pick_ref),
        (dest_hbm, dest_ref),
        (block_hbm, block_ref),
    ]
    copies = [
        pltpu.make_async_copy(source, target, sems.at[i]) for i, (source, target) in enumerate(moves)
    ]
    for copy in copies:
        copy.start()
    for copy in copies:
        copy.wait()
    order, blocks = keep_ref.shape[0], pattern_ref.shape[0]
    member_of = (
        lax.broadcasted_iota(jnp.int32, (order, blocks), 0) // BLOCK
        == lax.broadcasted_iota(jnp.int32, (order, blocks), 1)
    ).astype(jnp.bfloat16)
    marks = (pattern_ref[...] == 1).astype(jnp.float32).astype(jnp.bfloat16)
    wide = jnp.dot(member_of, marks, preferred_element_type=jnp.float32).astype(jnp.bfloat16)
    keep_ref[...] = lax.dot_general(
        wide, member_of, (((1,), (1,)), ((), ())), preferred_element_type=jnp.float32
    ).astype(jnp.bfloat16)

    entries = lists_ref.shape[1]
    distinct = [min(3, count) for count in counts]
    domains = distinct[0] * distinct[1] * distinct[2]
    keys = []
    for b in range(entries // SUB):
        for a in range(SUB):
            slot = lists_ref[0, b * SUB : (b + 1) * SUB, a * LANES : (a + 1) * LANES]
            member = lists_ref[1, b * SUB : (b + 1) * SUB, a * LANES : (a + 1) * LANES]
            p, q, r = places_of(slot)
            domain = (
                compact(p, counts[0]) * distinct[1] + compact(q, counts[1])
            ) * distinct[2] + compact(r, counts[2])
            key = ((domain * (SUB * LANES) + member) << KEY_BITS) + (slot << GROUP_BITS) + a
            keys.append(key.astype(jnp.float32))
    size = len(keys)
    sublane = lax.broadcasted_iota(jnp.int32, (SUB, LANES), 0)

    def turned(values, bit):
        sign = jnp.where((sublane >> bit) & 1 == 1, -1.0, 1.0)
        return [value * sign for value in values]

    def by_sublane(values):
        for v in range(size):
            spread_ref[pl.ds(v, SUB, stride=size), :] = values[v]
        return [spread_ref[n * SUB : (n + 1) * SUB, :] for n in range(size)]

    def by_register(values):
        for n in range(size):
            spread_ref[n * SUB : (n + 1) * SUB, :] = values[n]
        return [spread_ref[pl.ds(v, SUB, stride=size), :] for v in range(size)]

    def exchange(values, i, j, up=True):
        low, high = jnp.minimum(values[i], values[j]), jnp.maximum(values[i], values[j])
        values[i], values[j] = (low, high) if up else (high, low)

    keys = turned(keys, 0)
    for i, j in network(size):
        exchange(keys, i, j)
    keys = turned(keys, 0)
    run = size // SUB
    for level in range(1, 4):
        keys = by_sublane(keys)
        for step in reversed(range(level)):
            for s in range(SUB):
                if not s >> step & 1:
                    for n in range(run):
                        exchange(
                            keys,
                            s * run + n,
                            (s | 1 << step) * run + n,
                            level == 3 or not s >> level & 1,
                        )
        keys = by_register(keys)
        if level < 3:
            keys = turned(keys, level)
        stride = size // 2
        while stride:
            for v in range(size):
                if not v & stride:
                    exchange(keys, v, v | stride)
            stride //= 2
        if level < 3:
            keys = turned(keys, level)

    whole = [key.astype(jnp.int32) for key in keys]
    for v in range(size):
        keys_ref[v] = whole[v]
    base = sublane * domains
    lows = [(whole[v] >> (KEY_BITS + 7)) - base for v in range(0, size, BATCH)]
    highs = [(whole[v + BATCH - 1] >> (KEY_BITS + 7)) - base for v in range(0, size, BATCH)]
    least = jnp.concatenate(
        [jnp.min(low.astype(jnp.float32), axis=0, keepdims=True) for low in lows], axis=0
    )
    most = jnp.concatenate(
        [jnp.max(high.astype(jnp.float32), axis=0, keepdims=True) for high in highs], axis=0
    )
    least = jnp.min(least, axis=1, keepdims=True)
    most = jnp.max(most, axis=1, keepdims=True)
    both = jnp.concatenate([least, most], axis=0).astype(jnp.int32)
    range_ref[...] = jnp.broadcast_to(both, range_ref.shape)


def sorting(counts, order, lists, pattern, pick, dest, block):
    entries = lists.shape[1]
    records = jax.ShapeDtypeStruct(pick.shape, jnp.int32)
    return pl.pallas_call(
        functools.partial(sorting_kernel, counts),
        out_shape=(
            jax.ShapeDtypeStruct((entries, SUB, LANES), jnp.int32),
            jax.ShapeDtypeStruct((2 * entries // BATCH, LANES), jnp.int32),
            jax.ShapeDtypeStruct((order, order), jnp.bfloat16),
            records,
            records,
            records,
        ),
        in_specs=[pl.BlockSpec(memory_space=pltpu.MemorySpace.HBM)] * 5,
        out_specs=(pl.BlockSpec(memory_space=VMEM),) * 6,
        scratch_shapes=[
            pltpu.VMEM((entries * SUB, LANES), jnp.float32),
            pltpu.VMEM(lists.shape, jnp.int32),
            pltpu.VMEM(pattern.shape, jnp.int32),
            pltpu.SemaphoreType.DMA((5,)),
        ],
        cost_estimate=pl.CostEstimate(flops=10**7, bytes_accessed=5 * 10**6, transcendentals=0),
        compiler_params=pltpu.CompilerParams(vmem_limit_bytes=GRANT),
        name="sorting",
    )(*in_place(lists, pattern, pick, dest, block))


def pair_kernel(
    domains, first, last, range_ref, keys_ref, own_ref, packed_ref, scale_ref, start_ref, force_ref
):
    blocks = keys_ref.shape[0] // BATCH
    front = (SUB - 1) * domains
    base = lax.broadcasted_iota(jnp.int32, (SUB, LANES), 0) * domains

    def step(j, sums):
        keys = [keys_ref[j * BATCH + i] for i in range(BATCH)]
        rows = [(key >> (KEY_BITS + 7)) - base for key in keys]
        lanes = [(key >> KEY_BITS) & (LANES - 1) for key in keys]
        low = range_ref[j, 0]
        rounds = (range_ref[blocks + j, 0] - low) // CHUNK + 1

        def scan(i, words):
            words = list(words)
            start = low + i * CHUNK
            for m in range(BATCH):
                for u in range(CHUNK):
                    here = rows[m] == start + u
                    for w in range(2):
                        lines = packed_ref[w, pl.ds(front + start + u, SUB, stride=domains), :]
                        k = 2 * m + w
                        words[k] = jnp.where(here, pick_lanes(lines, lanes[m]), words[k])
            return tuple(words)

        zero = jnp.zeros((SUB, LANES), jnp.int32)
        words = lax.fori_loop(0, rounds, scan, (zero,) * (2 * BATCH))
        sums = list(sums)
        for m in range(BATCH):
            group = keys[m] & ((1 << GROUP_BITS) - 1)
            places = places_of((keys[m] >> GROUP_BITS) & 31)
            mine = [group == g for g in range(SUB)]
            one, two = words[2 * m], words[2 * m + 1]
            code = [one & 0xFFFF, (one >> 16) & 0xFFFF, two & 0xFFFF, (two >> 16) & 0xFFFF]
            value = [code[c].astype(jnp.float32) * scale_ref[4 + c] + scale_ref[c] for c in range(4)]
            offset = []
            for c in range(3):
                place = own_ref[c, 0:1, :]
                for g in range(1, SUB):
                    place = jnp.where(mine[g], own_ref[c, g : g + 1, :], place)
                shift = (places[c] - 1).astype(jnp.float32) * domain_edge
                offset.append(place - (value[c] + shift))
            distance = (
                offset[0] * offset[0] + offset[1] * offset[1] + offset[2] * offset[2] + soften
            )
            inverse = lax.rsqrt(distance)
            strength = value[3] * (inverse * inverse * inverse)
            for c in range(3):
                push = offset[c] * strength
                for g in range(SUB):
                    k = c * SUB + g
                    sums[k] = sums[k] + jnp.where(mine[g], push, 0.0)
        return tuple(sums)

    zero = jnp.zeros((SUB, LANES), jnp.float32)
    sums = lax.fori_loop(first, last, step, (zero,) * (3 * SUB))
    for c in range(3):
        total = jnp.concatenate(
            [jnp.sum(sums[c * SUB + g], axis=0, keepdims=True) for g in range(SUB)], axis=0
        )
        force_ref[c] = start_ref[c] + coulomb * own_ref[3] * total


def pair_forces(domains, first, last, ranges, keys, own, packed, scale, start):
    return pl.pallas_call(
        functools.partial(pair_kernel, domains, first, last),
        out_shape=jax.ShapeDtypeStruct((3, SUB, LANES), jnp.float32),
        in_specs=[pl.BlockSpec(memory_space=SMEM)] + [pl.BlockSpec(memory_space=VMEM)] * 5,
        out_specs=pl.BlockSpec(memory_space=VMEM),
        cost_estimate=pl.CostEstimate(
            flops=10**7, bytes_accessed=(last - first) * BATCH * 10**5 * 3, transcendentals=0
        ),
        compiler_params=pltpu.CompilerParams(vmem_limit_bytes=GRANT),
        name="pairs",
    )(ranges, keys, own, packed, scale, start)


def neighbourhood(counts, along_rows):
    reach = [(-1, 0, 1) if n >= 3 else (0, 1) if n == 2 else (0,) for n in counts]
    mine = jnp.stack([along_rows[(-i) % counts[0]] for i in reach[0]])
    columns, layers = counts[1:]
    near = []
    for j in reach[1]:
        for k in reach[2]:
            if (j, k) == (0, 0):
                near.append(mine)
                continue
            pairs = [
                (((c + j) % columns) * layers + (g + k) % layers, c * layers + g)
                for c in range(columns)
                for g in range(layers)
            ]
            near.append(lax.ppermute(mine, ("qc", "grp"), pairs))
    return near


def crossed(value, axis):
    count = lax.axis_size(axis)
    if count & (count - 1):
        return rotated(value, axis), [lambda me, k=k: modulo(me - k, count) for k in range(count)]
    return (
        [value]
        + [lax.ppermute(value, axis, [(i, i ^ k) for i in range(count)]) for k in range(1, count)],
        [lambda me, k=k: me ^ k for k in range(count)],
    )


def per_device(
    kohn_sham, pattern, basis_centers, occupations, atoms, neighbours, emb_atom, emb_dest, emb_block
):
    counts = tuple(lax.axis_size(axis) for axis in ALL)
    layers = counts[2]
    order = kohn_sham.shape[0]
    width = order // layers
    record_count = emb_atom.shape[0]
    own = atoms.reshape(4, SUB, LANES)
    after = lax.optimization_barrier

    left_own, right_own, packet = prepare(width, kohn_sham, own, basis_centers, occupations)
    rights = rotated(right_own, "qr")
    packets = rotated(packet, "qr")
    lefts, places = crossed(left_own, "qc")
    keys, ranges, keep, *records = sorting(
        counts,
        order,
        neighbours[0, 0, 0],
        pattern,
        emb_atom.reshape(1, record_count),
        emb_dest.reshape(1, record_count),
        emb_block.reshape(1, record_count),
    )
    domains = min(3, counts[0]) * min(3, counts[1]) * min(3, counts[2])
    field, embed_force = embedding(order, packets, *records)
    near = neighbourhood(counts, [piece[:4] for piece in packets])

    def from_layers(send):
        if layers == 2:
            return lax.ppermute(send, "grp", [(0, 1), (1, 0)])
        got = lax.all_to_all(
            send.reshape(layers, width, order), "grp", split_axis=0, concat_axis=0, tiled=True
        )
        other = jnp.arange(layers)[:, None, None] != lax.axis_index("grp")
        return jnp.sum(jnp.where(other, got.astype(jnp.float32), 0.0), axis=0)

    blocks = keys.shape[0] // BATCH

    *arrived, keys = after((*rights[1:], keys))
    mine, send, table = product_part(keep, lefts, places, [right_own] + arrived)
    got = from_layers(send)
    field_all = everyone(field, ALL)
    rows, columns = whole_field(field_all)
    product_rows = (mine + got.astype(jnp.float32)).astype(jnp.bfloat16)
    products = rotated(product_rows, "qr")
    packed, scale = packing(near)
    product_rows, packed = after((product_rows, packed))
    force = pair_forces(domains, 0, blocks, ranges, keys, own, packed, scale, embed_force)
    *received, force = after((*products[1:], force))
    products = [products[0]] + received

    mine, send = cube_part(keep, table, rows, columns, products, rights)
    got = from_layers(send)
    sign_step = final_step(mine, got, right_own, columns)
    return (sign_step, force.reshape(3, 1, 1, 1, SUB * LANES))


def solution(mesh):
    in_specs = (
        P("qr", "qc"),
        P("qr", "qc"),
        P(None, "qr"),
        P("qr"),
        P(None, "qr", "qc", "grp", None),
        P("qr", "qc", "grp", None, None, None),
        P(("qr", "qc", "grp")),
        P(("qr", "qc", "grp"), None),
        P(("qr", "qc", "grp")),
    )
    out_specs = (P(("qr", "grp"), "qc"), P(None, "qr", "qc", "grp", None))

    return jax.shard_map(
        per_device, mesh=mesh, in_specs=in_specs, out_specs=out_specs, check_vma=False
    )
```

profile of v0, /device:TPU:0, one launch (start us, length us, event | category | flops | bytes accessed | tf_op | source)
XLA Modules:
  0.0 66.8 jit_solution(7727067722945261436)
XLA Ops:
  0.6 1.0 %prepare.1 = (bf16[384,192]{1,0:T(8,128)(2,1)S(1)}, bf16[192,384]{1,0:T(8,128)(2,1)S(1)}, f32[6,8,128]{2,1,0:T(8,128)S(1)}) custom-call(bf16[384,384]{1,0:T(8,128)(2,1)} %matrix_ref.1, f32[4,8,128]{2,1,0:T(8,128)} %bitcast.12, f32[3,384]{1,0:T(4,128)} %centers_ref.1, f32[384]{0:T(512)} %weights_ref.1), custom_call_target="tpu_custom_call" | custom-call | flops 1000000 | bytes 1000000 | tf_op jit(solution)/shard_map/prepare/pallas_call | solution.py:115
  1.7 5.1 %collective-permute-start.8 = (f32[6,8,128]{2,1,0:T(8,128)S(1)}, f32[6,8,128]{2,1,0:T(8,128)S(1)}, u32[]{:S(2)}, u32[]{:S(2)}) collective-permute-start(f32[6,8,128]{2,1,0:T(8,128)S(1)} %get-tuple-element.39.refs_0_), channel_id=1, source_target_pairs={{0,24},{8,0},{16,8},{24,16},{1,25},{9,1},{17,9},{25,17},{2,26},{10... | collective-permute-start | bytes 73736 | tf_op jit(solution)/shard_map/ppermute | solution.py:50
  6.8 0.0 collective-permute-start.6
  6.8 0.0 collective-permute-start.3
  6.8 4.4 %collective-permute-start.4 = (bf16[192,384]{1,0:T(8,128)(2,1)S(1)}, bf16[192,384]{1,0:T(8,128)(2,1)S(1)}, u32[]{:S(2)}, u32[]{:S(2)}) collective-permute-start(bf16[192,384]{1,0:T(8,128)(2,1)S(1)} %get-tuple-element.33.refs_4_.right_ref), channel_id=1, source_target_pairs={{0,16},{8,24},{16,0},{24,8},{1,17},{9,25},{17,1},{25,9},{2,18},{10... | collective-permute-start | bytes 442376 | tf_op jit(solution)/shard_map/ppermute | solution.py:50
  11.2 0.0 collective-permute-start.5
  11.2 2.9 %sorting.1 = (s32[64,8,128]{2,1,0:T(8,128)S(1)}, s32[16,128]{1,0:T(8,128)S(1)}, bf16[384,384]{1,0:T(8,128)(2,1)S(1)}, s32[1,256]{1,0:T(1,128)S(1)}, s32[1,256]{1,0:T(1,128)S(1)}, /*index=5*/s32[1,256]{1,0:T(1,128)S(1)}) custom-call(s32[2,64,1024]{2,1,0:T(8,128)} %bitcast.14, s32[6,6]{1,0:T(8,128)} %pattern_hbm.1, s32[1,256]{1,0:T(1,128)} %bitcast.16, ...), custom_call_target="tpu_custom_call" | custom-call | flops 10000000 | bytes 5000000 | tf_op jit(solution)/shard_map/sorting/pallas_call | solution.py:624
  14.1 0.0 collective-permute-done.8.refs_3_
  14.1 0.1 collective-permute-start
  14.2 1.7 %collective-permute-done.3.refs_5_ = bf16[192,384]{1,0:T(8,128)(2,1)S(1)} collective-permute-done((bf16[192,384]{1,0:T(8,128)(2,1)S(1)}, bf16[192,384]{1,0:T(8,128)(2,1)S(1)}, u32[]{:S(2)}, u32[]{:S(2)}) %collective-permute-start.3) | collective-permute-done | bytes 147488 | tf_op jit(solution)/shard_map/ppermute | solution.py:50
  15.9 1.5 %collective-permute-start.1 = (bf16[384,192]{1,0:T(8,128)(2,1)S(1)}, bf16[384,192]{1,0:T(8,128)(2,1)S(1)}, u32[]{:S(2)}, u32[]{:S(2)}) collective-permute-start(bf16[384,192]{1,0:T(8,128)(2,1)S(1)} %get-tuple-element.32.refs_0_), channel_id=1, source_target_pairs={{0,4},{2,6},{4,0},{6,2},{1,5},{3,7},{5,1},{7,3},{8,12},{10,14},{12... | collective-permute-start | bytes 442376 | tf_op jit(solution)/shard_map/ppermute | solution.py:751
  17.4 3.4 %collective-permute-done.4.refs_6_ = bf16[192,384]{1,0:T(8,128)(2,1)S(1)} collective-permute-done((bf16[192,384]{1,0:T(8,128)(2,1)S(1)}, bf16[192,384]{1,0:T(8,128)(2,1)S(1)}, u32[]{:S(2)}, u32[]{:S(2)}) %collective-permute-start.4) | collective-permute-done | bytes 147488 | tf_op jit(solution)/shard_map/ppermute | solution.py:50
  20.8 1.0 %collective-permute-start.2 = (bf16[384,192]{1,0:T(8,128)(2,1)S(1)}, bf16[384,192]{1,0:T(8,128)(2,1)S(1)}, u32[]{:S(2)}, u32[]{:S(2)}) collective-permute-start(bf16[384,192]{1,0:T(8,128)(2,1)S(1)} %get-tuple-element.32.refs_0_), channel_id=1, source_target_pairs={{0,6},{2,4},{4,2},{6,0},{1,7},{3,5},{5,3},{7,1},{8,14},{10,12},{12... | collective-permute-start | bytes 442376 | tf_op jit(solution)/shard_map/ppermute | solution.py:751
  21.9 0.0 collective-permute-done.5.refs_7_
  21.9 1.6 %collective-permute-start.7 = (f32[6,8,128]{2,1,0:T(8,128)S(1)}, f32[6,8,128]{2,1,0:T(8,128)S(1)}, u32[]{:S(2)}, u32[]{:S(2)}) collective-permute-start(f32[6,8,128]{2,1,0:T(8,128)S(1)} %get-tuple-element.39.refs_0_), channel_id=1, source_target_pairs={{0,16},{8,24},{16,0},{24,8},{1,17},{9,25},{17,1},{25,9},{2,18},{10... | collective-permute-start | bytes 73736 | tf_op jit(solution)/shard_map/ppermute | solution.py:50
  23.5 0.0 collective-permute-done.refs_1_
  23.5 0.0 collective-permute-done.1.refs_2_
  23.5 4.5 %collective-permute-done.2.refs_3_ = bf16[384,192]{1,0:T(8,128)(2,1)S(1)} collective-permute-done((bf16[384,192]{1,0:T(8,128)(2,1)S(1)}, bf16[384,192]{1,0:T(8,128)(2,1)S(1)}, u32[]{:S(2)}, u32[]{:S(2)}) %collective-permute-start.2) | collective-permute-done | bytes 147488 | tf_op jit(solution)/shard_map/ppermute | solution.py:751
  27.9 0.7 %product.1 = (f32[192,384]{1,0:T(8,128)S(1)}, bf16[192,384]{1,0:T(8,128)(2,1)S(1)}, bf16[4,384,192]{2,1,0:T(8,128)(2,1)S(1)}) custom-call(bf16[384,384]{1,0:T(8,128)(2,1)S(1)} %get-tuple-element.31.keep_ref, bf16[384,192]{1,0:T(8,128)(2,1)S(1)} %get-tuple-element.32.refs_0_, bf16[384,192]{1,0:T(8,128)(2,1)S(1)} %collective-permute-done.refs_1_, ...), custom_call_target="tpu_custom_call" | custom-call | flops 226492416 | bytes 3000000 | tf_op jit(solution)/shard_map/product/pallas_call | solution.py:301
  28.6 1.7 %collective-permute-start.9 = (bf16[192,384]{1,0:T(8,128)(2,1)S(1)}, bf16[192,384]{1,0:T(8,128)(2,1)S(1)}, u32[]{:S(2)}, u32[]{:S(2)}) collective-permute-start(bf16[192,384]{1,0:T(8,128)(2,1)S(1)} %get-tuple-element.47), channel_id=1, source_target_pairs={{0,1},{1,0},{2,3},{3,2},{4,5},{5,4},{6,7},{7,6},{8,9},{9,8},{10,11... | collective-permute-start | bytes 442376 | tf_op jit(solution)/shard_map/ppermute | solution.py:786
  30.3 0.0 collective-permute-done.6.refs_1_
  30.3 0.1 collective-permute-start.13
  30.4 0.0 collective-permute-done.7.refs_2_
  30.4 0.6 embedding.1
  31.0 0.8 %broadcast_in_dim.2 = f32[32,12,128]{2,1,0:T(8,128)} broadcast(f32[12,128]{1,0:T(8,128)S(1)} %get-tuple-element.43), dimensions={1,2} | broadcast | bytes 202752 | tf_op jit(solution)/shard_map/broadcast_in_dim | solution.py:43
  31.8 4.8 %all-to-all-start = ((f32[32,12,128]{2,1,0:T(8,128)}), f32[32,12,128]{2,1,0:T(8,128)S(1)}, u32[]{:S(2)}, u32[]{:S(2)}) async-start(f32[32,12,128]{2,1,0:T(8,128)} %broadcast_in_dim.2), calls=%async_computation | async-start | bytes 524288 | tf_op jit(solution)/shard_map/all_to_all | solution.py:44
  36.6 0.0 collective-permute-done.9
  36.6 1.8 %collective-permute-start.10 = (bf16[192,384]{1,0:T(8,128)(2,1)S(1)}, bf16[192,384]{1,0:T(8,128)(2,1)S(1)}, u32[]{:S(2)}, u32[]{:S(2)}) collective-permute-start(bf16[192,384]{1,0:T(8,128)(2,1)S(1)} %add_convert_fusion.refs_0_), channel_id=1, source_target_pairs={{0,8},{8,16},{16,24},{24,0},{1,9},{9,17},{17,25},{25,1},{2,10},{10... | collective-permute-start | bytes 442376 | tf_op jit(solution)/shard_map/ppermute | solution.py:50
  38.4 2.4 %collective-permute-start.11 = (bf16[192,384]{1,0:T(8,128)(2,1)S(1)}, bf16[192,384]{1,0:T(8,128)(2,1)S(1)}, u32[]{:S(2)}, u32[]{:S(2)}) collective-permute-start(bf16[192,384]{1,0:T(8,128)(2,1)S(1)} %add_convert_fusion.refs_0_), channel_id=1, source_target_pairs={{0,16},{8,24},{16,0},{24,8},{1,17},{9,25},{17,1},{25,9},{2,18},{10... | collective-permute-start | bytes 442376 | tf_op jit(solution)/shard_map/ppermute | solution.py:50
  40.8 1.4 %collective-permute-start.12 = (bf16[192,384]{1,0:T(8,128)(2,1)S(1)}, bf16[192,384]{1,0:T(8,128)(2,1)S(1)}, u32[]{:S(2)}, u32[]{:S(2)}) collective-permute-start(bf16[192,384]{1,0:T(8,128)(2,1)S(1)} %add_convert_fusion.refs_0_), channel_id=1, source_target_pairs={{0,24},{8,0},{16,8},{24,16},{1,25},{9,1},{17,9},{25,17},{2,26},{10... | collective-permute-start | bytes 442376 | tf_op jit(solution)/shard_map/ppermute | solution.py:50
  42.3 0.4 collective-permute-start.14
  42.6 0.0 collective-permute-done.13.refs_0_
  42.6 1.1 %collective-permute-start.15 = (f32[3,4,8,128]{3,2,1,0:T(8,128)S(1)}, f32[3,4,8,128]{3,2,1,0:T(8,128)S(1)}, u32[]{:S(2)}, u32[]{:S(2)}) collective-permute-start(f32[3,4,8,128]{3,2,1,0:T(8,128)S(1)} %pad_maximum_fusion.refs_2_), channel_id=1, source_target_pairs={{1,0},{0,1},{3,2},{2,3},{5,4},{4,5},{7,6},{6,7},{9,8},{8,9},{11,10... | collective-permute-start | bytes 147464 | tf_op jit(solution)/shard_map/ppermute | solution.py:741
  43.7 3.2 %collective-permute-done.14.refs_1_ = f32[3,4,8,128]{3,2,1,0:T(8,128)S(1)} collective-permute-done((f32[3,4,8,128]{3,2,1,0:T(8,128)S(1)}, f32[3,4,8,128]{3,2,1,0:T(8,128)S(1)}, u32[]{:S(2)}, u32[]{:S(2)}) %collective-permute-start.14) | collective-permute-done | bytes 49184 | tf_op jit(solution)/shard_map/ppermute | solution.py:741
  46.9 0.1 collective-permute-start.16
  47.0 0.4 collective-permute-done.15.refs_3_
  47.4 1.9 %collective-permute-start.17 = (f32[3,4,8,128]{3,2,1,0:T(8,128)S(1)}, f32[3,4,8,128]{3,2,1,0:T(8,128)S(1)}, u32[]{:S(2)}, u32[]{:S(2)}) collective-permute-start(f32[3,4,8,128]{3,2,1,0:T(8,128)S(1)} %pad_maximum_fusion.refs_2_), channel_id=1, source_target_pairs={{3,0},{2,1},{5,2},{4,3},{7,4},{6,5},{1,6},{0,7},{11,8},{10,9},{13,... | collective-permute-start | bytes 147464 | tf_op jit(solution)/shard_map/ppermute | solution.py:741
  49.3 0.0 collective-permute-done.16.refs_4_
  49.3 1.7 %collective-permute-done.17.refs_5_ = f32[3,4,8,128]{3,2,1,0:T(8,128)S(1)} collective-permute-done((f32[3,4,8,128]{3,2,1,0:T(8,128)S(1)}, f32[3,4,8,128]{3,2,1,0:T(8,128)S(1)}, u32[]{:S(2)}, u32[]{:S(2)}) %collective-permute-start.17) | collective-permute-done | bytes 49184 | tf_op jit(solution)/shard_map/ppermute | solution.py:741
  51.0 0.0 copy-start
  51.0 0.2 packing.1
  51.3 0.5 copy-done
  51.8 7.1 %pairs.1 = f32[3,8,128]{2,1,0:T(8,128)} custom-call(s32[16,128]{1,0:T(8,128)S(1)} %get-tuple-element.48.range_ref, s32[64,8,128]{2,1,0:T(8,128)S(1)} %get-tuple-element.49.keys_ref, f32[4,8,128]{2,1,0:T(8,128)S(1)} %bitcast.13, s32[2,420,128]{2,1,0:T(8,128)S(1)} %get-tuple-element.51.packed_ref, f32[8,8,128]{2,1,0:T(8,128)S(1)} %get-tuple-element.52.scale_ref, ...), custom_call_target="tpu_custom_call" | custom-call | flops 10000000 | bytes 19200000 | tf_op jit(solution)/shard_map/pairs/pallas_call | solution.py:713
  58.9 0.0 all-to-all-done.parts_ref
  58.9 0.3 field.1
  59.2 0.0 collective-permute-done.10.refs_1_
  59.2 0.0 collective-permute-done.11.refs_2_
  59.2 0.0 collective-permute-done.12.refs_3_
  59.2 0.8 %cube.1 = (f32[192,384]{1,0:T(8,128)S(1)}, bf16[192,384]{1,0:T(8,128)(2,1)S(1)}) custom-call(bf16[384,384]{1,0:T(8,128)(2,1)S(1)} %get-tuple-element.31.keep_ref, bf16[4,384,192]{2,1,0:T(8,128)(2,1)S(1)} %get-tuple-element.38.table_ref, f32[12,128]{1,0:T(8,128)S(1)} %get-tuple-element.44.rows_ref, f32[1536,128]{1,0:T(8,128)S(1)} %get-tuple-element.45.columns_ref, ...), custom_call_target="tpu_custom_call" | custom-call | flops 226492416 | bytes 3000000 | tf_op jit(solution)/shard_map/cube/pallas_call | solution.py:361
  60.1 0.8 %collective-permute-start.18 = (bf16[192,384]{1,0:T(8,128)(2,1)S(1)}, bf16[192,384]{1,0:T(8,128)(2,1)S(1)}, u32[]{:S(2)}, u32[]{:S(2)}) collective-permute-start(bf16[192,384]{1,0:T(8,128)(2,1)S(1)} %get-tuple-element.58), channel_id=1, source_target_pairs={{0,1},{1,0},{2,3},{3,2},{4,5},{5,4},{6,7},{7,6},{8,9},{9,8},{10,11... | collective-permute-start | bytes 442376 | tf_op jit(solution)/shard_map/ppermute | solution.py:786
  60.8 5.2 %collective-permute-done.18.got_ref = bf16[192,384]{1,0:T(8,128)(2,1)S(1)} collective-permute-done((bf16[192,384]{1,0:T(8,128)(2,1)S(1)}, bf16[192,384]{1,0:T(8,128)(2,1)S(1)}, u32[]{:S(2)}, u32[]{:S(2)}) %collective-permute-start.18) | collective-permute-done | bytes 147488 | tf_op jit(solution)/shard_map/ppermute | solution.py:786
  66.0 0.8 %final.1 = bf16[192,384]{1,0:T(8,128)(2,1)} custom-call(f32[192,384]{1,0:T(8,128)S(1)} %get-tuple-element.57.mine_ref, bf16[192,384]{1,0:T(8,128)(2,1)S(1)} %collective-permute-done.18.got_ref, bf16[192,384]{1,0:T(8,128)(2,1)S(1)} %get-tuple-element.33.refs_4_.right_ref, f32[1536,128]{1,0:T(8,128)S(1)} %get-tuple-element.45.columns_ref), custom_call_target="tpu_custom_call" | custom-call | flops 1000000 | bytes 1000000 | tf_op jit(solution)/shard_map/final/pallas_call | solution.py:393
  (5 shorter events, 0.1 us)
Async XLA Ops:
  1.7 12.4 %collective-permute-start.8 = (f32[6,8,128]{2,1,0:T(8,128)S(1)}, f32[6,8,128]{2,1,0:T(8,128)S(1)}, u32[]{:S(2)}, u32[]{:S(2)}) collective-permute-start(f32[6,8,128]{2,1,0:T(8,128)S(1)} %get-tuple-element.39.refs_0_), channel_id=1, source_target_pairs={{0,24},{8,0},{16,8},{24,16},{1,25},{9,1},{17,9},{25,17},{2,26},{10... | collective-permute-start | bytes 73736 | tf_op jit(solution)/shard_map/ppermute | solution.py:50
  6.8 23.5 %collective-permute-start.6 = (f32[6,8,128]{2,1,0:T(8,128)S(1)}, f32[6,8,128]{2,1,0:T(8,128)S(1)}, u32[]{:S(2)}, u32[]{:S(2)}) collective-permute-start(f32[6,8,128]{2,1,0:T(8,128)S(1)} %get-tuple-element.39.refs_0_), channel_id=1, source_target_pairs={{0,8},{8,16},{16,24},{24,0},{1,9},{9,17},{17,25},{25,1},{2,10},{10... | collective-permute-start | bytes 73736 | tf_op jit(solution)/shard_map/ppermute | solution.py:50
  6.8 9.1 %collective-permute-start.3 = (bf16[192,384]{1,0:T(8,128)(2,1)S(1)}, bf16[192,384]{1,0:T(8,128)(2,1)S(1)}, u32[]{:S(2)}, u32[]{:S(2)}) collective-permute-start(bf16[192,384]{1,0:T(8,128)(2,1)S(1)} %get-tuple-element.33.refs_4_.right_ref), channel_id=1, source_target_pairs={{0,8},{8,16},{16,24},{24,0},{1,9},{9,17},{17,25},{25,1},{2,10},{10... | collective-permute-start | bytes 442376 | tf_op jit(solution)/shard_map/ppermute | solution.py:50
  6.8 14.0 %collective-permute-start.4 = (bf16[192,384]{1,0:T(8,128)(2,1)S(1)}, bf16[192,384]{1,0:T(8,128)(2,1)S(1)}, u32[]{:S(2)}, u32[]{:S(2)}) collective-permute-start(bf16[192,384]{1,0:T(8,128)(2,1)S(1)} %get-tuple-element.33.refs_4_.right_ref), channel_id=1, source_target_pairs={{0,16},{8,24},{16,0},{24,8},{1,17},{9,25},{17,1},{25,9},{2,18},{10... | collective-permute-start | bytes 442376 | tf_op jit(solution)/shard_map/ppermute | solution.py:50
  11.2 10.7 %collective-permute-start.5 = (bf16[192,384]{1,0:T(8,128)(2,1)S(1)}, bf16[192,384]{1,0:T(8,128)(2,1)S(1)}, u32[]{:S(2)}, u32[]{:S(2)}) collective-permute-start(bf16[192,384]{1,0:T(8,128)(2,1)S(1)} %get-tuple-element.33.refs_4_.right_ref), channel_id=1, source_target_pairs={{0,24},{8,0},{16,8},{24,16},{1,25},{9,1},{17,9},{25,17},{2,26},{10... | collective-permute-start | bytes 442376 | tf_op jit(solution)/shard_map/ppermute | solution.py:50
  14.1 9.3 %collective-permute-start = (bf16[384,192]{1,0:T(8,128)(2,1)S(1)}, bf16[384,192]{1,0:T(8,128)(2,1)S(1)}, u32[]{:S(2)}, u32[]{:S(2)}) collective-permute-start(bf16[384,192]{1,0:T(8,128)(2,1)S(1)} %get-tuple-element.32.refs_0_), channel_id=1, source_target_pairs={{0,2},{2,0},{4,6},{6,4},{1,3},{3,1},{5,7},{7,5},{8,10},{10,8},{12,... | collective-permute-start | bytes 442376 | tf_op jit(solution)/shard_map/ppermute | solution.py:751
  15.9 7.5 %collective-permute-start.1 = (bf16[384,192]{1,0:T(8,128)(2,1)S(1)}, bf16[384,192]{1,0:T(8,128)(2,1)S(1)}, u32[]{:S(2)}, u32[]{:S(2)}) collective-permute-start(bf16[384,192]{1,0:T(8,128)(2,1)S(1)} %get-tuple-element.32.refs_0_), channel_id=1, source_target_pairs={{0,4},{2,6},{4,0},{6,2},{1,5},{3,7},{5,1},{7,3},{8,12},{10,14},{12... | collective-permute-start | bytes 442376 | tf_op jit(solution)/shard_map/ppermute | solution.py:751
  20.8 7.1 %collective-permute-start.2 = (bf16[384,192]{1,0:T(8,128)(2,1)S(1)}, bf16[384,192]{1,0:T(8,128)(2,1)S(1)}, u32[]{:S(2)}, u32[]{:S(2)}) collective-permute-start(bf16[384,192]{1,0:T(8,128)(2,1)S(1)} %get-tuple-element.32.refs_0_), channel_id=1, source_target_pairs={{0,6},{2,4},{4,2},{6,0},{1,7},{3,5},{5,3},{7,1},{8,14},{10,12},{12... | collective-permute-start | bytes 442376 | tf_op jit(solution)/shard_map/ppermute | solution.py:751
  21.9 8.5 %collective-permute-start.7 = (f32[6,8,128]{2,1,0:T(8,128)S(1)}, f32[6,8,128]{2,1,0:T(8,128)S(1)}, u32[]{:S(2)}, u32[]{:S(2)}) collective-permute-start(f32[6,8,128]{2,1,0:T(8,128)S(1)} %get-tuple-element.39.refs_0_), channel_id=1, source_target_pairs={{0,16},{8,24},{16,0},{24,8},{1,17},{9,25},{17,1},{25,9},{2,18},{10... | collective-permute-start | bytes 73736 | tf_op jit(solution)/shard_map/ppermute | solution.py:50
  28.6 7.9 %collective-permute-start.9 = (bf16[192,384]{1,0:T(8,128)(2,1)S(1)}, bf16[192,384]{1,0:T(8,128)(2,1)S(1)}, u32[]{:S(2)}, u32[]{:S(2)}) collective-permute-start(bf16[192,384]{1,0:T(8,128)(2,1)S(1)} %get-tuple-element.47), channel_id=1, source_target_pairs={{0,1},{1,0},{2,3},{3,2},{4,5},{5,4},{6,7},{7,6},{8,9},{9,8},{10,11... | collective-permute-start | bytes 442376 | tf_op jit(solution)/shard_map/ppermute | solution.py:786
  30.3 12.3 %collective-permute-start.13 = (f32[3,4,8,128]{3,2,1,0:T(8,128)S(1)}, f32[3,4,8,128]{3,2,1,0:T(8,128)S(1)}, u32[]{:S(2)}, u32[]{:S(2)}) collective-permute-start(f32[3,4,8,128]{3,2,1,0:T(8,128)S(1)} %pad_maximum_fusion.refs_2_), channel_id=1, source_target_pairs={{6,0},{7,1},{0,2},{1,3},{2,4},{3,5},{4,6},{5,7},{14,8},{15,9},{8,1... | collective-permute-start | bytes 147464 | tf_op jit(solution)/shard_map/ppermute | solution.py:741
  31.8 27.1 %all-to-all-start = ((f32[32,12,128]{2,1,0:T(8,128)}), f32[32,12,128]{2,1,0:T(8,128)S(1)}, u32[]{:S(2)}, u32[]{:S(2)}) async-start(f32[32,12,128]{2,1,0:T(8,128)} %broadcast_in_dim.2), calls=%async_computation | async-start | bytes 524288 | tf_op jit(solution)/shard_map/all_to_all | solution.py:44
  36.6 22.6 %collective-permute-start.10 = (bf16[192,384]{1,0:T(8,128)(2,1)S(1)}, bf16[192,384]{1,0:T(8,128)(2,1)S(1)}, u32[]{:S(2)}, u32[]{:S(2)}) collective-permute-start(bf16[192,384]{1,0:T(8,128)(2,1)S(1)} %add_convert_fusion.refs_0_), channel_id=1, source_target_pairs={{0,8},{8,16},{16,24},{24,0},{1,9},{9,17},{17,25},{25,1},{2,10},{10... | collective-permute-start | bytes 442376 | tf_op jit(solution)/shard_map/ppermute | solution.py:50
  38.4 20.8 %collective-permute-start.11 = (bf16[192,384]{1,0:T(8,128)(2,1)S(1)}, bf16[192,384]{1,0:T(8,128)(2,1)S(1)}, u32[]{:S(2)}, u32[]{:S(2)}) collective-permute-start(bf16[192,384]{1,0:T(8,128)(2,1)S(1)} %add_convert_fusion.refs_0_), channel_id=1, source_target_pairs={{0,16},{8,24},{16,0},{24,8},{1,17},{9,25},{17,1},{25,9},{2,18},{10... | collective-permute-start | bytes 442376 | tf_op jit(solution)/shard_map/ppermute | solution.py:50
  40.8 18.4 %collective-permute-start.12 = (bf16[192,384]{1,0:T(8,128)(2,1)S(1)}, bf16[192,384]{1,0:T(8,128)(2,1)S(1)}, u32[]{:S(2)}, u32[]{:S(2)}) collective-permute-start(bf16[192,384]{1,0:T(8,128)(2,1)S(1)} %add_convert_fusion.refs_0_), channel_id=1, source_target_pairs={{0,24},{8,0},{16,8},{24,16},{1,25},{9,1},{17,9},{25,17},{2,26},{10... | collective-permute-start | bytes 442376 | tf_op jit(solution)/shard_map/ppermute | solution.py:50
  42.3 4.7 %collective-permute-start.14 = (f32[3,4,8,128]{3,2,1,0:T(8,128)S(1)}, f32[3,4,8,128]{3,2,1,0:T(8,128)S(1)}, u32[]{:S(2)}, u32[]{:S(2)}) collective-permute-start(f32[3,4,8,128]{3,2,1,0:T(8,128)S(1)} %pad_maximum_fusion.refs_2_), channel_id=1, source_target_pairs={{7,0},{6,1},{1,2},{0,3},{3,4},{2,5},{5,6},{4,7},{15,8},{14,9},{9,1... | collective-permute-start | bytes 147464 | tf_op jit(solution)/shard_map/ppermute | solution.py:741
  42.6 4.8 %collective-permute-start.15 = (f32[3,4,8,128]{3,2,1,0:T(8,128)S(1)}, f32[3,4,8,128]{3,2,1,0:T(8,128)S(1)}, u32[]{:S(2)}, u32[]{:S(2)}) collective-permute-start(f32[3,4,8,128]{3,2,1,0:T(8,128)S(1)} %pad_maximum_fusion.refs_2_), channel_id=1, source_target_pairs={{1,0},{0,1},{3,2},{2,3},{5,4},{4,5},{7,6},{6,7},{9,8},{8,9},{11,10... | collective-permute-start | bytes 147464 | tf_op jit(solution)/shard_map/ppermute | solution.py:741
  46.9 2.3 %collective-permute-start.16 = (f32[3,4,8,128]{3,2,1,0:T(8,128)S(1)}, f32[3,4,8,128]{3,2,1,0:T(8,128)S(1)}, u32[]{:S(2)}, u32[]{:S(2)}) collective-permute-start(f32[3,4,8,128]{3,2,1,0:T(8,128)S(1)} %pad_maximum_fusion.refs_2_), channel_id=1, source_target_pairs={{2,0},{3,1},{4,2},{5,3},{6,4},{7,5},{0,6},{1,7},{10,8},{11,9},{12,... | collective-permute-start | bytes 147464 | tf_op jit(solution)/shard_map/ppermute | solution.py:741
  47.4 3.6 %collective-permute-start.17 = (f32[3,4,8,128]{3,2,1,0:T(8,128)S(1)}, f32[3,4,8,128]{3,2,1,0:T(8,128)S(1)}, u32[]{:S(2)}, u32[]{:S(2)}) collective-permute-start(f32[3,4,8,128]{3,2,1,0:T(8,128)S(1)} %pad_maximum_fusion.refs_2_), channel_id=1, source_target_pairs={{3,0},{2,1},{5,2},{4,3},{7,4},{6,5},{1,6},{0,7},{11,8},{10,9},{13,... | collective-permute-start | bytes 147464 | tf_op jit(solution)/shard_map/ppermute | solution.py:741
  51.0 0.7 %copy-start = (f32[4,1,1,1,1024]{4,3,2,1,0:T(1,128)S(1)}, f32[4,1,1,1,1024]{4,3,2,1,0:T(1,128)}, u32[]{:S(2)}) copy-start(f32[4,1,1,1,1024]{4,3,2,1,0:T(1,128)} %param.13) | copy-start | bytes 49156
  60.1 6.0 %collective-permute-start.18 = (bf16[192,384]{1,0:T(8,128)(2,1)S(1)}, bf16[192,384]{1,0:T(8,128)(2,1)S(1)}, u32[]{:S(2)}, u32[]{:S(2)}) collective-permute-start(bf16[192,384]{1,0:T(8,128)(2,1)S(1)} %get-tuple-element.58), channel_id=1, source_target_pairs={{0,1},{1,0},{2,3},{3,2},{4,5},{5,4},{6,7},{7,6},{8,9},{9,8},{10,11... | collective-permute-start | bytes 442376 | tf_op jit(solution)/shard_map/ppermute | solution.py:786
where the time goes:
time: 67.9 us; the launch traced here: 66.8 us
  starting transfers between devices  30 us (44%)
  waiting for transfers between devices  20.2 us (30%)
  Pallas kernels  14.5 us (21%)
  local copies, waits for them, and re-layouts  1.23 us (2%)
  between operations  0.76 us (1%)
    ppermute x9, starting transfers between devices, rotated(): lax.ppermute(value, axis, [(i, (i + k) % count) for i in range(count)])  16.8 us
    pallas_call x1, Pallas kernels, pair_forces(): pl.pallas_call(functools.partial(pair_kernel, domains, first, last), out_...  7.14 us
    ppermute x5, waiting for transfers between devices, neighbourhood(): near.append(lax.ppermute(mine, ('qc', 'grp'), pairs))  5.34 us
    ppermute x2, waiting for transfers between devices, from_layers(): return lax.ppermute(send, 'grp', [(0, 1), (1, 0)])  5.19 us
    ppermute x9, waiting for transfers between devices, rotated(): lax.ppermute(value, axis, [(i, (i + k) % count) for i in range(count)])  5.17 us
    all_to_all x1, starting transfers between devices, everyone(): return lax.all_to_all(copies, axes, split_axis=0, concat_axis=0, tiled=True)  4.75 us
    ppermute x3, waiting for transfers between devices, crossed(): lax.ppermute(value, axis, [(i, i ^ k) for i in range(count)])  4.48 us
    ppermute x5, starting transfers between devices, neighbourhood(): near.append(lax.ppermute(mine, ('qc', 'grp'), pairs))  3.49 us
  transfers between devices with their start and end apart: 20, of which 7 were waited for; matrix products, arithmetic and copies ran while one was open for 1% of the time, Pallas kernels for 18%

commit v1 on v0

--- a/solution.py
+++ b/solution.py
@@ -64,26 +64,19 @@
     return high, middle, low
 
 
-def prepare_kernel(
-    matrix_ref,
-    atoms_ref,
-    centers_ref,
-    weights_ref,
-    left_ref,
-    right_ref,
-    packet_ref,
-    matrix_buf,
-    centers_buf,
-    weights_buf,
-    sems,
-):
+def prepare_kernel(count, *refs):
+    inputs, (left_ref, right_ref, packet_ref), kept, (matrix_buf, centers_buf, weights_buf, sems) = (
+        refs[:count],
+        refs[count : count + 3],
+        refs[count + 3 : -4],
+        refs[-4:],
+    )
     order, width = left_ref.shape
     layer = lax.axis_index("grp")
+    targets = [matrix_buf, packet_ref.at[0:4], centers_buf, weights_buf] + list(kept)
     copies = [
-        pltpu.make_async_copy(matrix_ref, matrix_buf, sems.at[0]),
-        pltpu.make_async_copy(atoms_ref, packet_ref.at[0:4], sems.at[1]),
-        pltpu.make_async_copy(centers_ref, centers_buf, sems.at[2]),
-        pltpu.make_async_copy(weights_ref, weights_buf, sems.at[3]),
+        pltpu.make_async_copy(source, target, sems.at[i])
+        for i, (source, target) in enumerate(zip(inputs, targets))
     ]
     for copy in copies:
         copy.start()
@@ -106,31 +99,34 @@
         def _():
             left_ref[...] = matrix_buf[:, i * width : (i + 1) * width]
 
-    copies[1].wait()
-
-
-def prepare(width, matrix, atoms, centers, weights):
+    for copy in copies[1:2] + copies[4:]:
+        copy.wait()
+
+
+def prepare(width, matrix, atoms, centers, weights, *kept):
     order = matrix.shape[0]
     planes = -(-4 * (order // LANES) // SUB)
-    return pl.pallas_call(
-        prepare_kernel,
+    inputs = (matrix, atoms, centers, weights) + kept
+    return pl.pallas_call(
+        functools.partial(prepare_kernel, len(inputs)),
         out_shape=(
             jax.ShapeDtypeStruct((order, width), matrix.dtype),
             jax.ShapeDtypeStruct((width, order), matrix.dtype),
             jax.ShapeDtypeStruct((4 + planes, SUB, LANES), jnp.float32),
-        ),
-        in_specs=[pl.BlockSpec(memory_space=pltpu.MemorySpace.HBM)] * 4,
-        out_specs=(pl.BlockSpec(memory_space=VMEM),) * 3,
+        )
+        + tuple(jax.ShapeDtypeStruct(value.shape, value.dtype) for value in kept),
+        in_specs=[pl.BlockSpec(memory_space=pltpu.MemorySpace.HBM)] * len(inputs),
+        out_specs=(pl.BlockSpec(memory_space=VMEM),) * (3 + len(kept)),
         scratch_shapes=[
             pltpu.VMEM(matrix.shape, matrix.dtype),
             pltpu.VMEM(centers.shape, centers.dtype),
             pltpu.VMEM(weights.shape, weights.dtype),
-            pltpu.SemaphoreType.DMA((4,)),
+            pltpu.SemaphoreType.DMA((len(inputs),)),
         ],
         cost_estimate=pl.CostEstimate(flops=10**6, bytes_accessed=10**6, transcendentals=0),
         compiler_params=pltpu.CompilerParams(vmem_limit_bytes=GRANT),
         name="prepare",
-    )(*in_place(matrix, atoms, centers, weights))
+    )(*in_place(*inputs))
 
 
 def records_kernel(extent, lines, *refs):
@@ -186,10 +182,11 @@
     terms = hartree_nm * charge * inverse
     terms = jnp.concatenate([jnp.where(odd, 0.0, terms), jnp.where(odd, terms, 0.0)], axis=0)
     high, middle, low = thirds(terms)
-    field_ref[...] = sum(
+    field = sum(
         lax.dot_general(one_out, piece, (((1,), (1,)), ((), ())), preferred_element_type=jnp.float32)
         for piece in (high, middle, low)
     )
+    field_ref[...] = field.astype(field_ref.dtype)
     strength = weight * (inverse * inverse * inverse)
     pushes = [
         coulomb * charge * jnp.sum(strength * offset[c], axis=0, keepdims=True) for c in range(3)
@@ -205,7 +202,7 @@
     return pl.pallas_call(
         functools.partial(records_kernel, extent, lines),
         out_shape=(
-            jax.ShapeDtypeStruct((extent * lines, LANES), jnp.float32),
+            jax.ShapeDtypeStruct((extent * lines, LANES), jnp.bfloat16),
             jax.ShapeDtypeStruct((3, SUB, LANES), jnp.float32),
         ),
         in_specs=[pl.BlockSpec(memory_space=VMEM)] * (extent + 3),
@@ -217,9 +214,9 @@
 
 
 def field_kernel(parts_ref, rows_ref, columns_ref):
-    total = parts_ref[0]
+    total = parts_ref[0].astype(jnp.float32)
     for k in range(1, parts_ref.shape[0]):
-        total = total + parts_ref[k]
+        total = total + parts_ref[k].astype(jnp.float32)
     rows_ref[...] = total
     for n in range(total.shape[0]):
         columns_ref[n * LANES : (n + 1) * LANES, :] = jnp.broadcast_to(
@@ -247,8 +244,18 @@
     return jnp.where(value < 0, value + count, value)
 
 
-def keep_pattern(keep_ref, value):
-    return jnp.where(keep_ref[...].astype(jnp.float32) > 0.5, value, 0.0)
+def keep_pattern(pattern_ref, value):
+    order, blocks = value.shape[0], pattern_ref.shape[0]
+    member_of = (
+        lax.broadcasted_iota(jnp.int32, (order, blocks), 0) // BLOCK
+        == lax.broadcasted_iota(jnp.int32, (order, blocks), 1)
+    ).astype(jnp.bfloat16)
+    marks = (pattern_ref[...] == 1).astype(jnp.float32).astype(jnp.bfloat16)
+    wide = jnp.dot(member_of, marks, preferred_element_type=jnp.float32).astype(jnp.bfloat16)
+    keep = lax.dot_general(
+        wide, member_of, (((1,), (1,)), ((), ())), preferred_element_type=jnp.float32
+    )
+    return jnp.where(keep > 0.5, value, 0.0)
 
 
 def part_outputs(layers, value, hold_ref, mine_ref, send_ref):
@@ -264,7 +271,7 @@
         send_ref[...] = value.astype(send_ref.dtype)
 
 
-def product_kernel(places, keep_ref, *refs):
+def product_kernel(places, pattern_ref, *refs):
     extent = len(refs) - 4 - len(places)
     left_refs, right_refs = refs[: len(places)], refs[len(places) : len(places) + extent]
     mine_ref, send_ref, table_ref, hold_ref = refs[len(places) + extent :]
@@ -280,7 +287,7 @@
         )
     part_outputs(
         hold_ref.shape[0] // mine_ref.shape[0],
-        keep_pattern(keep_ref, total),
+        keep_pattern(pattern_ref, total),
         hold_ref,
         mine_ref,
         send_ref,
@@ -295,7 +302,7 @@
     )
 
 
-def product_part(keep, lefts, places, rights):
+def product_part(pattern, lefts, places, rights):
     order, width = lefts[0].shape
     inputs = len(lefts) + len(rights)
     return pl.pallas_call(
@@ -312,10 +319,10 @@
         ),
         compiler_params=pltpu.CompilerParams(vmem_limit_bytes=GRANT),
         name="product",
-    )(keep, *lefts, *rights)
-
-
-def cube_kernel(keep_ref, table_ref, rows_ref, columns_ref, *refs):
+    )(pattern, *lefts, *rights)
+
+
+def cube_kernel(pattern_ref, table_ref, rows_ref, columns_ref, *refs):
     extent = (len(refs) - 3) // 2
     product_refs, right_refs = refs[:extent], refs[extent : 2 * extent]
     mine_ref, send_ref, hold_ref = refs[2 * extent :]
@@ -351,11 +358,11 @@
             operand = (operand.astype(jnp.float32) + added).astype(jnp.bfloat16)
         total = total + jnp.dot(operand, square, preferred_element_type=jnp.float32)
     part_outputs(
-        order // width, keep_pattern(keep_ref, total), hold_ref, mine_ref, send_ref
-    )
-
-
-def cube_part(keep, table, rows, columns, products, rights):
+        order // width, keep_pattern(pattern_ref, total), hold_ref, mine_ref, send_ref
+    )
+
+
+def cube_part(pattern, table, rows, columns, products, rights):
     _, order, width = table.shape
     inputs = 3 + len(products) + len(rights)
     return pl.pallas_call(
@@ -371,7 +378,7 @@
         ),
         compiler_params=pltpu.CompilerParams(vmem_limit_bytes=GRANT),
         name="cube",
-    )(keep, table, rows, columns, *products, *rights)
+    )(pattern, table, rows, columns, *products, *rights)
 
 
 def final_kernel(mine_ref, got_ref, right_ref, columns_ref, out_ref):
@@ -493,49 +500,10 @@
     return pairs
 
 
-def sorting_kernel(
-    counts,
-    lists_hbm,
-    pattern_hbm,
-    pick_hbm,
-    dest_hbm,
-    block_hbm,
-    keys_ref,
-    range_ref,
-    keep_ref,
-    pick_ref,
-    dest_ref,
-    block_ref,
-    spread_ref,
-    lists_ref,
-    pattern_ref,
-    sems,
-):
-    moves = [
-        (lists_hbm, lists_ref),
-        (pattern_hbm, pattern_ref),
-        (pick_hbm, pick_ref),
-        (dest_hbm, dest_ref),
-        (block_hbm, block_ref),
-    ]
-    copies = [
-        pltpu.make_async_copy(source, target, sems.at[i]) for i, (source, target) in enumerate(moves)
-    ]
-    for copy in copies:
-        copy.start()
-    for copy in copies:
-        copy.wait()
-    order, blocks = keep_ref.shape[0], pattern_ref.shape[0]
-    member_of = (
-        lax.broadcasted_iota(jnp.int32, (order, blocks), 0) // BLOCK
-        == lax.broadcasted_iota(jnp.int32, (order, blocks), 1)
-    ).astype(jnp.bfloat16)
-    marks = (pattern_ref[...] == 1).astype(jnp.float32).astype(jnp.bfloat16)
-    wide = jnp.dot(member_of, marks, preferred_element_type=jnp.float32).astype(jnp.bfloat16)
-    keep_ref[...] = lax.dot_general(
-        wide, member_of, (((1,), (1,)), ((), ())), preferred_element_type=jnp.float32
-    ).astype(jnp.bfloat16)
-
+def sorting_kernel(counts, lists_hbm, keys_ref, range_ref, spread_ref, lists_ref, sem):
+    copy = pltpu.make_async_copy(lists_hbm, lists_ref, sem)
+    copy.start()
+    copy.wait()
     entries = lists_ref.shape[1]
     distinct = [min(3, count) for count in counts]
     domains = distinct[0] * distinct[1] * distinct[2]
@@ -618,31 +586,25 @@
     range_ref[...] = jnp.broadcast_to(both, range_ref.shape)
 
 
-def sorting(counts, order, lists, pattern, pick, dest, block):
+def sorting(counts, lists):
     entries = lists.shape[1]
-    records = jax.ShapeDtypeStruct(pick.shape, jnp.int32)
     return pl.pallas_call(
         functools.partial(sorting_kernel, counts),
         out_shape=(
             jax.ShapeDtypeStruct((entries, SUB, LANES), jnp.int32),
             jax.ShapeDtypeStruct((2 * entries // BATCH, LANES), jnp.int32),
-            jax.ShapeDtypeStruct((order, order), jnp.bfloat16),
-            records,
-            records,
-            records,
         ),
-        in_specs=[pl.BlockSpec(memory_space=pltpu.MemorySpace.HBM)] * 5,
-        out_specs=(pl.BlockSpec(memory_space=VMEM),) * 6,
+        in_specs=[pl.BlockSpec(memory_space=pltpu.MemorySpace.HBM)],
+        out_specs=(pl.BlockSpec(memory_space=VMEM),) * 2,
         scratch_shapes=[
             pltpu.VMEM((entries * SUB, LANES), jnp.float32),
             pltpu.VMEM(lists.shape, jnp.int32),
-            pltpu.VMEM(pattern.shape, jnp.int32),
-            pltpu.SemaphoreType.DMA((5,)),
+            pltpu.SemaphoreType.DMA,
         ],
         cost_estimate=pl.CostEstimate(flops=10**7, bytes_accessed=5 * 10**6, transcendentals=0),
         compiler_params=pltpu.CompilerParams(vmem_limit_bytes=GRANT),
         name="sorting",
-    )(*in_place(lists, pattern, pick, dest, block))
+    )(*in_place(lists))
 
 
 def pair_kernel(
@@ -709,9 +671,9 @@
         force_ref[c] = start_ref[c] + coulomb * own_ref[3] * total
 
 
-def pair_forces(domains, first, last, ranges, keys, own, packed, scale, start):
-    return pl.pallas_call(
-        functools.partial(pair_kernel, domains, first, last),
+def pair_forces(first, last, ranges, keys, own, packed, scale, start):
+    return pl.pallas_call(
+        functools.partial(pair_kernel, (packed.shape[1] - CHUNK) // (3 * SUB - 2), first, last),
         out_shape=jax.ShapeDtypeStruct((3, SUB, LANES), jnp.float32),
         in_specs=[pl.BlockSpec(memory_space=SMEM)] + [pl.BlockSpec(memory_space=VMEM)] * 5,
         out_specs=pl.BlockSpec(memory_space=VMEM),
@@ -764,21 +726,22 @@
     own = atoms.reshape(4, SUB, LANES)
     after = lax.optimization_barrier
 
-    left_own, right_own, packet = prepare(width, kohn_sham, own, basis_centers, occupations)
-    rights = rotated(right_own, "qr")
-    packets = rotated(packet, "qr")
-    lefts, places = crossed(left_own, "qc")
-    keys, ranges, keep, *records = sorting(
-        counts,
-        order,
-        neighbours[0, 0, 0],
+    left_own, right_own, packet, pattern, *records = prepare(
+        width,
+        kohn_sham,
+        own,
+        basis_centers,
+        occupations,
         pattern,
         emb_atom.reshape(1, record_count),
         emb_dest.reshape(1, record_count),
         emb_block.reshape(1, record_count),
     )
-    domains = min(3, counts[0]) * min(3, counts[1]) * min(3, counts[2])
+    packets = rotated(packet, "qr")
+    rights = rotated(right_own, "qr")
+    lefts, places = crossed(left_own, "qc")
     field, embed_force = embedding(order, packets, *records)
+    field_all = everyone(field, ALL)
     near = neighbourhood(counts, [piece[:4] for piece in packets])
 
     def from_layers(send):
@@ -790,23 +753,26 @@
         other = jnp.arange(layers)[:, None, None] != lax.axis_index("grp")
         return jnp.sum(jnp.where(other, got.astype(jnp.float32), 0.0), axis=0)
 
+    mine, send, table = product_part(pattern, lefts, places, rights)
+    got = from_layers(send)
+    lists, mine = after((neighbours[0, 0, 0], mine))
+    keys, ranges = sorting(counts, lists)
     blocks = keys.shape[0] // BATCH
-
-    *arrived, keys = after((*rights[1:], keys))
-    mine, send, table = product_part(keep, lefts, places, [right_own] + arrived)
-    got = from_layers(send)
-    field_all = everyone(field, ALL)
+    got, keys = after((got, keys))
     rows, columns = whole_field(field_all)
     product_rows = (mine + got.astype(jnp.float32)).astype(jnp.bfloat16)
     products = rotated(product_rows, "qr")
     packed, scale = packing(near)
     product_rows, packed = after((product_rows, packed))
-    force = pair_forces(domains, 0, blocks, ranges, keys, own, packed, scale, embed_force)
+    force = pair_forces(0, blocks // 2, ranges, keys, own, packed, scale, embed_force)
     *received, force = after((*products[1:], force))
     products = [products[0]] + received
 
-    mine, send = cube_part(keep, table, rows, columns, products, rights)
+    mine, send = cube_part(pattern, table, rows, columns, products, rights)
     got = from_layers(send)
+    mine, force = after((mine, force))
+    force = pair_forces(blocks // 2, blocks, ranges, keys, own, packed, scale, force)
+    got, force = after((got, force))
     sign_step = final_step(mine, got, right_own, columns)
     return (sign_step, force.reshape(3, 1, 1, 1, SUB * LANES))
 

time: 67.9 us -> 61.8 us (0.910)
  waiting for transfers between devices: 20.2 us -> 14.1 us
  Pallas kernels: 14.5 us -> 15.6 us
    ppermute x2, waiting for transfers between devices: 5.19 us -> 0.47 us  [from_layers(): return lax.ppermute(send, 'grp', [(0, 1), (1, 0)])]
    ppermute x9, waiting for transfers between devices: 5.17 us -> 9.87 us  [rotated(): lax.ppermute(value, axis, [(i, (i + k) % count) for i in range(count)])]
    ppermute x3, waiting for transfers between devices: 4.48 us -> 0.01 us  [crossed(): lax.ppermute(value, axis, [(i, i ^ k) for i in range(count)])]
    ppermute x5, waiting for transfers between devices: 5.34 us -> 3.77 us  [neighbourhood(): near.append(lax.ppermute(mine, ('qc', 'grp'), pairs))]
    ppermute x3, starting transfers between devices: 2.58 us -> 1.5 us  [crossed(): lax.ppermute(value, axis, [(i, i ^ k) for i in range(count)])]
    ppermute x5, starting transfers between devices: 3.49 us -> 4.55 us  [neighbourhood(): near.append(lax.ppermute(mine, ('qc', 'grp'), pairs))]
    pallas_call x2 -> x3, Pallas kernels: 8.17 us -> 8.93 us  [the longest x2 7.85 us: pair_forces(): pl.pallas_call(functools.partial(pair_kernel, (packed.shape[1] - CHUNK) /...]
  transfers between devices with their start and end apart: 20 -> 20, of which waited for: 7 -> 6; matrix products, arithmetic and copies ran while one was open for 1% -> 1% of each run, Pallas kernels for 18% -> 21%
where the time goes in v1:
time: 61.8 us; the launch traced here: 61.3 us
  starting transfers between devices  29.7 us (48%)
  Pallas kernels  15.6 us (25%)
  waiting for transfers between devices  14.1 us (23%)
  local copies, waits for them, and re-layouts  1.11 us (2%)
  between operations  0.78 us (1%)
    ppermute x9, starting transfers between devices, rotated(): lax.ppermute(value, axis, [(i, (i + k) % count) for i in range(count)])  16.8 us
    ppermute x9, waiting for transfers between devices, rotated(): lax.ppermute(value, axis, [(i, (i + k) % count) for i in range(count)])  9.87 us
    pallas_call x2, Pallas kernels, pair_forces(): pl.pallas_call(functools.partial(pair_kernel, (packed.shape[1] - CHUNK) /...  7.85 us
    ppermute x5, starting transfers between devices, neighbourhood(): near.append(lax.ppermute(mine, ('qc', 'grp'), pairs))  4.55 us
    all_to_all x1, starting transfers between devices, everyone(): return lax.all_to_all(copies, axes, split_axis=0, concat_axis=0, tiled=True)  4.36 us
    ppermute x5, waiting for transfers between devices, neighbourhood(): near.append(lax.ppermute(mine, ('qc', 'grp'), pairs))  3.77 us
    pallas_call x1, Pallas kernels, sorting(): pl.pallas_call(functools.partial(sorting_kernel, counts), out_shape=(jax....  2.68 us
    ppermute x2, starting transfers between devices, from_layers(): return lax.ppermute(send, 'grp', [(0, 1), (1, 0)])  2.45 us
  transfers between devices with their start and end apart: 20, of which 6 were waited for; matrix products, arithmetic and copies ran while one was open for 1% of the time, Pallas kernels for 21%

profile of v1, /device:TPU:0, one launch (start us, length us, event | category | flops | bytes accessed | tf_op | source)
XLA Modules:
  0.0 61.3 jit_solution(7801657890966603302)
XLA Ops:
  0.6 1.1 %prepare.1 = (bf16[384,192]{1,0:T(8,128)(2,1)S(1)}, bf16[192,384]{1,0:T(8,128)(2,1)S(1)}, f32[6,8,128]{2,1,0:T(8,128)S(1)}, s32[6,6]{1,0:T(8,128)S(1)}, s32[1,25...) custom-call(bf16[384,384]{1,0:T(8,128)(2,1)} %refs_0_.1, f32[4,8,128]{2,1,0:T(8,128)} %bitcast.12, ...), custom_call_target="tpu_custom_call" | custom-call | flops 1000000 | bytes 1000000 | tf_op jit(solution)/shard_map/prepare/pallas_call | solution.py:110
  1.7 5.1 %collective-permute-start.8 = (f32[6,8,128]{2,1,0:T(8,128)S(1)}, f32[6,8,128]{2,1,0:T(8,128)S(1)}, u32[]{:S(2)}, u32[]{:S(2)}) collective-permute-start(f32[6,8,128]{2,1,0:T(8,128)S(1)} %get-tuple-element.39.refs_0_), channel_id=1, source_target_pairs={{0,24},{8,0},{16,8},{24,16},{1,25},{9,1},{17,9},{25,17},{2,26},{10... | collective-permute-start | bytes 73736 | tf_op jit(solution)/shard_map/ppermute | solution.py:50
  6.8 0.0 collective-permute-start.6
  6.8 3.8 %collective-permute-start.5 = (bf16[192,384]{1,0:T(8,128)(2,1)S(1)}, bf16[192,384]{1,0:T(8,128)(2,1)S(1)}, u32[]{:S(2)}, u32[]{:S(2)}) collective-permute-start(bf16[192,384]{1,0:T(8,128)(2,1)S(1)} %get-tuple-element.37.refs_4_.right_ref), channel_id=1, source_target_pairs={{0,24},{8,0},{16,8},{24,16},{1,25},{9,1},{17,9},{25,17},{2,26},{10... | collective-permute-start | bytes 442376 | tf_op jit(solution)/shard_map/ppermute | solution.py:50
  10.7 0.0 collective-permute-start.4
  10.7 0.6 collective-permute-start.3
  11.2 0.0 collective-permute-done.8.refs_3_
  11.2 0.0 collective-permute-start.2
  11.2 3.7 %collective-permute-done.5.refs_7_ = bf16[192,384]{1,0:T(8,128)(2,1)S(1)} collective-permute-done((bf16[192,384]{1,0:T(8,128)(2,1)S(1)}, bf16[192,384]{1,0:T(8,128)(2,1)S(1)}, u32[]{:S(2)}, u32[]{:S(2)}) %collective-permute-start.5) | collective-permute-done | bytes 147488 | tf_op jit(solution)/shard_map/ppermute | solution.py:50
  14.9 1.5 %collective-permute-start.1 = (bf16[384,192]{1,0:T(8,128)(2,1)S(1)}, bf16[384,192]{1,0:T(8,128)(2,1)S(1)}, u32[]{:S(2)}, u32[]{:S(2)}) collective-permute-start(bf16[384,192]{1,0:T(8,128)(2,1)S(1)} %get-tuple-element.36.refs_0_), channel_id=1, source_target_pairs={{0,4},{2,6},{4,0},{6,2},{1,5},{3,7},{5,1},{7,3},{8,12},{10,14},{12... | collective-permute-start | bytes 442376 | tf_op jit(solution)/shard_map/ppermute | solution.py:713
  16.4 6.2 %collective-permute-done.4.refs_6_ = bf16[192,384]{1,0:T(8,128)(2,1)S(1)} collective-permute-done((bf16[192,384]{1,0:T(8,128)(2,1)S(1)}, bf16[192,384]{1,0:T(8,128)(2,1)S(1)}, u32[]{:S(2)}, u32[]{:S(2)}) %collective-permute-start.4) | collective-permute-done | bytes 147488 | tf_op jit(solution)/shard_map/ppermute | solution.py:50
  22.6 0.0 collective-permute-start
  22.6 0.0 collective-permute-done.3.refs_5_
  22.6 2.6 %collective-permute-start.7 = (f32[6,8,128]{2,1,0:T(8,128)S(1)}, f32[6,8,128]{2,1,0:T(8,128)S(1)}, u32[]{:S(2)}, u32[]{:S(2)}) collective-permute-start(f32[6,8,128]{2,1,0:T(8,128)S(1)} %get-tuple-element.39.refs_0_), channel_id=1, source_target_pairs={{0,16},{8,24},{16,0},{24,8},{1,17},{9,25},{17,1},{25,9},{2,18},{10... | collective-permute-start | bytes 73736 | tf_op jit(solution)/shard_map/ppermute | solution.py:50
  25.2 0.0 collective-permute-done.2.refs_3_
  25.2 0.0 collective-permute-done.1.refs_2_
  25.2 0.0 collective-permute-done.refs_1_
  25.2 0.9 %product.1 = (f32[192,384]{1,0:T(8,128)S(1)}, bf16[192,384]{1,0:T(8,128)(2,1)S(1)}, bf16[4,384,192]{2,1,0:T(8,128)(2,1)S(1)}) custom-call(s32[6,6]{1,0:T(8,128)S(1)} %get-tuple-element.35.pattern_ref, bf16[384,192]{1,0:T(8,128)(2,1)S(1)} %get-tuple-element.36.refs_0_, bf16[384,192]{1,0:T(8,128)(2,1)S(1)} %collective-permute-done.refs_1_, ...), custom_call_target="tpu_custom_call" | custom-call | flops 226492416 | bytes 3000000 | tf_op jit(solution)/shard_map/product/pallas_call | solution.py:308
  26.1 1.7 %collective-permute-start.9 = (bf16[192,384]{1,0:T(8,128)(2,1)S(1)}, bf16[192,384]{1,0:T(8,128)(2,1)S(1)}, u32[]{:S(2)}, u32[]{:S(2)}) collective-permute-start(bf16[192,384]{1,0:T(8,128)(2,1)S(1)} %get-tuple-element.48), channel_id=1, source_target_pairs={{0,1},{1,0},{2,3},{3,2},{4,5},{5,4},{6,7},{7,6},{8,9},{9,8},{10,11... | collective-permute-start | bytes 442376 | tf_op jit(solution)/shard_map/ppermute | solution.py:749
  27.8 0.0 collective-permute-done.6.refs_1_
  27.8 0.1 collective-permute-start.17
  27.9 0.0 collective-permute-done.7.refs_2_
  27.9 0.6 %embedding.1 = (bf16[12,128]{1,0:T(8,128)(2,1)S(1)}, f32[3,8,128]{2,1,0:T(8,128)S(1)}) custom-call(f32[6,8,128]{2,1,0:T(8,128)S(1)} %get-tuple-element.39.refs_0_, f32[6,8,128]{2,1,0:T(8,128)S(1)} %collective-permute-done.6.refs_1_, f32[6,8,128]{2,1,0:T(8,128)S(1)} %collective-permute-done.7.refs_2_, f32[6,8,128]{2,1,0:T(8,128)S(1)} %collective-permute-done.8.refs_3_, ...), custom_call_target="tpu_custom_call" | custom-call | flops 10000000 | bytes 5000000 | tf_op jit(solution)/shard_map/embedding/pallas_call | solution.py:202
  28.5 0.7 %broadcast_in_dim.2 = bf16[32,12,128]{2,1,0:T(8,128)(2,1)} broadcast(bf16[12,128]{1,0:T(8,128)(2,1)S(1)} %get-tuple-element.43), dimensions={1,2} | broadcast | bytes 101376 | tf_op jit(solution)/shard_map/broadcast_in_dim | solution.py:43
  29.2 4.4 %all-to-all-start = ((bf16[32,12,128]{2,1,0:T(8,128)(2,1)}), bf16[32,12,128]{2,1,0:T(8,128)(2,1)S(1)}, u32[]{:S(2)}, u32[]{:S(2)}) async-start(bf16[32,12,128]{2,1,0:T(8,128)(2,1)} %broadcast_in_dim.2), calls=%async_computation | async-start | bytes 262144 | tf_op jit(solution)/shard_map/all_to_all | solution.py:44
  33.6 2.7 %sorting.1 = (s32[64,8,128]{2,1,0:T(8,128)S(1)}, s32[16,128]{1,0:T(8,128)S(1)}) custom-call(s32[2,64,1024]{2,1,0:T(8,128)} %bitcast.15), custom_call_target="tpu_custom_call" | custom-call | flops 10000000 | bytes 5000000 | tf_op jit(solution)/shard_map/sorting/pallas_call | solution.py:591
  36.3 0.0 collective-permute-done.9
  36.3 3.7 %collective-permute-start.12 = (bf16[192,384]{1,0:T(8,128)(2,1)S(1)}, bf16[192,384]{1,0:T(8,128)(2,1)S(1)}, u32[]{:S(2)}, u32[]{:S(2)}) collective-permute-start(bf16[192,384]{1,0:T(8,128)(2,1)S(1)} %add_convert_fusion.refs_0_), channel_id=1, source_target_pairs={{0,24},{8,0},{16,8},{24,16},{1,25},{9,1},{17,9},{25,17},{2,26},{10... | collective-permute-start | bytes 442376 | tf_op jit(solution)/shard_map/ppermute | solution.py:50
  40.0 0.0 collective-permute-start.11
  40.0 1.1 %collective-permute-start.10 = (bf16[192,384]{1,0:T(8,128)(2,1)S(1)}, bf16[192,384]{1,0:T(8,128)(2,1)S(1)}, u32[]{:S(2)}, u32[]{:S(2)}) collective-permute-start(bf16[192,384]{1,0:T(8,128)(2,1)S(1)} %add_convert_fusion.refs_0_), channel_id=1, source_target_pairs={{0,8},{8,16},{16,24},{24,0},{1,9},{9,17},{17,25},{25,1},{2,10},{10... | collective-permute-start | bytes 442376 | tf_op jit(solution)/shard_map/ppermute | solution.py:50
  41.1 0.3 collective-permute-start.16
  41.4 0.0 collective-permute-done.17.refs_5_
  41.4 1.5 %collective-permute-start.15 = (f32[3,4,8,128]{3,2,1,0:T(8,128)S(1)}, f32[3,4,8,128]{3,2,1,0:T(8,128)S(1)}, u32[]{:S(2)}, u32[]{:S(2)}) collective-permute-start(f32[3,4,8,128]{3,2,1,0:T(8,128)S(1)} %pad_maximum_fusion.refs_2_), channel_id=1, source_target_pairs={{1,0},{0,1},{3,2},{2,3},{5,4},{4,5},{7,6},{6,7},{9,8},{8,9},{11,10... | collective-permute-start | bytes 147464 | tf_op jit(solution)/shard_map/ppermute | solution.py:703
  42.9 0.3 collective-permute-done.16.refs_4_
  43.2 2.6 %collective-permute-start.14 = (f32[3,4,8,128]{3,2,1,0:T(8,128)S(1)}, f32[3,4,8,128]{3,2,1,0:T(8,128)S(1)}, u32[]{:S(2)}, u32[]{:S(2)}) collective-permute-start(f32[3,4,8,128]{3,2,1,0:T(8,128)S(1)} %pad_maximum_fusion.refs_2_), channel_id=1, source_target_pairs={{7,0},{6,1},{1,2},{0,3},{3,4},{2,5},{5,6},{4,7},{15,8},{14,9},{9,1... | collective-permute-start | bytes 147464 | tf_op jit(solution)/shard_map/ppermute | solution.py:703
  45.8 0.0 collective-permute-done.15.refs_3_
  45.8 0.0 collective-permute-start.13
  45.8 1.8 %collective-permute-done.14.refs_1_ = f32[3,4,8,128]{3,2,1,0:T(8,128)S(1)} collective-permute-done((f32[3,4,8,128]{3,2,1,0:T(8,128)S(1)}, f32[3,4,8,128]{3,2,1,0:T(8,128)S(1)}, u32[]{:S(2)}, u32[]{:S(2)}) %collective-permute-start.14) | collective-permute-done | bytes 49184 | tf_op jit(solution)/shard_map/ppermute | solution.py:703
  47.7 1.7 %collective-permute-done.13.refs_0_ = f32[3,4,8,128]{3,2,1,0:T(8,128)S(1)} collective-permute-done((f32[3,4,8,128]{3,2,1,0:T(8,128)S(1)}, f32[3,4,8,128]{3,2,1,0:T(8,128)S(1)}, u32[]{:S(2)}, u32[]{:S(2)}) %collective-permute-start.13) | collective-permute-done | bytes 49184 | tf_op jit(solution)/shard_map/ppermute | solution.py:703
  49.4 0.2 packing.1
  49.6 0.0 all-to-all-done.parts_ref
  49.6 0.0 copy-start
  49.6 0.3 field.1
  49.9 0.4 copy-done
  50.3 3.9 %pairs.2.start_ref = f32[3,8,128]{2,1,0:T(8,128)S(1)} custom-call(s32[16,128]{1,0:T(8,128)S(1)} %get-tuple-element.52.range_ref, s32[64,8,128]{2,1,0:T(8,128)S(1)} %get-tuple-element.53.keys_ref, f32[4,8,128]{2,1,0:T(8,128)S(1)} %bitcast.13, s32[2,420,128]{2,1,0:T(8,128)S(1)} %get-tuple-element.55.packed_ref, f32[8,8,128]{2,1,0:T(8,128)S(1)} %get-tuple-element.56.scale_ref, ...), custom_call_target="tpu_custom_call" | custom-call | flops 10000000 | bytes 9600000 | tf_op jit(solution)/shard_map/pairs/pallas_call | solution.py:675
  54.2 0.0 collective-permute-done.12.refs_3_
  54.2 0.0 collective-permute-done.11.refs_2_
  54.2 0.0 collective-permute-done.10.refs_1_
  54.3 1.1 %cube.1 = (f32[192,384]{1,0:T(8,128)S(1)}, bf16[192,384]{1,0:T(8,128)(2,1)S(1)}) custom-call(s32[6,6]{1,0:T(8,128)S(1)} %get-tuple-element.35.pattern_ref, bf16[4,384,192]{2,1,0:T(8,128)(2,1)S(1)} %get-tuple-element.38.table_ref, f32[12,128]{1,0:T(8,128)S(1)} %get-tuple-element.44.rows_ref, f32[1536,128]{1,0:T(8,128)S(1)} %get-tuple-element.45.columns_ref, ...), custom_call_target="tpu_custom_call" | custom-call | flops 226492416 | bytes 3000000 | tf_op jit(solution)/shard_map/cube/pallas_call | solution.py:368
  55.3 0.8 %collective-permute-start.18 = (bf16[192,384]{1,0:T(8,128)(2,1)S(1)}, bf16[192,384]{1,0:T(8,128)(2,1)S(1)}, u32[]{:S(2)}, u32[]{:S(2)}) collective-permute-start(bf16[192,384]{1,0:T(8,128)(2,1)S(1)} %get-tuple-element.64), channel_id=1, source_target_pairs={{0,1},{1,0},{2,3},{3,2},{4,5},{5,4},{6,7},{7,6},{8,9},{9,8},{10,11... | collective-permute-start | bytes 442376 | tf_op jit(solution)/shard_map/ppermute | solution.py:749
  56.1 4.0 %pairs.3 = f32[3,8,128]{2,1,0:T(8,128)} custom-call(s32[16,128]{1,0:T(8,128)S(1)} %get-tuple-element.52.range_ref, s32[64,8,128]{2,1,0:T(8,128)S(1)} %get-tuple-element.53.keys_ref, f32[4,8,128]{2,1,0:T(8,128)S(1)} %bitcast.14, s32[2,420,128]{2,1,0:T(8,128)S(1)} %get-tuple-element.55.packed_ref, f32[8,8,128]{2,1,0:T(8,128)S(1)} %get-tuple-element.56.scale_ref, ...), custom_call_target="tpu_custom_call" | custom-call | flops 10000000 | bytes 9600000 | tf_op jit(solution)/shard_map/pairs/pallas_call | solution.py:675
  60.1 0.5 collective-permute-done.18.got_ref
  60.5 0.8 %final.1 = bf16[192,384]{1,0:T(8,128)(2,1)} custom-call(f32[192,384]{1,0:T(8,128)S(1)} %get-tuple-element.63.mine_ref, bf16[192,384]{1,0:T(8,128)(2,1)S(1)} %collective-permute-done.18.got_ref, bf16[192,384]{1,0:T(8,128)(2,1)S(1)} %get-tuple-element.37.refs_4_.right_ref, f32[1536,128]{1,0:T(8,128)S(1)} %get-tuple-element.45.columns_ref), custom_call_target="tpu_custom_call" | custom-call | flops 1000000 | bytes 1000000 | tf_op jit(solution)/shard_map/final/pallas_call | solution.py:400
  (5 shorter events, 0.1 us)
Async XLA Ops:
  1.7 9.5 %collective-permute-start.8 = (f32[6,8,128]{2,1,0:T(8,128)S(1)}, f32[6,8,128]{2,1,0:T(8,128)S(1)}, u32[]{:S(2)}, u32[]{:S(2)}) collective-permute-start(f32[6,8,128]{2,1,0:T(8,128)S(1)} %get-tuple-element.39.refs_0_), channel_id=1, source_target_pairs={{0,24},{8,0},{16,8},{24,16},{1,25},{9,1},{17,9},{25,17},{2,26},{10... | collective-permute-start | bytes 73736 | tf_op jit(solution)/shard_map/ppermute | solution.py:50
  6.8 21.0 %collective-permute-start.6 = (f32[6,8,128]{2,1,0:T(8,128)S(1)}, f32[6,8,128]{2,1,0:T(8,128)S(1)}, u32[]{:S(2)}, u32[]{:S(2)}) collective-permute-start(f32[6,8,128]{2,1,0:T(8,128)S(1)} %get-tuple-element.39.refs_0_), channel_id=1, source_target_pairs={{0,8},{8,16},{16,24},{24,0},{1,9},{9,17},{17,25},{25,1},{2,10},{10... | collective-permute-start | bytes 73736 | tf_op jit(solution)/shard_map/ppermute | solution.py:50
  6.8 8.1 %collective-permute-start.5 = (bf16[192,384]{1,0:T(8,128)(2,1)S(1)}, bf16[192,384]{1,0:T(8,128)(2,1)S(1)}, u32[]{:S(2)}, u32[]{:S(2)}) collective-permute-start(bf16[192,384]{1,0:T(8,128)(2,1)S(1)} %get-tuple-element.37.refs_4_.right_ref), channel_id=1, source_target_pairs={{0,24},{8,0},{16,8},{24,16},{1,25},{9,1},{17,9},{25,17},{2,26},{10... | collective-permute-start | bytes 442376 | tf_op jit(solution)/shard_map/ppermute | solution.py:50
  10.7 11.9 %collective-permute-start.4 = (bf16[192,384]{1,0:T(8,128)(2,1)S(1)}, bf16[192,384]{1,0:T(8,128)(2,1)S(1)}, u32[]{:S(2)}, u32[]{:S(2)}) collective-permute-start(bf16[192,384]{1,0:T(8,128)(2,1)S(1)} %get-tuple-element.37.refs_4_.right_ref), channel_id=1, source_target_pairs={{0,16},{8,24},{16,0},{24,8},{1,17},{9,25},{17,1},{25,9},{2,18},{10... | collective-permute-start | bytes 442376 | tf_op jit(solution)/shard_map/ppermute | solution.py:50
  10.7 11.9 %collective-permute-start.3 = (bf16[192,384]{1,0:T(8,128)(2,1)S(1)}, bf16[192,384]{1,0:T(8,128)(2,1)S(1)}, u32[]{:S(2)}, u32[]{:S(2)}) collective-permute-start(bf16[192,384]{1,0:T(8,128)(2,1)S(1)} %get-tuple-element.37.refs_4_.right_ref), channel_id=1, source_target_pairs={{0,8},{8,16},{16,24},{24,0},{1,9},{9,17},{17,25},{25,1},{2,10},{10... | collective-permute-start | bytes 442376 | tf_op jit(solution)/shard_map/ppermute | solution.py:50
  11.2 13.9 %collective-permute-start.2 = (bf16[384,192]{1,0:T(8,128)(2,1)S(1)}, bf16[384,192]{1,0:T(8,128)(2,1)S(1)}, u32[]{:S(2)}, u32[]{:S(2)}) collective-permute-start(bf16[384,192]{1,0:T(8,128)(2,1)S(1)} %get-tuple-element.36.refs_0_), channel_id=1, source_target_pairs={{0,6},{2,4},{4,2},{6,0},{1,7},{3,5},{5,3},{7,1},{8,14},{10,12},{12... | collective-permute-start | bytes 442376 | tf_op jit(solution)/shard_map/ppermute | solution.py:713
  14.9 10.3 %collective-permute-start.1 = (bf16[384,192]{1,0:T(8,128)(2,1)S(1)}, bf16[384,192]{1,0:T(8,128)(2,1)S(1)}, u32[]{:S(2)}, u32[]{:S(2)}) collective-permute-start(bf16[384,192]{1,0:T(8,128)(2,1)S(1)} %get-tuple-element.36.refs_0_), channel_id=1, source_target_pairs={{0,4},{2,6},{4,0},{6,2},{1,5},{3,7},{5,1},{7,3},{8,12},{10,14},{12... | collective-permute-start | bytes 442376 | tf_op jit(solution)/shard_map/ppermute | solution.py:713
  22.6 2.6 %collective-permute-start = (bf16[384,192]{1,0:T(8,128)(2,1)S(1)}, bf16[384,192]{1,0:T(8,128)(2,1)S(1)}, u32[]{:S(2)}, u32[]{:S(2)}) collective-permute-start(bf16[384,192]{1,0:T(8,128)(2,1)S(1)} %get-tuple-element.36.refs_0_), channel_id=1, source_target_pairs={{0,2},{2,0},{4,6},{6,4},{1,3},{3,1},{5,7},{7,5},{8,10},{10,8},{12,... | collective-permute-start | bytes 442376 | tf_op jit(solution)/shard_map/ppermute | solution.py:713
  22.6 5.3 %collective-permute-start.7 = (f32[6,8,128]{2,1,0:T(8,128)S(1)}, f32[6,8,128]{2,1,0:T(8,128)S(1)}, u32[]{:S(2)}, u32[]{:S(2)}) collective-permute-start(f32[6,8,128]{2,1,0:T(8,128)S(1)} %get-tuple-element.39.refs_0_), channel_id=1, source_target_pairs={{0,16},{8,24},{16,0},{24,8},{1,17},{9,25},{17,1},{25,9},{2,18},{10... | collective-permute-start | bytes 73736 | tf_op jit(solution)/shard_map/ppermute | solution.py:50
  26.1 10.2 %collective-permute-start.9 = (bf16[192,384]{1,0:T(8,128)(2,1)S(1)}, bf16[192,384]{1,0:T(8,128)(2,1)S(1)}, u32[]{:S(2)}, u32[]{:S(2)}) collective-permute-start(bf16[192,384]{1,0:T(8,128)(2,1)S(1)} %get-tuple-element.48), channel_id=1, source_target_pairs={{0,1},{1,0},{2,3},{3,2},{4,5},{5,4},{6,7},{7,6},{8,9},{9,8},{10,11... | collective-permute-start | bytes 442376 | tf_op jit(solution)/shard_map/ppermute | solution.py:749
  27.8 13.6 %collective-permute-start.17 = (f32[3,4,8,128]{3,2,1,0:T(8,128)S(1)}, f32[3,4,8,128]{3,2,1,0:T(8,128)S(1)}, u32[]{:S(2)}, u32[]{:S(2)}) collective-permute-start(f32[3,4,8,128]{3,2,1,0:T(8,128)S(1)} %pad_maximum_fusion.refs_2_), channel_id=1, source_target_pairs={{3,0},{2,1},{5,2},{4,3},{7,4},{6,5},{1,6},{0,7},{11,8},{10,9},{13,... | collective-permute-start | bytes 147464 | tf_op jit(solution)/shard_map/ppermute | solution.py:703
  29.2 20.4 %all-to-all-start = ((bf16[32,12,128]{2,1,0:T(8,128)(2,1)}), bf16[32,12,128]{2,1,0:T(8,128)(2,1)S(1)}, u32[]{:S(2)}, u32[]{:S(2)}) async-start(bf16[32,12,128]{2,1,0:T(8,128)(2,1)} %broadcast_in_dim.2), calls=%async_computation | async-start | bytes 262144 | tf_op jit(solution)/shard_map/all_to_all | solution.py:44
  36.3 17.9 %collective-permute-start.12 = (bf16[192,384]{1,0:T(8,128)(2,1)S(1)}, bf16[192,384]{1,0:T(8,128)(2,1)S(1)}, u32[]{:S(2)}, u32[]{:S(2)}) collective-permute-start(bf16[192,384]{1,0:T(8,128)(2,1)S(1)} %add_convert_fusion.refs_0_), channel_id=1, source_target_pairs={{0,24},{8,0},{16,8},{24,16},{1,25},{9,1},{17,9},{25,17},{2,26},{10... | collective-permute-start | bytes 442376 | tf_op jit(solution)/shard_map/ppermute | solution.py:50
  40.0 14.2 %collective-permute-start.11 = (bf16[192,384]{1,0:T(8,128)(2,1)S(1)}, bf16[192,384]{1,0:T(8,128)(2,1)S(1)}, u32[]{:S(2)}, u32[]{:S(2)}) collective-permute-start(bf16[192,384]{1,0:T(8,128)(2,1)S(1)} %add_convert_fusion.refs_0_), channel_id=1, source_target_pairs={{0,16},{8,24},{16,0},{24,8},{1,17},{9,25},{17,1},{25,9},{2,18},{10... | collective-permute-start | bytes 442376 | tf_op jit(solution)/shard_map/ppermute | solution.py:50
  40.0 14.2 %collective-permute-start.10 = (bf16[192,384]{1,0:T(8,128)(2,1)S(1)}, bf16[192,384]{1,0:T(8,128)(2,1)S(1)}, u32[]{:S(2)}, u32[]{:S(2)}) collective-permute-start(bf16[192,384]{1,0:T(8,128)(2,1)S(1)} %add_convert_fusion.refs_0_), channel_id=1, source_target_pairs={{0,8},{8,16},{16,24},{24,0},{1,9},{9,17},{17,25},{25,1},{2,10},{10... | collective-permute-start | bytes 442376 | tf_op jit(solution)/shard_map/ppermute | solution.py:50
  41.1 2.1 %collective-permute-start.16 = (f32[3,4,8,128]{3,2,1,0:T(8,128)S(1)}, f32[3,4,8,128]{3,2,1,0:T(8,128)S(1)}, u32[]{:S(2)}, u32[]{:S(2)}) collective-permute-start(f32[3,4,8,128]{3,2,1,0:T(8,128)S(1)} %pad_maximum_fusion.refs_2_), channel_id=1, source_target_pairs={{2,0},{3,1},{4,2},{5,3},{6,4},{7,5},{0,6},{1,7},{10,8},{11,9},{12,... | collective-permute-start | bytes 147464 | tf_op jit(solution)/shard_map/ppermute | solution.py:703
  41.4 4.4 %collective-permute-start.15 = (f32[3,4,8,128]{3,2,1,0:T(8,128)S(1)}, f32[3,4,8,128]{3,2,1,0:T(8,128)S(1)}, u32[]{:S(2)}, u32[]{:S(2)}) collective-permute-start(f32[3,4,8,128]{3,2,1,0:T(8,128)S(1)} %pad_maximum_fusion.refs_2_), channel_id=1, source_target_pairs={{1,0},{0,1},{3,2},{2,3},{5,4},{4,5},{7,6},{6,7},{9,8},{8,9},{11,10... | collective-permute-start | bytes 147464 | tf_op jit(solution)/shard_map/ppermute | solution.py:703
  43.2 4.5 %collective-permute-start.14 = (f32[3,4,8,128]{3,2,1,0:T(8,128)S(1)}, f32[3,4,8,128]{3,2,1,0:T(8,128)S(1)}, u32[]{:S(2)}, u32[]{:S(2)}) collective-permute-start(f32[3,4,8,128]{3,2,1,0:T(8,128)S(1)} %pad_maximum_fusion.refs_2_), channel_id=1, source_target_pairs={{7,0},{6,1},{1,2},{0,3},{3,4},{2,5},{5,6},{4,7},{15,8},{14,9},{9,1... | collective-permute-start | bytes 147464 | tf_op jit(solution)/shard_map/ppermute | solution.py:703
  45.8 3.5 %collective-permute-start.13 = (f32[3,4,8,128]{3,2,1,0:T(8,128)S(1)}, f32[3,4,8,128]{3,2,1,0:T(8,128)S(1)}, u32[]{:S(2)}, u32[]{:S(2)}) collective-permute-start(f32[3,4,8,128]{3,2,1,0:T(8,128)S(1)} %pad_maximum_fusion.refs_2_), channel_id=1, source_target_pairs={{6,0},{7,1},{0,2},{1,3},{2,4},{3,5},{4,6},{5,7},{14,8},{15,9},{8,1... | collective-permute-start | bytes 147464 | tf_op jit(solution)/shard_map/ppermute | solution.py:703
  49.6 0.7 %copy-start = (f32[4,1,1,1,1024]{4,3,2,1,0:T(1,128)S(1)}, f32[4,1,1,1,1024]{4,3,2,1,0:T(1,128)}, u32[]{:S(2)}) copy-start(f32[4,1,1,1,1024]{4,3,2,1,0:T(1,128)} %param.13) | copy-start | bytes 49156
  55.3 5.2 %collective-permute-start.18 = (bf16[192,384]{1,0:T(8,128)(2,1)S(1)}, bf16[192,384]{1,0:T(8,128)(2,1)S(1)}, u32[]{:S(2)}, u32[]{:S(2)}) collective-permute-start(bf16[192,384]{1,0:T(8,128)(2,1)S(1)} %get-tuple-element.64), channel_id=1, source_target_pairs={{0,1},{1,0},{2,3},{3,2},{4,5},{5,4},{6,7},{7,6},{8,9},{9,8},{10,11... | collective-permute-start | bytes 442376 | tf_op jit(solution)/shard_map/ppermute | solution.py:749

commit v2 on v1

--- a/solution.py
+++ b/solution.py
@@ -36,18 +36,11 @@
     )
 
 
-def everyone(value, axes):
-    count = 1
-    for axis in (axes,) if isinstance(axes, str) else axes:
-        count *= lax.axis_size(axis)
-    copies = jnp.broadcast_to(value[None], (count,) + value.shape)
-    return lax.all_to_all(copies, axes, split_axis=0, concat_axis=0, tiled=True)
-
-
 def rotated(value, axis):
     count = lax.axis_size(axis)
-    return [value] + [
-        lax.ppermute(value, axis, [(i, (i + k) % count) for i in range(count)])
+    of = value if callable(value) else lambda k: value
+    return [of(0)] + [
+        lax.ppermute(of(k), axis, [(i, (i + k) % count) for i in range(count)])
         for k in range(1, count)
     ]
 
@@ -65,12 +58,13 @@
 
 
 def prepare_kernel(count, *refs):
-    inputs, (left_ref, right_ref, packet_ref), kept, (matrix_buf, centers_buf, weights_buf, sems) = (
+    inputs, (left_ref, right_ref, packet_ref, basis_ref), kept, buffers = (
         refs[:count],
-        refs[count : count + 3],
-        refs[count + 3 : -4],
+        refs[count : count + 4],
+        refs[count + 4 : -4],
         refs[-4:],
     )
+    matrix_buf, centers_buf, weights_buf, sems = buffers
     order, width = left_ref.shape
     layer = lax.axis_index("grp")
     targets = [matrix_buf, packet_ref.at[0:4], centers_buf, weights_buf] + list(kept)
@@ -90,7 +84,9 @@
     planes = packet_ref.shape[0] - 4
     rows = rows + [jnp.zeros((1, LANES), jnp.float32)] * (planes * SUB - len(rows))
     for n in range(planes):
-        packet_ref[4 + n] = jnp.concatenate(rows[n * SUB : (n + 1) * SUB], axis=0)
+        basis = jnp.concatenate(rows[n * SUB : (n + 1) * SUB], axis=0)
+        packet_ref[4 + n] = basis
+        basis_ref[n] = basis
     copies[0].wait()
     right_ref[...] = matrix_buf[pl.ds(pl.multiple_of(layer * width, width), width), :]
     for i in range(order // width):
@@ -113,10 +109,11 @@
             jax.ShapeDtypeStruct((order, width), matrix.dtype),
             jax.ShapeDtypeStruct((width, order), matrix.dtype),
             jax.ShapeDtypeStruct((4 + planes, SUB, LANES), jnp.float32),
+            jax.ShapeDtypeStruct((planes, SUB, LANES), jnp.float32),
         )
         + tuple(jax.ShapeDtypeStruct(value.shape, value.dtype) for value in kept),
         in_specs=[pl.BlockSpec(memory_space=pltpu.MemorySpace.HBM)] * len(inputs),
-        out_specs=(pl.BlockSpec(memory_space=VMEM),) * (3 + len(kept)),
+        out_specs=(pl.BlockSpec(memory_space=VMEM),) * (4 + len(kept)),
         scratch_shapes=[
             pltpu.VMEM(matrix.shape, matrix.dtype),
             pltpu.VMEM(centers.shape, centers.dtype),
@@ -129,7 +126,7 @@
     )(*in_place(*inputs))
 
 
-def records_kernel(extent, lines, *refs):
+def records_kernel(extent, lines, offsets, *refs):
     packet_refs = refs[:extent]
     pick_ref, dest_ref, block_ref, field_ref, force_ref = refs[extent:]
     count = pick_ref.shape[1]
@@ -165,7 +162,7 @@
     ]
 
     def line(k, n):
-        return packet_refs[k][4 + n // SUB, n % SUB : n % SUB + 1, :]
+        return packet_refs[k][offsets[k] + n // SUB, n % SUB : n % SUB + 1, :]
 
     def chosen(c):
         table = jnp.concatenate(
@@ -186,7 +183,15 @@
         lax.dot_general(one_out, piece, (((1,), (1,)), ((), ())), preferred_element_type=jnp.float32)
         for piece in (high, middle, low)
     )
-    field_ref[...] = field.astype(field_ref.dtype)
+    field = jnp.concatenate(
+        [
+            jnp.concatenate([field[r * lines + n : r * lines + n + 1] for n in range(lines)], axis=1)
+            for r in range(extent)
+        ],
+        axis=0,
+    ).astype(field_ref.dtype)
+    for device in range(field_ref.shape[0]):
+        field_ref[device] = field
     strength = weight * (inverse * inverse * inverse)
     pushes = [
         coulomb * charge * jnp.sum(strength * offset[c], axis=0, keepdims=True) for c in range(3)
@@ -197,215 +202,229 @@
         force_ref[c] = total[c * SUB : (c + 1) * SUB]
 
 
-def embedding(order, packets, pick, dest, block):
+def embedding(order, devices, packets, offsets, pick, dest, block):
     extent, lines = len(packets), order // LANES
-    return pl.pallas_call(
-        functools.partial(records_kernel, extent, lines),
-        out_shape=(
-            jax.ShapeDtypeStruct((extent * lines, LANES), jnp.bfloat16),
+    return in_vmem(
+        functools.partial(records_kernel, extent, lines, offsets),
+        (
+            jax.ShapeDtypeStruct((devices, extent, order), jnp.bfloat16),
             jax.ShapeDtypeStruct((3, SUB, LANES), jnp.float32),
         ),
-        in_specs=[pl.BlockSpec(memory_space=VMEM)] * (extent + 3),
-        out_specs=(pl.BlockSpec(memory_space=VMEM),) * 2,
-        cost_estimate=pl.CostEstimate(flops=10**7, bytes_accessed=5 * 10**6, transcendentals=0),
-        compiler_params=pltpu.CompilerParams(vmem_limit_bytes=GRANT),
-        name="embedding",
-    )(*packets, pick, dest, block)
+        *packets,
+        pick,
+        dest,
+        block,
+    )
 
 
 def field_kernel(parts_ref, rows_ref, columns_ref):
+    devices, extent, order = parts_ref.shape
     total = parts_ref[0].astype(jnp.float32)
-    for k in range(1, parts_ref.shape[0]):
+    for k in range(1, devices):
         total = total + parts_ref[k].astype(jnp.float32)
-    rows_ref[...] = total
-    for n in range(total.shape[0]):
-        columns_ref[n * LANES : (n + 1) * LANES, :] = jnp.broadcast_to(
-            total[n : n + 1], (LANES, LANES)
-        ).T
+    lines = order // LANES
+    for r in range(extent):
+        for n in range(lines):
+            line = total[r : r + 1, n * LANES : (n + 1) * LANES]
+            k = r * lines + n
+            rows_ref[k : k + 1, :] = line
+            columns_ref[k * LANES : (k + 1) * LANES, :] = jnp.broadcast_to(line, (LANES, LANES)).T
 
 
 def whole_field(parts):
-    lines = parts.shape[1]
-    return pl.pallas_call(
+    _, extent, order = parts.shape
+    size = extent * order
+    return in_vmem(
         field_kernel,
-        out_shape=(
-            jax.ShapeDtypeStruct((lines, LANES), jnp.float32),
-            jax.ShapeDtypeStruct((lines * LANES, LANES), jnp.float32),
+        (
+            jax.ShapeDtypeStruct((size // LANES, LANES), jnp.float32),
+            jax.ShapeDtypeStruct((size, LANES), jnp.float32),
         ),
-        in_specs=[pl.BlockSpec(memory_space=VMEM)],
-        out_specs=(pl.BlockSpec(memory_space=VMEM),) * 2,
-        cost_estimate=pl.CostEstimate(flops=10**6, bytes_accessed=3 * 10**6, transcendentals=0),
-        compiler_params=pltpu.CompilerParams(vmem_limit_bytes=GRANT),
-        name="field",
-    )(parts)
+        parts,
+    )
 
 
 def modulo(value, count):
     return jnp.where(value < 0, value + count, value)
 
 
-def keep_pattern(pattern_ref, value):
-    order, blocks = value.shape[0], pattern_ref.shape[0]
-    member_of = (
+def keep_pattern(pattern_ref, first, value):
+    rows, order, blocks = value.shape[0], value.shape[1], pattern_ref.shape[0]
+    row_block = lax.broadcasted_iota(jnp.int32, (rows, blocks), 0) + first
+    below = (
+        row_block // BLOCK == lax.broadcasted_iota(jnp.int32, (rows, blocks), 1)
+    ).astype(jnp.bfloat16)
+    across = (
         lax.broadcasted_iota(jnp.int32, (order, blocks), 0) // BLOCK
         == lax.broadcasted_iota(jnp.int32, (order, blocks), 1)
     ).astype(jnp.bfloat16)
     marks = (pattern_ref[...] == 1).astype(jnp.float32).astype(jnp.bfloat16)
-    wide = jnp.dot(member_of, marks, preferred_element_type=jnp.float32).astype(jnp.bfloat16)
-    keep = lax.dot_general(
-        wide, member_of, (((1,), (1,)), ((), ())), preferred_element_type=jnp.float32
-    )
+    wide = jnp.dot(below, marks, preferred_element_type=jnp.float32).astype(jnp.bfloat16)
+    keep = lax.dot_general(wide, across, (((1,), (1,)), ((), ())), preferred_element_type=jnp.float32)
     return jnp.where(keep > 0.5, value, 0.0)
 
 
-def part_outputs(layers, value, hold_ref, mine_ref, send_ref):
-    width = mine_ref.shape[0]
+def sent_rows(order, width):
+    return width if order == 2 * width else order
+
+
+def first_row(order, width, sent):
     layer = lax.axis_index("grp")
-    hold_ref[...] = value
-    mine_ref[...] = hold_ref[pl.ds(pl.multiple_of(layer * width, width), width), :]
-    if layers == 2:
-        send_ref[...] = hold_ref[
-            pl.ds(pl.multiple_of((1 - layer) * width, width), width), :
-        ].astype(send_ref.dtype)
-    else:
-        send_ref[...] = value.astype(send_ref.dtype)
-
-
-def product_kernel(places, pattern_ref, *refs):
-    extent = len(refs) - 4 - len(places)
-    left_refs, right_refs = refs[: len(places)], refs[len(places) : len(places) + extent]
-    mine_ref, send_ref, table_ref, hold_ref = refs[len(places) + extent :]
-    row, column = lax.axis_index("qr"), lax.axis_index("qc")
+    if not sent:
+        return pl.multiple_of(layer * width, width)
+    return pl.multiple_of((1 - layer) * width, width) if order == 2 * width else 0
+
+
+def row_product(table_ref, tiles, right_refs, first, rows):
+    total = jnp.zeros((rows, right_refs[0].shape[-1]), jnp.float32)
+    for tile, right_ref in zip(tiles, right_refs):
+        total = total + jnp.dot(
+            table_ref[tile, pl.ds(first, rows), :],
+            right_ref[...],
+            preferred_element_type=jnp.float32,
+        )
+    return total
+
+
+def tiles_behind(extent):
+    row = lax.axis_index("qr")
+    return [modulo(row - k, extent) for k in range(extent)]
+
+
+def product_send_kernel(places, pattern_ref, *refs):
+    left_refs, right_refs, (send_ref, table_ref) = refs[: len(places)], refs[len(places) : -2], refs[-2:]
+    column = lax.axis_index("qc")
     for left_ref, place in zip(left_refs, places):
         table_ref[place(column)] = left_ref[...]
-    total = jnp.zeros(hold_ref.shape, jnp.float32)
-    for k in range(extent):
-        total = total + jnp.dot(
-            table_ref[modulo(row - k, extent)],
-            right_refs[k][...],
-            preferred_element_type=jnp.float32,
-        )
-    part_outputs(
-        hold_ref.shape[0] // mine_ref.shape[0],
-        keep_pattern(pattern_ref, total),
-        hold_ref,
-        mine_ref,
-        send_ref,
-    )
-
-
-def part_shapes(order, width):
-    rows = width if order == 2 * width else order
-    return (
-        jax.ShapeDtypeStruct((width, order), jnp.float32),
-        jax.ShapeDtypeStruct((rows, order), jnp.bfloat16),
-    )
-
-
-def product_part(pattern, lefts, places, rights):
+    _, order, width = table_ref.shape
+    rows = sent_rows(order, width)
+    first = first_row(order, width, True)
+    value = row_product(table_ref, tiles_behind(len(right_refs)), right_refs, first, rows)
+    send_ref[...] = keep_pattern(pattern_ref, first, value).astype(send_ref.dtype)
+
+
+def product_own_kernel(pattern_ref, table_ref, *refs):
+    right_refs, own_ref = refs[:-1], refs[-1]
+    _, order, width = table_ref.shape
+    first = first_row(order, width, False)
+    value = row_product(table_ref, tiles_behind(len(right_refs)), right_refs, first, width)
+    own_ref[...] = keep_pattern(pattern_ref, first, value)
+
+
+def in_vmem(kernel, out_shape, *values, work=10**6):
+    return pl.pallas_call(
+        kernel,
+        out_shape=out_shape,
+        in_specs=[pl.BlockSpec(memory_space=VMEM)] * len(values),
+        out_specs=jax.tree.map(lambda _: pl.BlockSpec(memory_space=VMEM), out_shape),
+        cost_estimate=pl.CostEstimate(flops=work, bytes_accessed=work, transcendentals=0),
+        compiler_params=pltpu.CompilerParams(vmem_limit_bytes=GRANT),
+    )(*values)
+
+
+def product_send(pattern, lefts, places, rights):
     order, width = lefts[0].shape
-    inputs = len(lefts) + len(rights)
-    return pl.pallas_call(
-        functools.partial(product_kernel, places),
-        out_shape=part_shapes(order, width)
-        + (jax.ShapeDtypeStruct((len(lefts), order, width), jnp.bfloat16),),
-        in_specs=[pl.BlockSpec(memory_space=VMEM)] * (inputs + 1),
-        out_specs=(pl.BlockSpec(memory_space=VMEM),) * 3,
-        scratch_shapes=[pltpu.VMEM((order, order), jnp.float32)],
-        cost_estimate=pl.CostEstimate(
-            flops=2 * order * order * width * len(rights),
-            bytes_accessed=3 * 10**6,
-            transcendentals=0,
+    return in_vmem(
+        functools.partial(product_send_kernel, places),
+        (
+            jax.ShapeDtypeStruct((sent_rows(order, width), order), jnp.bfloat16),
+            jax.ShapeDtypeStruct((len(lefts), order, width), jnp.bfloat16),
         ),
-        compiler_params=pltpu.CompilerParams(vmem_limit_bytes=GRANT),
-        name="product",
-    )(pattern, *lefts, *rights)
-
-
-def cube_kernel(pattern_ref, table_ref, rows_ref, columns_ref, *refs):
-    extent = (len(refs) - 3) // 2
+        pattern,
+        *lefts,
+        *rights,
+    )
+
+
+def product_own(pattern, table, rights):
+    _, order, width = table.shape
+    out = jax.ShapeDtypeStruct((width, order), jnp.float32)
+    return in_vmem(product_own_kernel, out, pattern, table, *rights)
+
+
+def cube_send_kernel(pattern_ref, table_ref, rows_ref, columns_ref, *refs):
+    extent = (len(refs) - 2) // 2
     product_refs, right_refs = refs[:extent], refs[extent : 2 * extent]
-    mine_ref, send_ref, hold_ref = refs[2 * extent :]
-    width, order = mine_ref.shape
+    send_ref, square_ref = refs[2 * extent :]
+    _, order, width = table_ref.shape
     lines = order // LANES
-    row, column, layer = (lax.axis_index(axis) for axis in ALL)
-    first = layer * width
+    column, layer = lax.axis_index("qc"), lax.axis_index("grp")
+    start = layer * width
     iota = functools.partial(lax.broadcasted_iota, jnp.int32)
-    total = jnp.zeros((order, order), jnp.float32)
-    for k in range(extent):
-        tile = modulo(row - k, extent)
-        down = columns_ref[pl.ds(pl.multiple_of(tile * order + first, width), width), :]
-        pieces = []
+    tiles = tiles_behind(extent)
+    for k, tile in enumerate(tiles):
+        down = columns_ref[pl.ds(pl.multiple_of(tile * order + start, width), width), :]
         for n in range(lines):
             spot = slice(n * LANES, (n + 1) * LANES)
             across = rows_ref[pl.ds(column * lines + n, 1), :]
             matrix = right_refs[k][:, spot].astype(jnp.float32)
-            on_diagonal = iota((width, LANES), 0) + first == iota((width, LANES), 1) + n * LANES
+            on_diagonal = iota((width, LANES), 0) + start == iota((width, LANES), 1) + n * LANES
             corner = jnp.where(on_diagonal & (tile == column), down * down, 0.0)
             piece = product_refs[k][:, spot].astype(jnp.float32) + matrix * (down + across) + corner
-            pieces.append(piece.astype(jnp.bfloat16))
-        square = jnp.concatenate(pieces, axis=1)
-        operand = table_ref[tile]
-        if k == 0:
-            own = columns_ref[pl.ds(pl.multiple_of(row * order, order), order), :]
-            parts = []
-            for start in range(0, width, LANES):
-                size = min(LANES, width - start)
-                shape = (order, size)
-                on_diagonal = iota(shape, 0) == iota(shape, 1) + (first + start)
-                parts.append(jnp.where(on_diagonal, own[:, :size], 0.0))
-            added = parts[0] if len(parts) == 1 else jnp.concatenate(parts, axis=1)
-            operand = (operand.astype(jnp.float32) + added).astype(jnp.bfloat16)
-        total = total + jnp.dot(operand, square, preferred_element_type=jnp.float32)
-    part_outputs(
-        order // width, keep_pattern(pattern_ref, total), hold_ref, mine_ref, send_ref
-    )
-
-
-def cube_part(pattern, table, rows, columns, products, rights):
-    _, order, width = table.shape
-    inputs = 3 + len(products) + len(rights)
-    return pl.pallas_call(
-        cube_kernel,
-        out_shape=part_shapes(order, width),
-        in_specs=[pl.BlockSpec(memory_space=VMEM)] * (inputs + 1),
-        out_specs=(pl.BlockSpec(memory_space=VMEM),) * 2,
-        scratch_shapes=[pltpu.VMEM((order, order), jnp.float32)],
-        cost_estimate=pl.CostEstimate(
-            flops=2 * order * order * width * len(rights),
-            bytes_accessed=3 * 10**6,
-            transcendentals=0,
+            square_ref[k, :, spot] = piece.astype(jnp.bfloat16)
+    rows = sent_rows(order, width)
+    first = first_row(order, width, True)
+    squares = [square_ref.at[k] for k in range(extent)]
+    value = row_product(table_ref, tiles, squares, first, rows)
+    send_ref[...] = keep_pattern(pattern_ref, first, value).astype(send_ref.dtype)
+
+
+def cube_send(pattern, table, rows, columns, products, rights):
+    extent, (_, order, width) = len(rights), table.shape
+    return in_vmem(
+        cube_send_kernel,
+        (
+            jax.ShapeDtypeStruct((sent_rows(order, width), order), jnp.bfloat16),
+            jax.ShapeDtypeStruct((extent, width, order), jnp.bfloat16),
         ),
-        compiler_params=pltpu.CompilerParams(vmem_limit_bytes=GRANT),
-        name="cube",
-    )(pattern, table, rows, columns, *products, *rights)
-
-
-def final_kernel(mine_ref, got_ref, right_ref, columns_ref, out_ref):
-    width, order = mine_ref.shape
-    row, column, layer = (lax.axis_index(axis) for axis in ALL)
-    first = layer * width
+        pattern,
+        table,
+        rows,
+        columns,
+        *products,
+        *rights,
+    )
+
+
+def cube_own_kernel(pattern_ref, table_ref, square_ref, columns_ref, right_ref, out_ref):
+    extent, width, order = square_ref.shape
+    row, column = lax.axis_index("qr"), lax.axis_index("qc")
+    first = first_row(order, width, False)
     down = columns_ref[pl.ds(pl.multiple_of(row * order + first, width), width), :]
     iota = functools.partial(lax.broadcasted_iota, jnp.int32)
+    parts = []
+    for start in range(0, width, LANES):
+        size = min(LANES, width - start)
+        on_diagonal = iota((width, size), 0) == iota((width, size), 1) + start
+        parts.append(jnp.where(on_diagonal, down[:, :size], 0.0))
+    added = parts[0] if len(parts) == 1 else jnp.concatenate(parts, axis=1)
+    value = jnp.zeros((width, order), jnp.float32)
+    for k, tile in enumerate(tiles_behind(extent)):
+        operand = table_ref[tile, pl.ds(first, width), :]
+        if k == 0:
+            operand = (operand.astype(jnp.float32) + added).astype(jnp.bfloat16)
+        value = value + jnp.dot(operand, square_ref[k], preferred_element_type=jnp.float32)
+    value = keep_pattern(pattern_ref, first, value)
     for n in range(order // LANES):
         spot = slice(n * LANES, (n + 1) * LANES)
         on_diagonal = iota((width, LANES), 0) + first == iota((width, LANES), 1) + n * LANES
-        added = jnp.where(on_diagonal & (row == column), down, 0.0)
-        shifted = (right_ref[:, spot].astype(jnp.float32) + added).astype(jnp.bfloat16)
-        cube = mine_ref[:, spot] + got_ref[:, spot].astype(jnp.float32)
-        out_ref[:, spot] = (0.5 * (3.0 * shifted.astype(jnp.float32) - cube)).astype(jnp.bfloat16)
-
-
-def final_step(mine, got, right, columns):
-    return pl.pallas_call(
-        final_kernel,
-        out_shape=jax.ShapeDtypeStruct(mine.shape, jnp.bfloat16),
-        in_specs=[pl.BlockSpec(memory_space=VMEM)] * 4,
-        out_specs=pl.BlockSpec(memory_space=VMEM),
-        cost_estimate=pl.CostEstimate(flops=10**6, bytes_accessed=10**6, transcendentals=0),
-        compiler_params=pltpu.CompilerParams(vmem_limit_bytes=GRANT),
-        name="final",
-    )(mine, got, right, columns)
+        diagonal = jnp.where(on_diagonal & (row == column), down, 0.0)
+        shifted = (right_ref[:, spot].astype(jnp.float32) + diagonal).astype(jnp.bfloat16)
+        out_ref[:, spot] = 0.5 * (3.0 * shifted.astype(jnp.float32) - value[:, spot])
+
+
+def cube_own(pattern, table, squares, columns, right):
+    _, width, order = squares.shape
+    out = jax.ShapeDtypeStruct((width, order), jnp.float32)
+    return in_vmem(cube_own_kernel, out, pattern, table, squares, columns, right)
+
+
+def final_kernel(own_ref, got_ref, out_ref):
+    out_ref[...] = (own_ref[...] - 0.5 * got_ref[...].astype(jnp.float32)).astype(out_ref.dtype)
+
+
+def final_step(own, got):
+    return in_vmem(final_kernel, jax.ShapeDtypeStruct(own.shape, jnp.bfloat16), own, got)
 
 
 KEY_BITS = 8
@@ -726,7 +745,7 @@
     own = atoms.reshape(4, SUB, LANES)
     after = lax.optimization_barrier
 
-    left_own, right_own, packet, pattern, *records = prepare(
+    left_own, right_own, packet, basis, pattern, *records = prepare(
         width,
         kohn_sham,
         own,
@@ -737,11 +756,18 @@
         emb_dest.reshape(1, record_count),
         emb_block.reshape(1, record_count),
     )
-    packets = rotated(packet, "qr")
+    near_row = [min(k, counts[0] - k) <= 1 for k in range(counts[0])]
+    packets = rotated(lambda k: packet if near_row[k] else basis, "qr")
     rights = rotated(right_own, "qr")
     lefts, places = crossed(left_own, "qc")
-    field, embed_force = embedding(order, packets, *records)
-    field_all = everyone(field, ALL)
+    field, embed_force = embedding(
+        order,
+        counts[0] * counts[1] * counts[2],
+        packets,
+        [4 if close else 0 for close in near_row],
+        *records,
+    )
+    field_all = lax.all_to_all(field, ALL, split_axis=0, concat_axis=0, tiled=True)
     near = neighbourhood(counts, [piece[:4] for piece in packets])
 
     def from_layers(send):
@@ -753,8 +779,9 @@
         other = jnp.arange(layers)[:, None, None] != lax.axis_index("grp")
         return jnp.sum(jnp.where(other, got.astype(jnp.float32), 0.0), axis=0)
 
-    mine, send, table = product_part(pattern, lefts, places, rights)
+    send, table = product_send(pattern, lefts, places, rights)
     got = from_layers(send)
+    mine = product_own(pattern, table, rights)
     lists, mine = after((neighbours[0, 0, 0], mine))
     keys, ranges = sorting(counts, lists)
     blocks = keys.shape[0] // BATCH
@@ -764,16 +791,18 @@
     products = rotated(product_rows, "qr")
     packed, scale = packing(near)
     product_rows, packed = after((product_rows, packed))
-    force = pair_forces(0, blocks // 2, ranges, keys, own, packed, scale, embed_force)
+    cut = (blocks + 1) // 2
+    force = pair_forces(0, cut, ranges, keys, own, packed, scale, embed_force)
     *received, force = after((*products[1:], force))
     products = [products[0]] + received
 
-    mine, send = cube_part(pattern, table, rows, columns, products, rights)
+    send, squares = cube_send(pattern, table, rows, columns, products, rights)
     got = from_layers(send)
-    mine, force = after((mine, force))
-    force = pair_forces(blocks // 2, blocks, ranges, keys, own, packed, scale, force)
-    got, force = after((got, force))
-    sign_step = final_step(mine, got, right_own, columns)
+    squares, force = after((squares, force))
+    result = cube_own(pattern, table, squares, columns, right_own)
+    force = pair_forces(cut, blocks, ranges, keys, own, packed, scale, force)
+    got, force, result = after((got, force, result))
+    sign_step = final_step(result, got)
     return (sign_step, force.reshape(3, 1, 1, 1, SUB * LANES))
 
 

time: 61.8 us -> 66.2 us (1.071)
  starting transfers between devices: 29.7 us -> 31.9 us
  waiting for transfers between devices: 14.1 us -> 16 us
  Pallas kernels: 15.6 us -> 16.8 us
  local copies, waits for them, and re-layouts: 1.11 us -> 0.42 us
    ppermute x9, waiting for transfers between devices: 9.87 us -> 6.21 us  [rotated(): lax.ppermute(of(k), axis, [(i, (i + k) % count) for i in range(count)])]
    ppermute x3, waiting for transfers between devices: 0.01 us -> 2.58 us  [crossed(): lax.ppermute(value, axis, [(i, i ^ k) for i in range(count)])]
    ppermute x9, starting transfers between devices: 16.8 us -> 18.7 us  [rotated(): lax.ppermute(of(k), axis, [(i, (i + k) % count) for i in range(count)])]
    ppermute x5, starting transfers between devices: 4.55 us -> 2.73 us  [neighbourhood(): near.append(lax.ppermute(mine, ('qc', 'grp'), pairs))]
    ppermute x2, waiting for transfers between devices: 0.47 us -> 2.22 us  [from_layers(): return lax.ppermute(send, 'grp', [(0, 1), (1, 0)])]
    all_to_all x1, starting transfers between devices: 4.36 us -> 5.63 us  [per_device(): lax.all_to_all(field, ALL, split_axis=0, concat_axis=0, tiled=True)]
    pallas_call x5 -> x7, Pallas kernels: 3.71 us -> 4.92 us  [in_vmem(): pl.pallas_call(kernel, out_shape=out_shape, in_specs=[pl.BlockSpec(memory...]
    ppermute x5, waiting for transfers between devices: 3.77 us -> 4.94 us  [neighbourhood(): near.append(lax.ppermute(mine, ('qc', 'grp'), pairs))]
  transfers between devices with their start and end apart: 20 -> 20, of which waited for: 6 -> 6; matrix products, arithmetic and copies ran while one was open for 1% -> 0% of each run, Pallas kernels for 21% -> 21%
where the time goes in v2:
time: 66.2 us; the launch traced here: 65.9 us
  starting transfers between devices  31.9 us (48%)
  Pallas kernels  16.8 us (25%)
  waiting for transfers between devices  16 us (24%)
  between operations  0.79 us (1%)
    ppermute x9, starting transfers between devices, rotated(): lax.ppermute(of(k), axis, [(i, (i + k) % count) for i in range(count)])  18.7 us
    pallas_call x2, Pallas kernels, pair_forces(): pl.pallas_call(functools.partial(pair_kernel, (packed.shape[1] - CHUNK) /...  7.86 us
    ppermute x9, waiting for transfers between devices, rotated(): lax.ppermute(of(k), axis, [(i, (i + k) % count) for i in range(count)])  6.21 us
    all_to_all x1, starting transfers between devices, per_device(): lax.all_to_all(field, ALL, split_axis=0, concat_axis=0, tiled=True)  5.63 us
    ppermute x5, waiting for transfers between devices, neighbourhood(): near.append(lax.ppermute(mine, ('qc', 'grp'), pairs))  4.94 us
    pallas_call x7, Pallas kernels, in_vmem(): pl.pallas_call(kernel, out_shape=out_shape, in_specs=[pl.BlockSpec(memory...  4.92 us
    ppermute x2, starting transfers between devices, from_layers(): return lax.ppermute(send, 'grp', [(0, 1), (1, 0)])  2.99 us
    ppermute x5, starting transfers between devices, neighbourhood(): near.append(lax.ppermute(mine, ('qc', 'grp'), pairs))  2.73 us
  transfers between devices with their start and end apart: 20, of which 6 were waited for; matrix products, arithmetic and copies ran while one was open for 0% of the time, Pallas kernels for 21%

profile of v2, /device:TPU:0, one launch (start us, length us, event | category | flops | bytes accessed | tf_op | source)
XLA Modules:
  0.0 65.9 jit_solution(17758177309427836269)
XLA Ops:
  0.6 1.1 %prepare.1 = (bf16[384,192]{1,0:T(8,128)(2,1)S(1)}, bf16[192,384]{1,0:T(8,128)(2,1)S(1)}, f32[6,8,128]{2,1,0:T(8,128)S(1)}, f32[2,8,128]{2,1,0:T(8,128)S(1)}, s3...) custom-call(bf16[384,384]{1,0:T(8,128)(2,1)} %refs_0_.1, ...), custom_call_target="tpu_custom_call" | custom-call | flops 1000000 | bytes 1000000 | tf_op jit(solution)/shard_map/prepare/pallas_call | solution.py:106
  1.7 5.1 %collective-permute-start.8 = (f32[6,8,128]{2,1,0:T(8,128)S(1)}, f32[6,8,128]{2,1,0:T(8,128)S(1)}, u32[]{:S(2)}, u32[]{:S(2)}) collective-permute-start(f32[6,8,128]{2,1,0:T(8,128)S(1)} %get-tuple-element.40.refs_0_), channel_id=1, source_target_pairs={{0,24},{8,0},{16,8},{24,16},{1,25},{9,1},{17,9},{25,17},{2,26},{10... | collective-permute-start | bytes 73736 | tf_op jit(solution)/shard_map/ppermute | solution.py:43
  6.8 0.0 collective-permute-start.6
  6.8 3.8 %collective-permute-start.5 = (bf16[192,384]{1,0:T(8,128)(2,1)S(1)}, bf16[192,384]{1,0:T(8,128)(2,1)S(1)}, u32[]{:S(2)}, u32[]{:S(2)}) collective-permute-start(bf16[192,384]{1,0:T(8,128)(2,1)S(1)} %get-tuple-element.38.refs_4_.refs_0_.right_ref), channel_id=1, source_target_pairs={{0,24},{8,0},{16,8},{24,16},{1,25},{9,1},{17,9},{25,17},{2,26},{10... | collective-permute-start | bytes 442376 | tf_op jit(solution)/shard_map/ppermute | solution.py:43
  10.7 0.0 collective-permute-start.4
  10.7 2.9 %collective-permute-start.7 = (f32[2,8,128]{2,1,0:T(8,128)S(1)}, f32[2,8,128]{2,1,0:T(8,128)S(1)}, u32[]{:S(2)}, u32[]{:S(2)}) collective-permute-start(f32[2,8,128]{2,1,0:T(8,128)S(1)} %get-tuple-element.41), channel_id=1, source_target_pairs={{0,16},{8,24},{16,0},{24,8},{1,17},{9,25},{17,1},{25,9},{2,18},{10... | collective-permute-start | bytes 24584 | tf_op jit(solution)/shard_map/ppermute | solution.py:43
  13.6 6.2 %collective-permute-done.7.refs_2_ = f32[2,8,128]{2,1,0:T(8,128)S(1)} collective-permute-done((f32[2,8,128]{2,1,0:T(8,128)S(1)}, f32[2,8,128]{2,1,0:T(8,128)S(1)}, u32[]{:S(2)}, u32[]{:S(2)}) %collective-permute-start.7) | collective-permute-done | bytes 8224 | tf_op jit(solution)/shard_map/ppermute | solution.py:43
  19.8 1.2 %collective-permute-start.3 = (bf16[192,384]{1,0:T(8,128)(2,1)S(1)}, bf16[192,384]{1,0:T(8,128)(2,1)S(1)}, u32[]{:S(2)}, u32[]{:S(2)}) collective-permute-start(bf16[192,384]{1,0:T(8,128)(2,1)S(1)} %get-tuple-element.38.refs_4_.refs_0_.right_ref), channel_id=1, source_target_pairs={{0,8},{8,16},{16,24},{24,0},{1,9},{9,17},{17,25},{25,1},{2,10},{10... | collective-permute-start | bytes 442376 | tf_op jit(solution)/shard_map/ppermute | solution.py:43
  20.9 0.0 collective-permute-done.8.refs_3_
  20.9 0.0 collective-permute-start.2
  20.9 0.0 collective-permute-done.6.refs_1_
  20.9 1.6 %collective-permute-start.1 = (bf16[384,192]{1,0:T(8,128)(2,1)S(1)}, bf16[384,192]{1,0:T(8,128)(2,1)S(1)}, u32[]{:S(2)}, u32[]{:S(2)}) collective-permute-start(bf16[384,192]{1,0:T(8,128)(2,1)S(1)} %get-tuple-element.37.refs_0_), channel_id=1, source_target_pairs={{0,4},{2,6},{4,0},{6,2},{1,5},{3,7},{5,1},{7,3},{8,12},{10,14},{12... | collective-permute-start | bytes 442376 | tf_op jit(solution)/shard_map/ppermute | solution.py:732
  22.5 1.3 %shard_map.105 = (bf16[32,4,384]{2,1,0:T(4,128)(2,1)}, f32[3,8,128]{2,1,0:T(8,128)S(1)}) custom-call(f32[6,8,128]{2,1,0:T(8,128)S(1)} %get-tuple-element.40.refs_0_, f32[6,8,128]{2,1,0:T(8,128)S(1)} %collective-permute-done.6.refs_1_, f32[2,8,128]{2,1,0:T(8,128)S(1)} %collective-permute-done.7.refs_2_, f32[6,8,128]{2,1,0:T(8,128)S(1)} %collective-permute-done.8.refs_3_, ...), custom_call_target="tpu_custom_call" | custom-call | flops 1000000 | bytes 1000000 | tf_op jit(solution)/shard_map/pallas_call | solution.py:315
  23.8 5.6 %all-to-all-start = ((bf16[32,4,384]{2,1,0:T(4,128)(2,1)}), bf16[32,4,384]{2,1,0:T(4,128)(2,1)S(1)}, u32[]{:S(2)}, u32[]{:S(2)}) async-start(bf16[32,4,384]{2,1,0:T(4,128)(2,1)} %get-tuple-element.45), calls=%async_computation | async-start | bytes 196608 | tf_op jit(solution)/shard_map/all_to_all | solution.py:770
  29.5 0.0 collective-permute-done.5.refs_7_.refs_3_
  29.5 0.3 collective-permute-start
  29.8 0.0 collective-permute-done.4.refs_6_.refs_2_
  29.8 0.0 collective-permute-done.3.refs_5_.refs_1_
  29.8 0.0 collective-permute-done.2.refs_3_
  29.8 2.6 %collective-permute-done.1.refs_2_ = bf16[384,192]{1,0:T(8,128)(2,1)S(1)} collective-permute-done((bf16[384,192]{1,0:T(8,128)(2,1)S(1)}, bf16[384,192]{1,0:T(8,128)(2,1)S(1)}, u32[]{:S(2)}, u32[]{:S(2)}) %collective-permute-start.1) | collective-permute-done | bytes 147488 | tf_op jit(solution)/shard_map/ppermute | solution.py:732
  32.4 0.0 collective-permute-done.refs_1_
  32.4 0.6 shard_map.104
  33.0 1.7 %collective-permute-start.9 = (bf16[192,384]{1,0:T(8,128)(2,1)S(1)}, bf16[192,384]{1,0:T(8,128)(2,1)S(1)}, u32[]{:S(2)}, u32[]{:S(2)}) collective-permute-start(bf16[192,384]{1,0:T(8,128)(2,1)S(1)} %get-tuple-element.49), channel_id=1, source_target_pairs={{0,1},{1,0},{2,3},{3,2},{4,5},{5,4},{6,7},{7,6},{8,9},{9,8},{10,11... | collective-permute-start | bytes 442376 | tf_op jit(solution)/shard_map/ppermute | solution.py:775
  34.7 0.0 collective-permute-start.17
  34.7 0.5 shard_map.107
  35.2 2.7 %sorting.1 = (s32[64,8,128]{2,1,0:T(8,128)S(1)}, s32[16,128]{1,0:T(8,128)S(1)}) custom-call(s32[2,64,1024]{2,1,0:T(8,128)} %bitcast.15), custom_call_target="tpu_custom_call" | custom-call | flops 10000000 | bytes 5000000 | tf_op jit(solution)/shard_map/sorting/pallas_call | solution.py:610
  37.9 2.2 %collective-permute-done.9 = bf16[192,384]{1,0:T(8,128)(2,1)S(1)} collective-permute-done((bf16[192,384]{1,0:T(8,128)(2,1)S(1)}, bf16[192,384]{1,0:T(8,128)(2,1)S(1)}, u32[]{:S(2)}, u32[]{:S(2)}) %collective-permute-start.9) | collective-permute-done | bytes 147488 | tf_op jit(solution)/shard_map/ppermute | solution.py:775
  40.2 2.6 %collective-permute-start.12 = (bf16[192,384]{1,0:T(8,128)(2,1)S(1)}, bf16[192,384]{1,0:T(8,128)(2,1)S(1)}, u32[]{:S(2)}, u32[]{:S(2)}) collective-permute-start(bf16[192,384]{1,0:T(8,128)(2,1)S(1)} %add_convert_fusion.refs_0_), channel_id=1, source_target_pairs={{0,24},{8,0},{16,8},{24,16},{1,25},{9,1},{17,9},{25,17},{2,26},{10... | collective-permute-start | bytes 442376 | tf_op jit(solution)/shard_map/ppermute | solution.py:43
  42.8 1.1 %collective-permute-start.11 = (bf16[192,384]{1,0:T(8,128)(2,1)S(1)}, bf16[192,384]{1,0:T(8,128)(2,1)S(1)}, u32[]{:S(2)}, u32[]{:S(2)}) collective-permute-start(bf16[192,384]{1,0:T(8,128)(2,1)S(1)} %add_convert_fusion.refs_0_), channel_id=1, source_target_pairs={{0,16},{8,24},{16,0},{24,8},{1,17},{9,25},{17,1},{25,9},{2,18},{10... | collective-permute-start | bytes 442376 | tf_op jit(solution)/shard_map/ppermute | solution.py:43
  43.9 1.9 %collective-permute-start.10 = (bf16[192,384]{1,0:T(8,128)(2,1)S(1)}, bf16[192,384]{1,0:T(8,128)(2,1)S(1)}, u32[]{:S(2)}, u32[]{:S(2)}) collective-permute-start(bf16[192,384]{1,0:T(8,128)(2,1)S(1)} %add_convert_fusion.refs_0_), channel_id=1, source_target_pairs={{0,8},{8,16},{16,24},{24,0},{1,9},{9,17},{17,25},{25,1},{2,10},{10... | collective-permute-start | bytes 442376 | tf_op jit(solution)/shard_map/ppermute | solution.py:43
  45.8 0.0 collective-permute-start.16
  45.8 0.0 collective-permute-done.17.refs_5_
  45.9 1.7 %collective-permute-start.15 = (f32[3,4,8,128]{3,2,1,0:T(8,128)S(1)}, f32[3,4,8,128]{3,2,1,0:T(8,128)S(1)}, u32[]{:S(2)}, u32[]{:S(2)}) collective-permute-start(f32[3,4,8,128]{3,2,1,0:T(8,128)S(1)} %pad_maximum_fusion.refs_2_), channel_id=1, source_target_pairs={{1,0},{0,1},{3,2},{2,3},{5,4},{4,5},{7,6},{6,7},{9,8},{8,9},{11,10... | collective-permute-start | bytes 147464 | tf_op jit(solution)/shard_map/ppermute | solution.py:722
  47.6 0.0 collective-permute-done.16.refs_4_
  47.6 1.0 %collective-permute-start.14 = (f32[3,4,8,128]{3,2,1,0:T(8,128)S(1)}, f32[3,4,8,128]{3,2,1,0:T(8,128)S(1)}, u32[]{:S(2)}, u32[]{:S(2)}) collective-permute-start(f32[3,4,8,128]{3,2,1,0:T(8,128)S(1)} %pad_maximum_fusion.refs_2_), channel_id=1, source_target_pairs={{7,0},{6,1},{1,2},{0,3},{3,4},{2,5},{5,6},{4,7},{15,8},{14,9},{9,1... | collective-permute-start | bytes 147464 | tf_op jit(solution)/shard_map/ppermute | solution.py:722
  48.6 1.4 %collective-permute-done.15.refs_3_ = f32[3,4,8,128]{3,2,1,0:T(8,128)S(1)} collective-permute-done((f32[3,4,8,128]{3,2,1,0:T(8,128)S(1)}, f32[3,4,8,128]{3,2,1,0:T(8,128)S(1)}, u32[]{:S(2)}, u32[]{:S(2)}) %collective-permute-start.15) | collective-permute-done | bytes 49184 | tf_op jit(solution)/shard_map/ppermute | solution.py:722
  50.0 0.0 collective-permute-start.13
  50.0 2.6 %collective-permute-done.14.refs_1_ = f32[3,4,8,128]{3,2,1,0:T(8,128)S(1)} collective-permute-done((f32[3,4,8,128]{3,2,1,0:T(8,128)S(1)}, f32[3,4,8,128]{3,2,1,0:T(8,128)S(1)}, u32[]{:S(2)}, u32[]{:S(2)}) %collective-permute-start.14) | collective-permute-done | bytes 49184 | tf_op jit(solution)/shard_map/ppermute | solution.py:722
  52.6 0.9 %collective-permute-done.13.refs_0_ = f32[3,4,8,128]{3,2,1,0:T(8,128)S(1)} collective-permute-done((f32[3,4,8,128]{3,2,1,0:T(8,128)S(1)}, f32[3,4,8,128]{3,2,1,0:T(8,128)S(1)}, u32[]{:S(2)}, u32[]{:S(2)}) %collective-permute-start.13) | collective-permute-done | bytes 49184 | tf_op jit(solution)/shard_map/ppermute | solution.py:722
  53.5 0.2 packing.1
  53.8 0.0 all-to-all-done.parts_ref
  53.8 0.0 copy-start
  53.8 0.3 shard_map.106
  54.1 0.4 copy-done
  54.5 3.9 %pairs.2.start_ref = f32[3,8,128]{2,1,0:T(8,128)S(1)} custom-call(s32[16,128]{1,0:T(8,128)S(1)} %get-tuple-element.53.range_ref, s32[64,8,128]{2,1,0:T(8,128)S(1)} %get-tuple-element.54.keys_ref, f32[4,8,128]{2,1,0:T(8,128)S(1)} %bitcast.13, s32[2,420,128]{2,1,0:T(8,128)S(1)} %get-tuple-element.56.packed_ref, f32[8,8,128]{2,1,0:T(8,128)S(1)} %get-tuple-element.57.scale_ref, ...), custom_call_target="tpu_custom_call" | custom-call | flops 10000000 | bytes 9600000 | tf_op jit(solution)/shard_map/pairs/pallas_call | solution.py:694
  58.4 0.0 collective-permute-done.12.refs_3_
  58.4 0.0 collective-permute-done.11.refs_2_
  58.4 0.0 collective-permute-done.10.refs_1_
  58.4 0.9 %shard_map.108 = (bf16[192,384]{1,0:T(8,128)(2,1)S(1)}, bf16[4,192,384]{2,1,0:T(8,128)(2,1)S(1)}) custom-call(s32[6,6]{1,0:T(8,128)S(1)} %get-tuple-element.36.pattern_ref, bf16[4,384,192]{2,1,0:T(8,128)(2,1)S(1)} %get-tuple-element.39.table_ref, f32[12,128]{1,0:T(8,128)S(1)} %get-tuple-element.46.rows_ref, f32[1536,128]{1,0:T(8,128)S(1)} %get-tuple-element.47.columns_ref, ...), custom_call_target="tpu_custom_call" | custom-call | flops 1000000 | bytes 1000000 | tf_op jit(solution)/shard_map/pallas_call | solution.py:315
  59.4 1.3 %collective-permute-start.18 = (bf16[192,384]{1,0:T(8,128)(2,1)S(1)}, bf16[192,384]{1,0:T(8,128)(2,1)S(1)}, u32[]{:S(2)}, u32[]{:S(2)}) collective-permute-start(bf16[192,384]{1,0:T(8,128)(2,1)S(1)} %get-tuple-element.62), channel_id=1, source_target_pairs={{0,1},{1,0},{2,3},{3,2},{4,5},{5,4},{6,7},{7,6},{8,9},{9,8},{10,11... | collective-permute-start | bytes 442376 | tf_op jit(solution)/shard_map/ppermute | solution.py:775
  60.7 0.5 shard_map.109.own_ref
  61.2 4.0 %pairs.3 = f32[3,8,128]{2,1,0:T(8,128)} custom-call(s32[16,128]{1,0:T(8,128)S(1)} %get-tuple-element.53.range_ref, s32[64,8,128]{2,1,0:T(8,128)S(1)} %get-tuple-element.54.keys_ref, f32[4,8,128]{2,1,0:T(8,128)S(1)} %bitcast.14, s32[2,420,128]{2,1,0:T(8,128)S(1)} %get-tuple-element.56.packed_ref, f32[8,8,128]{2,1,0:T(8,128)S(1)} %get-tuple-element.57.scale_ref, ...), custom_call_target="tpu_custom_call" | custom-call | flops 10000000 | bytes 9600000 | tf_op jit(solution)/shard_map/pairs/pallas_call | solution.py:694
  65.2 0.0 collective-permute-done.18.got_ref
  65.2 0.7 %shard_map.110 = bf16[192,384]{1,0:T(8,128)(2,1)} custom-call(f32[192,384]{1,0:T(8,128)S(1)} %shard_map.109.own_ref, bf16[192,384]{1,0:T(8,128)(2,1)S(1)} %collective-permute-done.18.got_ref), custom_call_target="tpu_custom_call" | custom-call | flops 1000000 | bytes 1000000 | tf_op jit(solution)/shard_map/pallas_call | solution.py:315
  (5 shorter events, 0.1 us)
Async XLA Ops:
  1.7 19.2 %collective-permute-start.8 = (f32[6,8,128]{2,1,0:T(8,128)S(1)}, f32[6,8,128]{2,1,0:T(8,128)S(1)}, u32[]{:S(2)}, u32[]{:S(2)}) collective-permute-start(f32[6,8,128]{2,1,0:T(8,128)S(1)} %get-tuple-element.40.refs_0_), channel_id=1, source_target_pairs={{0,24},{8,0},{16,8},{24,16},{1,25},{9,1},{17,9},{25,17},{2,26},{10... | collective-permute-start | bytes 73736 | tf_op jit(solution)/shard_map/ppermute | solution.py:43
  6.8 14.1 %collective-permute-start.6 = (f32[6,8,128]{2,1,0:T(8,128)S(1)}, f32[6,8,128]{2,1,0:T(8,128)S(1)}, u32[]{:S(2)}, u32[]{:S(2)}) collective-permute-start(f32[6,8,128]{2,1,0:T(8,128)S(1)} %get-tuple-element.40.refs_0_), channel_id=1, source_target_pairs={{0,8},{8,16},{16,24},{24,0},{1,9},{9,17},{17,25},{25,1},{2,10},{10... | collective-permute-start | bytes 73736 | tf_op jit(solution)/shard_map/ppermute | solution.py:43
  6.8 22.6 %collective-permute-start.5 = (bf16[192,384]{1,0:T(8,128)(2,1)S(1)}, bf16[192,384]{1,0:T(8,128)(2,1)S(1)}, u32[]{:S(2)}, u32[]{:S(2)}) collective-permute-start(bf16[192,384]{1,0:T(8,128)(2,1)S(1)} %get-tuple-element.38.refs_4_.refs_0_.right_ref), channel_id=1, source_target_pairs={{0,24},{8,0},{16,8},{24,16},{1,25},{9,1},{17,9},{25,17},{2,26},{10... | collective-permute-start | bytes 442376 | tf_op jit(solution)/shard_map/ppermute | solution.py:43
  10.7 19.1 %collective-permute-start.4 = (bf16[192,384]{1,0:T(8,128)(2,1)S(1)}, bf16[192,384]{1,0:T(8,128)(2,1)S(1)}, u32[]{:S(2)}, u32[]{:S(2)}) collective-permute-start(bf16[192,384]{1,0:T(8,128)(2,1)S(1)} %get-tuple-element.38.refs_4_.refs_0_.right_ref), channel_id=1, source_target_pairs={{0,16},{8,24},{16,0},{24,8},{1,17},{9,25},{17,1},{25,9},{2,18},{10... | collective-permute-start | bytes 442376 | tf_op jit(solution)/shard_map/ppermute | solution.py:43
  10.7 9.1 %collective-permute-start.7 = (f32[2,8,128]{2,1,0:T(8,128)S(1)}, f32[2,8,128]{2,1,0:T(8,128)S(1)}, u32[]{:S(2)}, u32[]{:S(2)}) collective-permute-start(f32[2,8,128]{2,1,0:T(8,128)S(1)} %get-tuple-element.41), channel_id=1, source_target_pairs={{0,16},{8,24},{16,0},{24,8},{1,17},{9,25},{17,1},{25,9},{2,18},{10... | collective-permute-start | bytes 24584 | tf_op jit(solution)/shard_map/ppermute | solution.py:43
  19.8 10.0 %collective-permute-start.3 = (bf16[192,384]{1,0:T(8,128)(2,1)S(1)}, bf16[192,384]{1,0:T(8,128)(2,1)S(1)}, u32[]{:S(2)}, u32[]{:S(2)}) collective-permute-start(bf16[192,384]{1,0:T(8,128)(2,1)S(1)} %get-tuple-element.38.refs_4_.refs_0_.right_ref), channel_id=1, source_target_pairs={{0,8},{8,16},{16,24},{24,0},{1,9},{9,17},{17,25},{25,1},{2,10},{10... | collective-permute-start | bytes 442376 | tf_op jit(solution)/shard_map/ppermute | solution.py:43
  20.9 8.9 %collective-permute-start.2 = (bf16[384,192]{1,0:T(8,128)(2,1)S(1)}, bf16[384,192]{1,0:T(8,128)(2,1)S(1)}, u32[]{:S(2)}, u32[]{:S(2)}) collective-permute-start(bf16[384,192]{1,0:T(8,128)(2,1)S(1)} %get-tuple-element.37.refs_0_), channel_id=1, source_target_pairs={{0,6},{2,4},{4,2},{6,0},{1,7},{3,5},{5,3},{7,1},{8,14},{10,12},{12... | collective-permute-start | bytes 442376 | tf_op jit(solution)/shard_map/ppermute | solution.py:732
  20.9 11.4 %collective-permute-start.1 = (bf16[384,192]{1,0:T(8,128)(2,1)S(1)}, bf16[384,192]{1,0:T(8,128)(2,1)S(1)}, u32[]{:S(2)}, u32[]{:S(2)}) collective-permute-start(bf16[384,192]{1,0:T(8,128)(2,1)S(1)} %get-tuple-element.37.refs_0_), channel_id=1, source_target_pairs={{0,4},{2,6},{4,0},{6,2},{1,5},{3,7},{5,1},{7,3},{8,12},{10,14},{12... | collective-permute-start | bytes 442376 | tf_op jit(solution)/shard_map/ppermute | solution.py:732
  23.8 29.9 %all-to-all-start = ((bf16[32,4,384]{2,1,0:T(4,128)(2,1)}), bf16[32,4,384]{2,1,0:T(4,128)(2,1)S(1)}, u32[]{:S(2)}, u32[]{:S(2)}) async-start(bf16[32,4,384]{2,1,0:T(4,128)(2,1)} %get-tuple-element.45), calls=%async_computation | async-start | bytes 196608 | tf_op jit(solution)/shard_map/all_to_all | solution.py:770
  29.5 2.9 %collective-permute-start = (bf16[384,192]{1,0:T(8,128)(2,1)S(1)}, bf16[384,192]{1,0:T(8,128)(2,1)S(1)}, u32[]{:S(2)}, u32[]{:S(2)}) collective-permute-start(bf16[384,192]{1,0:T(8,128)(2,1)S(1)} %get-tuple-element.37.refs_0_), channel_id=1, source_target_pairs={{0,2},{2,0},{4,6},{6,4},{1,3},{3,1},{5,7},{7,5},{8,10},{10,8},{12,... | collective-permute-start | bytes 442376 | tf_op jit(solution)/shard_map/ppermute | solution.py:732
  33.0 7.2 %collective-permute-start.9 = (bf16[192,384]{1,0:T(8,128)(2,1)S(1)}, bf16[192,384]{1,0:T(8,128)(2,1)S(1)}, u32[]{:S(2)}, u32[]{:S(2)}) collective-permute-start(bf16[192,384]{1,0:T(8,128)(2,1)S(1)} %get-tuple-element.49), channel_id=1, source_target_pairs={{0,1},{1,0},{2,3},{3,2},{4,5},{5,4},{6,7},{7,6},{8,9},{9,8},{10,11... | collective-permute-start | bytes 442376 | tf_op jit(solution)/shard_map/ppermute | solution.py:775
  34.7 11.2 %collective-permute-start.17 = (f32[3,4,8,128]{3,2,1,0:T(8,128)S(1)}, f32[3,4,8,128]{3,2,1,0:T(8,128)S(1)}, u32[]{:S(2)}, u32[]{:S(2)}) collective-permute-start(f32[3,4,8,128]{3,2,1,0:T(8,128)S(1)} %pad_maximum_fusion.refs_2_), channel_id=1, source_target_pairs={{3,0},{2,1},{5,2},{4,3},{7,4},{6,5},{1,6},{0,7},{11,8},{10,9},{13,... | collective-permute-start | bytes 147464 | tf_op jit(solution)/shard_map/ppermute | solution.py:722
  40.2 18.2 %collective-permute-start.12 = (bf16[192,384]{1,0:T(8,128)(2,1)S(1)}, bf16[192,384]{1,0:T(8,128)(2,1)S(1)}, u32[]{:S(2)}, u32[]{:S(2)}) collective-permute-start(bf16[192,384]{1,0:T(8,128)(2,1)S(1)} %add_convert_fusion.refs_0_), channel_id=1, source_target_pairs={{0,24},{8,0},{16,8},{24,16},{1,25},{9,1},{17,9},{25,17},{2,26},{10... | collective-permute-start | bytes 442376 | tf_op jit(solution)/shard_map/ppermute | solution.py:43
  42.8 15.6 %collective-permute-start.11 = (bf16[192,384]{1,0:T(8,128)(2,1)S(1)}, bf16[192,384]{1,0:T(8,128)(2,1)S(1)}, u32[]{:S(2)}, u32[]{:S(2)}) collective-permute-start(bf16[192,384]{1,0:T(8,128)(2,1)S(1)} %add_convert_fusion.refs_0_), channel_id=1, source_target_pairs={{0,16},{8,24},{16,0},{24,8},{1,17},{9,25},{17,1},{25,9},{2,18},{10... | collective-permute-start | bytes 442376 | tf_op jit(solution)/shard_map/ppermute | solution.py:43
  43.9 14.5 %collective-permute-start.10 = (bf16[192,384]{1,0:T(8,128)(2,1)S(1)}, bf16[192,384]{1,0:T(8,128)(2,1)S(1)}, u32[]{:S(2)}, u32[]{:S(2)}) collective-permute-start(bf16[192,384]{1,0:T(8,128)(2,1)S(1)} %add_convert_fusion.refs_0_), channel_id=1, source_target_pairs={{0,8},{8,16},{16,24},{24,0},{1,9},{9,17},{17,25},{25,1},{2,10},{10... | collective-permute-start | bytes 442376 | tf_op jit(solution)/shard_map/ppermute | solution.py:43
  45.8 1.8 %collective-permute-start.16 = (f32[3,4,8,128]{3,2,1,0:T(8,128)S(1)}, f32[3,4,8,128]{3,2,1,0:T(8,128)S(1)}, u32[]{:S(2)}, u32[]{:S(2)}) collective-permute-start(f32[3,4,8,128]{3,2,1,0:T(8,128)S(1)} %pad_maximum_fusion.refs_2_), channel_id=1, source_target_pairs={{2,0},{3,1},{4,2},{5,3},{6,4},{7,5},{0,6},{1,7},{10,8},{11,9},{12,... | collective-permute-start | bytes 147464 | tf_op jit(solution)/shard_map/ppermute | solution.py:722
  45.9 4.2 %collective-permute-start.15 = (f32[3,4,8,128]{3,2,1,0:T(8,128)S(1)}, f32[3,4,8,128]{3,2,1,0:T(8,128)S(1)}, u32[]{:S(2)}, u32[]{:S(2)}) collective-permute-start(f32[3,4,8,128]{3,2,1,0:T(8,128)S(1)} %pad_maximum_fusion.refs_2_), channel_id=1, source_target_pairs={{1,0},{0,1},{3,2},{2,3},{5,4},{4,5},{7,6},{6,7},{9,8},{8,9},{11,10... | collective-permute-start | bytes 147464 | tf_op jit(solution)/shard_map/ppermute | solution.py:722
  47.6 5.0 %collective-permute-start.14 = (f32[3,4,8,128]{3,2,1,0:T(8,128)S(1)}, f32[3,4,8,128]{3,2,1,0:T(8,128)S(1)}, u32[]{:S(2)}, u32[]{:S(2)}) collective-permute-start(f32[3,4,8,128]{3,2,1,0:T(8,128)S(1)} %pad_maximum_fusion.refs_2_), channel_id=1, source_target_pairs={{7,0},{6,1},{1,2},{0,3},{3,4},{2,5},{5,6},{4,7},{15,8},{14,9},{9,1... | collective-permute-start | bytes 147464 | tf_op jit(solution)/shard_map/ppermute | solution.py:722
  50.0 3.5 %collective-permute-start.13 = (f32[3,4,8,128]{3,2,1,0:T(8,128)S(1)}, f32[3,4,8,128]{3,2,1,0:T(8,128)S(1)}, u32[]{:S(2)}, u32[]{:S(2)}) collective-permute-start(f32[3,4,8,128]{3,2,1,0:T(8,128)S(1)} %pad_maximum_fusion.refs_2_), channel_id=1, source_target_pairs={{6,0},{7,1},{0,2},{1,3},{2,4},{3,5},{4,6},{5,7},{14,8},{15,9},{8,1... | collective-permute-start | bytes 147464 | tf_op jit(solution)/shard_map/ppermute | solution.py:722
  53.8 0.7 %copy-start = (f32[4,1,1,1,1024]{4,3,2,1,0:T(1,128)S(1)}, f32[4,1,1,1,1024]{4,3,2,1,0:T(1,128)}, u32[]{:S(2)}) copy-start(f32[4,1,1,1,1024]{4,3,2,1,0:T(1,128)} %param.13) | copy-start | bytes 49156
  59.4 5.8 %collective-permute-start.18 = (bf16[192,384]{1,0:T(8,128)(2,1)S(1)}, bf16[192,384]{1,0:T(8,128)(2,1)S(1)}, u32[]{:S(2)}, u32[]{:S(2)}) collective-permute-start(bf16[192,384]{1,0:T(8,128)(2,1)S(1)} %get-tuple-element.62), channel_id=1, source_target_pairs={{0,1},{1,0},{2,3},{3,2},{4,5},{5,4},{6,7},{7,6},{8,9},{9,8},{10,11... | collective-permute-start | bytes 442376 | tf_op jit(solution)/shard_map/ppermute | solution.py:775

commit v3 on v2

--- a/solution.py
+++ b/solution.py
@@ -782,16 +782,15 @@
     send, table = product_send(pattern, lefts, places, rights)
     got = from_layers(send)
     mine = product_own(pattern, table, rights)
-    lists, mine = after((neighbours[0, 0, 0], mine))
-    keys, ranges = sorting(counts, lists)
-    blocks = keys.shape[0] // BATCH
-    got, keys = after((got, keys))
     rows, columns = whole_field(field_all)
     product_rows = (mine + got.astype(jnp.float32)).astype(jnp.bfloat16)
     products = rotated(product_rows, "qr")
+    lists, product_rows = after((neighbours[0, 0, 0], product_rows))
+    keys, ranges = sorting(counts, lists)
+    blocks = keys.shape[0] // BATCH
     packed, scale = packing(near)
     product_rows, packed = after((product_rows, packed))
-    cut = (blocks + 1) // 2
+    cut = (5 * blocks + 7) // 8
     force = pair_forces(0, cut, ranges, keys, own, packed, scale, embed_force)
     *received, force = after((*products[1:], force))
     products = [products[0]] + received

time: 66.2 us -> 68.4 us (1.033)
  waiting for transfers between devices: 16 us -> 18.7 us
    ppermute x2, waiting for transfers between devices: 2.22 us -> 4.92 us  [from_layers(): return lax.ppermute(send, 'grp', [(0, 1), (1, 0)])]
where the time goes in v3:
time: 68.4 us; the launch traced here: 68.2 us
  starting transfers between devices  31.9 us (47%)
  waiting for transfers between devices  18.7 us (27%)
  Pallas kernels  16.8 us (25%)
  between operations  0.8 us (1%)
    ppermute x9, starting transfers between devices, rotated(): lax.ppermute(of(k), axis, [(i, (i + k) % count) for i in range(count)])  18.7 us
    pallas_call x2, Pallas kernels, pair_forces(): pl.pallas_call(functools.partial(pair_kernel, (packed.shape[1] - CHUNK) /...  7.86 us
    ppermute x9, waiting for transfers between devices, rotated(): lax.ppermute(of(k), axis, [(i, (i + k) % count) for i in range(count)])  6.21 us
    all_to_all x1, starting transfers between devices, per_device(): lax.all_to_all(field, ALL, split_axis=0, concat_axis=0, tiled=True)  5.64 us
    ppermute x5, waiting for transfers between devices, neighbourhood(): near.append(lax.ppermute(mine, ('qc', 'grp'), pairs))  4.94 us
    pallas_call x7, Pallas kernels, in_vmem(): pl.pallas_call(kernel, out_shape=out_shape, in_specs=[pl.BlockSpec(memory...  4.92 us
    ppermute x2, waiting for transfers between devices, from_layers(): return lax.ppermute(send, 'grp', [(0, 1), (1, 0)])  4.92 us
    ppermute x2, starting transfers between devices, from_layers(): return lax.ppermute(send, 'grp', [(0, 1), (1, 0)])  3 us
  transfers between devices with their start and end apart: 20, of which 6 were waited for; matrix products, arithmetic and copies ran while one was open for 0% of the time, Pallas kernels for 21%

profile of v3, /device:TPU:0, one launch (start us, length us, event | category | flops | bytes accessed | tf_op | source)
XLA Modules:
  0.0 68.2 jit_solution(5463515524953460478)
XLA Ops:
  0.6 1.1 %prepare.1 = (bf16[384,192]{1,0:T(8,128)(2,1)S(1)}, bf16[192,384]{1,0:T(8,128)(2,1)S(1)}, f32[6,8,128]{2,1,0:T(8,128)S(1)}, f32[2,8,128]{2,1,0:T(8,128)S(1)}, s3...) custom-call(bf16[384,384]{1,0:T(8,128)(2,1)} %refs_0_.1, ...), custom_call_target="tpu_custom_call" | custom-call | flops 1000000 | bytes 1000000 | tf_op jit(solution)/shard_map/prepare/pallas_call | solution.py:106
  1.7 5.1 %collective-permute-start.8 = (f32[6,8,128]{2,1,0:T(8,128)S(1)}, f32[6,8,128]{2,1,0:T(8,128)S(1)}, u32[]{:S(2)}, u32[]{:S(2)}) collective-permute-start(f32[6,8,128]{2,1,0:T(8,128)S(1)} %get-tuple-element.36.refs_0_), channel_id=1, source_target_pairs={{0,24},{8,0},{16,8},{24,16},{1,25},{9,1},{17,9},{25,17},{2,26},{10... | collective-permute-start | bytes 73736 | tf_op jit(solution)/shard_map/ppermute | solution.py:43
  6.8 0.0 collective-permute-start.6
  6.8 3.8 %collective-permute-start.5 = (bf16[192,384]{1,0:T(8,128)(2,1)S(1)}, bf16[192,384]{1,0:T(8,128)(2,1)S(1)}, u32[]{:S(2)}, u32[]{:S(2)}) collective-permute-start(bf16[192,384]{1,0:T(8,128)(2,1)S(1)} %get-tuple-element.34.refs_4_.refs_0_.right_ref), channel_id=1, source_target_pairs={{0,24},{8,0},{16,8},{24,16},{1,25},{9,1},{17,9},{25,17},{2,26},{10... | collective-permute-start | bytes 442376 | tf_op jit(solution)/shard_map/ppermute | solution.py:43
  10.7 0.0 collective-permute-start.4
  10.7 2.9 %collective-permute-start.7 = (f32[2,8,128]{2,1,0:T(8,128)S(1)}, f32[2,8,128]{2,1,0:T(8,128)S(1)}, u32[]{:S(2)}, u32[]{:S(2)}) collective-permute-start(f32[2,8,128]{2,1,0:T(8,128)S(1)} %get-tuple-element.37), channel_id=1, source_target_pairs={{0,16},{8,24},{16,0},{24,8},{1,17},{9,25},{17,1},{25,9},{2,18},{10... | collective-permute-start | bytes 24584 | tf_op jit(solution)/shard_map/ppermute | solution.py:43
  13.6 6.2 %collective-permute-done.7.refs_2_ = f32[2,8,128]{2,1,0:T(8,128)S(1)} collective-permute-done((f32[2,8,128]{2,1,0:T(8,128)S(1)}, f32[2,8,128]{2,1,0:T(8,128)S(1)}, u32[]{:S(2)}, u32[]{:S(2)}) %collective-permute-start.7) | collective-permute-done | bytes 8224 | tf_op jit(solution)/shard_map/ppermute | solution.py:43
  19.8 1.2 %collective-permute-start.3 = (bf16[192,384]{1,0:T(8,128)(2,1)S(1)}, bf16[192,384]{1,0:T(8,128)(2,1)S(1)}, u32[]{:S(2)}, u32[]{:S(2)}) collective-permute-start(bf16[192,384]{1,0:T(8,128)(2,1)S(1)} %get-tuple-element.34.refs_4_.refs_0_.right_ref), channel_id=1, source_target_pairs={{0,8},{8,16},{16,24},{24,0},{1,9},{9,17},{17,25},{25,1},{2,10},{10... | collective-permute-start | bytes 442376 | tf_op jit(solution)/shard_map/ppermute | solution.py:43
  20.9 0.0 collective-permute-done.8.refs_3_
  20.9 0.0 collective-permute-start.2
  20.9 0.0 collective-permute-done.6.refs_1_
  20.9 1.6 %collective-permute-start.1 = (bf16[384,192]{1,0:T(8,128)(2,1)S(1)}, bf16[384,192]{1,0:T(8,128)(2,1)S(1)}, u32[]{:S(2)}, u32[]{:S(2)}) collective-permute-start(bf16[384,192]{1,0:T(8,128)(2,1)S(1)} %get-tuple-element.33.refs_0_), channel_id=1, source_target_pairs={{0,4},{2,6},{4,0},{6,2},{1,5},{3,7},{5,1},{7,3},{8,12},{10,14},{12... | collective-permute-start | bytes 442376 | tf_op jit(solution)/shard_map/ppermute | solution.py:732
  22.5 1.3 %shard_map.105 = (bf16[32,4,384]{2,1,0:T(4,128)(2,1)}, f32[3,8,128]{2,1,0:T(8,128)S(1)}) custom-call(f32[6,8,128]{2,1,0:T(8,128)S(1)} %get-tuple-element.36.refs_0_, f32[6,8,128]{2,1,0:T(8,128)S(1)} %collective-permute-done.6.refs_1_, f32[2,8,128]{2,1,0:T(8,128)S(1)} %collective-permute-done.7.refs_2_, f32[6,8,128]{2,1,0:T(8,128)S(1)} %collective-permute-done.8.refs_3_, ...), custom_call_target="tpu_custom_call" | custom-call | flops 1000000 | bytes 1000000 | tf_op jit(solution)/shard_map/pallas_call | solution.py:315
  23.8 5.6 %all-to-all-start = ((bf16[32,4,384]{2,1,0:T(4,128)(2,1)}), bf16[32,4,384]{2,1,0:T(4,128)(2,1)S(1)}, u32[]{:S(2)}, u32[]{:S(2)}) async-start(bf16[32,4,384]{2,1,0:T(4,128)(2,1)} %get-tuple-element.41), calls=%async_computation | async-start | bytes 196608 | tf_op jit(solution)/shard_map/all_to_all | solution.py:770
  29.5 0.0 collective-permute-done.5.refs_7_.refs_3_
  29.5 0.3 collective-permute-start
  29.8 0.0 collective-permute-done.4.refs_6_.refs_2_
  29.8 0.0 collective-permute-done.3.refs_5_.refs_1_
  29.8 0.0 collective-permute-done.2.refs_3_
  29.8 2.6 %collective-permute-done.1.refs_2_ = bf16[384,192]{1,0:T(8,128)(2,1)S(1)} collective-permute-done((bf16[384,192]{1,0:T(8,128)(2,1)S(1)}, bf16[384,192]{1,0:T(8,128)(2,1)S(1)}, u32[]{:S(2)}, u32[]{:S(2)}) %collective-permute-start.1) | collective-permute-done | bytes 147488 | tf_op jit(solution)/shard_map/ppermute | solution.py:732
  32.4 0.0 collective-permute-done.refs_1_
  32.4 0.6 shard_map.104
  33.0 1.7 %collective-permute-start.9 = (bf16[192,384]{1,0:T(8,128)(2,1)S(1)}, bf16[192,384]{1,0:T(8,128)(2,1)S(1)}, u32[]{:S(2)}, u32[]{:S(2)}) collective-permute-start(bf16[192,384]{1,0:T(8,128)(2,1)S(1)} %get-tuple-element.44), channel_id=1, source_target_pairs={{0,1},{1,0},{2,3},{3,2},{4,5},{5,4},{6,7},{7,6},{8,9},{9,8},{10,11... | collective-permute-start | bytes 442376 | tf_op jit(solution)/shard_map/ppermute | solution.py:775
  34.7 0.0 collective-permute-start.17
  34.7 0.5 shard_map.107
  35.3 4.9 %collective-permute-done.9 = bf16[192,384]{1,0:T(8,128)(2,1)S(1)} collective-permute-done((bf16[192,384]{1,0:T(8,128)(2,1)S(1)}, bf16[192,384]{1,0:T(8,128)(2,1)S(1)}, u32[]{:S(2)}, u32[]{:S(2)}) %collective-permute-start.9) | collective-permute-done | bytes 147488 | tf_op jit(solution)/shard_map/ppermute | solution.py:775
  40.2 2.6 %collective-permute-start.12 = (bf16[192,384]{1,0:T(8,128)(2,1)S(1)}, bf16[192,384]{1,0:T(8,128)(2,1)S(1)}, u32[]{:S(2)}, u32[]{:S(2)}) collective-permute-start(bf16[192,384]{1,0:T(8,128)(2,1)S(1)} %add_convert_fusion.refs_0_), channel_id=1, source_target_pairs={{0,24},{8,0},{16,8},{24,16},{1,25},{9,1},{17,9},{25,17},{2,26},{10... | collective-permute-start | bytes 442376 | tf_op jit(solution)/shard_map/ppermute | solution.py:43
  42.8 1.1 %collective-permute-start.11 = (bf16[192,384]{1,0:T(8,128)(2,1)S(1)}, bf16[192,384]{1,0:T(8,128)(2,1)S(1)}, u32[]{:S(2)}, u32[]{:S(2)}) collective-permute-start(bf16[192,384]{1,0:T(8,128)(2,1)S(1)} %add_convert_fusion.refs_0_), channel_id=1, source_target_pairs={{0,16},{8,24},{16,0},{24,8},{1,17},{9,25},{17,1},{25,9},{2,18},{10... | collective-permute-start | bytes 442376 | tf_op jit(solution)/shard_map/ppermute | solution.py:43
  43.9 1.9 %collective-permute-start.10 = (bf16[192,384]{1,0:T(8,128)(2,1)S(1)}, bf16[192,384]{1,0:T(8,128)(2,1)S(1)}, u32[]{:S(2)}, u32[]{:S(2)}) collective-permute-start(bf16[192,384]{1,0:T(8,128)(2,1)S(1)} %add_convert_fusion.refs_0_), channel_id=1, source_target_pairs={{0,8},{8,16},{16,24},{24,0},{1,9},{9,17},{17,25},{25,1},{2,10},{10... | collective-permute-start | bytes 442376 | tf_op jit(solution)/shard_map/ppermute | solution.py:43
  45.8 0.0 collective-permute-start.16
  45.8 0.0 collective-permute-done.17.refs_5_
  45.8 1.7 %collective-permute-start.15 = (f32[3,4,8,128]{3,2,1,0:T(8,128)S(1)}, f32[3,4,8,128]{3,2,1,0:T(8,128)S(1)}, u32[]{:S(2)}, u32[]{:S(2)}) collective-permute-start(f32[3,4,8,128]{3,2,1,0:T(8,128)S(1)} %pad_maximum_fusion.refs_2_), channel_id=1, source_target_pairs={{1,0},{0,1},{3,2},{2,3},{5,4},{4,5},{7,6},{6,7},{9,8},{8,9},{11,10... | collective-permute-start | bytes 147464 | tf_op jit(solution)/shard_map/ppermute | solution.py:722
  47.6 0.0 collective-permute-done.16.refs_4_
  47.6 1.0 %collective-permute-start.14 = (f32[3,4,8,128]{3,2,1,0:T(8,128)S(1)}, f32[3,4,8,128]{3,2,1,0:T(8,128)S(1)}, u32[]{:S(2)}, u32[]{:S(2)}) collective-permute-start(f32[3,4,8,128]{3,2,1,0:T(8,128)S(1)} %pad_maximum_fusion.refs_2_), channel_id=1, source_target_pairs={{7,0},{6,1},{1,2},{0,3},{3,4},{2,5},{5,6},{4,7},{15,8},{14,9},{9,1... | collective-permute-start | bytes 147464 | tf_op jit(solution)/shard_map/ppermute | solution.py:722
  48.6 1.4 %collective-permute-done.15.refs_3_ = f32[3,4,8,128]{3,2,1,0:T(8,128)S(1)} collective-permute-done((f32[3,4,8,128]{3,2,1,0:T(8,128)S(1)}, f32[3,4,8,128]{3,2,1,0:T(8,128)S(1)}, u32[]{:S(2)}, u32[]{:S(2)}) %collective-permute-start.15) | collective-permute-done | bytes 49184 | tf_op jit(solution)/shard_map/ppermute | solution.py:722
  50.0 0.0 collective-permute-start.13
  50.0 2.6 %collective-permute-done.14.refs_1_ = f32[3,4,8,128]{3,2,1,0:T(8,128)S(1)} collective-permute-done((f32[3,4,8,128]{3,2,1,0:T(8,128)S(1)}, f32[3,4,8,128]{3,2,1,0:T(8,128)S(1)}, u32[]{:S(2)}, u32[]{:S(2)}) %collective-permute-start.14) | collective-permute-done | bytes 49184 | tf_op jit(solution)/shard_map/ppermute | solution.py:722
  52.6 0.9 %collective-permute-done.13.refs_0_ = f32[3,4,8,128]{3,2,1,0:T(8,128)S(1)} collective-permute-done((f32[3,4,8,128]{3,2,1,0:T(8,128)S(1)}, f32[3,4,8,128]{3,2,1,0:T(8,128)S(1)}, u32[]{:S(2)}, u32[]{:S(2)}) %collective-permute-start.13) | collective-permute-done | bytes 49184 | tf_op jit(solution)/shard_map/ppermute | solution.py:722
  53.5 0.2 packing.1
  53.8 0.0 all-to-all-done.parts_ref
  53.8 0.3 shard_map.106
  54.1 0.0 copy-start
  54.1 2.7 %sorting.1 = (s32[64,8,128]{2,1,0:T(8,128)S(1)}, s32[16,128]{1,0:T(8,128)S(1)}) custom-call(s32[2,64,1024]{2,1,0:T(8,128)} %bitcast.15), custom_call_target="tpu_custom_call" | custom-call | flops 10000000 | bytes 5000000 | tf_op jit(solution)/shard_map/sorting/pallas_call | solution.py:610
  56.8 0.0 copy-done
  56.8 4.5 %pairs.2.start_ref = f32[3,8,128]{2,1,0:T(8,128)S(1)} custom-call(s32[16,128]{1,0:T(8,128)S(1)} %get-tuple-element.46.range_ref, s32[64,8,128]{2,1,0:T(8,128)S(1)} %get-tuple-element.47.keys_ref, f32[4,8,128]{2,1,0:T(8,128)S(1)} %bitcast.13, s32[2,420,128]{2,1,0:T(8,128)S(1)} %get-tuple-element.48.packed_ref, f32[8,8,128]{2,1,0:T(8,128)S(1)} %get-tuple-element.49.scale_ref, ...), custom_call_target="tpu_custom_call" | custom-call | flops 10000000 | bytes 12000000 | tf_op jit(solution)/shard_map/pairs/pallas_call | solution.py:694
  61.3 0.0 collective-permute-done.12.refs_3_
  61.3 0.0 collective-permute-done.11.refs_2_
  61.4 0.0 collective-permute-done.10.refs_1_
  61.4 0.9 %shard_map.108 = (bf16[192,384]{1,0:T(8,128)(2,1)S(1)}, bf16[4,192,384]{2,1,0:T(8,128)(2,1)S(1)}) custom-call(s32[6,6]{1,0:T(8,128)S(1)} %get-tuple-element.32.pattern_ref, bf16[4,384,192]{2,1,0:T(8,128)(2,1)S(1)} %get-tuple-element.35.table_ref, f32[12,128]{1,0:T(8,128)S(1)} %get-tuple-element.42.rows_ref, f32[1536,128]{1,0:T(8,128)S(1)} %get-tuple-element.43.columns_ref, ...), custom_call_target="tpu_custom_call" | custom-call | flops 1000000 | bytes 1000000 | tf_op jit(solution)/shard_map/pallas_call | solution.py:315
  62.3 1.3 %collective-permute-start.18 = (bf16[192,384]{1,0:T(8,128)(2,1)S(1)}, bf16[192,384]{1,0:T(8,128)(2,1)S(1)}, u32[]{:S(2)}, u32[]{:S(2)}) collective-permute-start(bf16[192,384]{1,0:T(8,128)(2,1)S(1)} %get-tuple-element.54), channel_id=1, source_target_pairs={{0,1},{1,0},{2,3},{3,2},{4,5},{5,4},{6,7},{7,6},{8,9},{9,8},{10,11... | collective-permute-start | bytes 442376 | tf_op jit(solution)/shard_map/ppermute | solution.py:775
  63.6 0.5 shard_map.109.own_ref
  64.2 3.3 %pairs.3 = f32[3,8,128]{2,1,0:T(8,128)} custom-call(s32[16,128]{1,0:T(8,128)S(1)} %get-tuple-element.46.range_ref, s32[64,8,128]{2,1,0:T(8,128)S(1)} %get-tuple-element.47.keys_ref, f32[4,8,128]{2,1,0:T(8,128)S(1)} %bitcast.14, s32[2,420,128]{2,1,0:T(8,128)S(1)} %get-tuple-element.48.packed_ref, f32[8,8,128]{2,1,0:T(8,128)S(1)} %get-tuple-element.49.scale_ref, ...), custom_call_target="tpu_custom_call" | custom-call | flops 10000000 | bytes 7200000 | tf_op jit(solution)/shard_map/pairs/pallas_call | solution.py:694
  67.5 0.0 collective-permute-done.18.got_ref
  67.5 0.7 %shard_map.110 = bf16[192,384]{1,0:T(8,128)(2,1)} custom-call(f32[192,384]{1,0:T(8,128)S(1)} %shard_map.109.own_ref, bf16[192,384]{1,0:T(8,128)(2,1)S(1)} %collective-permute-done.18.got_ref), custom_call_target="tpu_custom_call" | custom-call | flops 1000000 | bytes 1000000 | tf_op jit(solution)/shard_map/pallas_call | solution.py:315
  (5 shorter events, 0.0 us)
Async XLA Ops:
  1.7 19.2 %collective-permute-start.8 = (f32[6,8,128]{2,1,0:T(8,128)S(1)}, f32[6,8,128]{2,1,0:T(8,128)S(1)}, u32[]{:S(2)}, u32[]{:S(2)}) collective-permute-start(f32[6,8,128]{2,1,0:T(8,128)S(1)} %get-tuple-element.36.refs_0_), channel_id=1, source_target_pairs={{0,24},{8,0},{16,8},{24,16},{1,25},{9,1},{17,9},{25,17},{2,26},{10... | collective-permute-start | bytes 73736 | tf_op jit(solution)/shard_map/ppermute | solution.py:43
  6.8 14.1 %collective-permute-start.6 = (f32[6,8,128]{2,1,0:T(8,128)S(1)}, f32[6,8,128]{2,1,0:T(8,128)S(1)}, u32[]{:S(2)}, u32[]{:S(2)}) collective-permute-start(f32[6,8,128]{2,1,0:T(8,128)S(1)} %get-tuple-element.36.refs_0_), channel_id=1, source_target_pairs={{0,8},{8,16},{16,24},{24,0},{1,9},{9,17},{17,25},{25,1},{2,10},{10... | collective-permute-start | bytes 73736 | tf_op jit(solution)/shard_map/ppermute | solution.py:43
  6.8 22.6 %collective-permute-start.5 = (bf16[192,384]{1,0:T(8,128)(2,1)S(1)}, bf16[192,384]{1,0:T(8,128)(2,1)S(1)}, u32[]{:S(2)}, u32[]{:S(2)}) collective-permute-start(bf16[192,384]{1,0:T(8,128)(2,1)S(1)} %get-tuple-element.34.refs_4_.refs_0_.right_ref), channel_id=1, source_target_pairs={{0,24},{8,0},{16,8},{24,16},{1,25},{9,1},{17,9},{25,17},{2,26},{10... | collective-permute-start | bytes 442376 | tf_op jit(solution)/shard_map/ppermute | solution.py:43
  10.7 19.1 %collective-permute-start.4 = (bf16[192,384]{1,0:T(8,128)(2,1)S(1)}, bf16[192,384]{1,0:T(8,128)(2,1)S(1)}, u32[]{:S(2)}, u32[]{:S(2)}) collective-permute-start(bf16[192,384]{1,0:T(8,128)(2,1)S(1)} %get-tuple-element.34.refs_4_.refs_0_.right_ref), channel_id=1, source_target_pairs={{0,16},{8,24},{16,0},{24,8},{1,17},{9,25},{17,1},{25,9},{2,18},{10... | collective-permute-start | bytes 442376 | tf_op jit(solution)/shard_map/ppermute | solution.py:43
  10.7 9.1 %collective-permute-start.7 = (f32[2,8,128]{2,1,0:T(8,128)S(1)}, f32[2,8,128]{2,1,0:T(8,128)S(1)}, u32[]{:S(2)}, u32[]{:S(2)}) collective-permute-start(f32[2,8,128]{2,1,0:T(8,128)S(1)} %get-tuple-element.37), channel_id=1, source_target_pairs={{0,16},{8,24},{16,0},{24,8},{1,17},{9,25},{17,1},{25,9},{2,18},{10... | collective-permute-start | bytes 24584 | tf_op jit(solution)/shard_map/ppermute | solution.py:43
  19.8 10.0 %collective-permute-start.3 = (bf16[192,384]{1,0:T(8,128)(2,1)S(1)}, bf16[192,384]{1,0:T(8,128)(2,1)S(1)}, u32[]{:S(2)}, u32[]{:S(2)}) collective-permute-start(bf16[192,384]{1,0:T(8,128)(2,1)S(1)} %get-tuple-element.34.refs_4_.refs_0_.right_ref), channel_id=1, source_target_pairs={{0,8},{8,16},{16,24},{24,0},{1,9},{9,17},{17,25},{25,1},{2,10},{10... | collective-permute-start | bytes 442376 | tf_op jit(solution)/shard_map/ppermute | solution.py:43
  20.9 8.9 %collective-permute-start.2 = (bf16[384,192]{1,0:T(8,128)(2,1)S(1)}, bf16[384,192]{1,0:T(8,128)(2,1)S(1)}, u32[]{:S(2)}, u32[]{:S(2)}) collective-permute-start(bf16[384,192]{1,0:T(8,128)(2,1)S(1)} %get-tuple-element.33.refs_0_), channel_id=1, source_target_pairs={{0,6},{2,4},{4,2},{6,0},{1,7},{3,5},{5,3},{7,1},{8,14},{10,12},{12... | collective-permute-start | bytes 442376 | tf_op jit(solution)/shard_map/ppermute | solution.py:732
  20.9 11.4 %collective-permute-start.1 = (bf16[384,192]{1,0:T(8,128)(2,1)S(1)}, bf16[384,192]{1,0:T(8,128)(2,1)S(1)}, u32[]{:S(2)}, u32[]{:S(2)}) collective-permute-start(bf16[384,192]{1,0:T(8,128)(2,1)S(1)} %get-tuple-element.33.refs_0_), channel_id=1, source_target_pairs={{0,4},{2,6},{4,0},{6,2},{1,5},{3,7},{5,1},{7,3},{8,12},{10,14},{12... | collective-permute-start | bytes 442376 | tf_op jit(solution)/shard_map/ppermute | solution.py:732
  23.8 29.9 %all-to-all-start = ((bf16[32,4,384]{2,1,0:T(4,128)(2,1)}), bf16[32,4,384]{2,1,0:T(4,128)(2,1)S(1)}, u32[]{:S(2)}, u32[]{:S(2)}) async-start(bf16[32,4,384]{2,1,0:T(4,128)(2,1)} %get-tuple-element.41), calls=%async_computation | async-start | bytes 196608 | tf_op jit(solution)/shard_map/all_to_all | solution.py:770
  29.5 2.9 %collective-permute-start = (bf16[384,192]{1,0:T(8,128)(2,1)S(1)}, bf16[384,192]{1,0:T(8,128)(2,1)S(1)}, u32[]{:S(2)}, u32[]{:S(2)}) collective-permute-start(bf16[384,192]{1,0:T(8,128)(2,1)S(1)} %get-tuple-element.33.refs_0_), channel_id=1, source_target_pairs={{0,2},{2,0},{4,6},{6,4},{1,3},{3,1},{5,7},{7,5},{8,10},{10,8},{12,... | collective-permute-start | bytes 442376 | tf_op jit(solution)/shard_map/ppermute | solution.py:732
  33.0 7.2 %collective-permute-start.9 = (bf16[192,384]{1,0:T(8,128)(2,1)S(1)}, bf16[192,384]{1,0:T(8,128)(2,1)S(1)}, u32[]{:S(2)}, u32[]{:S(2)}) collective-permute-start(bf16[192,384]{1,0:T(8,128)(2,1)S(1)} %get-tuple-element.44), channel_id=1, source_target_pairs={{0,1},{1,0},{2,3},{3,2},{4,5},{5,4},{6,7},{7,6},{8,9},{9,8},{10,11... | collective-permute-start | bytes 442376 | tf_op jit(solution)/shard_map/ppermute | solution.py:775
  34.7 11.1 %collective-permute-start.17 = (f32[3,4,8,128]{3,2,1,0:T(8,128)S(1)}, f32[3,4,8,128]{3,2,1,0:T(8,128)S(1)}, u32[]{:S(2)}, u32[]{:S(2)}) collective-permute-start(f32[3,4,8,128]{3,2,1,0:T(8,128)S(1)} %pad_maximum_fusion.refs_2_), channel_id=1, source_target_pairs={{3,0},{2,1},{5,2},{4,3},{7,4},{6,5},{1,6},{0,7},{11,8},{10,9},{13,... | collective-permute-start | bytes 147464 | tf_op jit(solution)/shard_map/ppermute | solution.py:722
  40.2 21.2 %collective-permute-start.12 = (bf16[192,384]{1,0:T(8,128)(2,1)S(1)}, bf16[192,384]{1,0:T(8,128)(2,1)S(1)}, u32[]{:S(2)}, u32[]{:S(2)}) collective-permute-start(bf16[192,384]{1,0:T(8,128)(2,1)S(1)} %add_convert_fusion.refs_0_), channel_id=1, source_target_pairs={{0,24},{8,0},{16,8},{24,16},{1,25},{9,1},{17,9},{25,17},{2,26},{10... | collective-permute-start | bytes 442376 | tf_op jit(solution)/shard_map/ppermute | solution.py:43
  42.8 18.5 %collective-permute-start.11 = (bf16[192,384]{1,0:T(8,128)(2,1)S(1)}, bf16[192,384]{1,0:T(8,128)(2,1)S(1)}, u32[]{:S(2)}, u32[]{:S(2)}) collective-permute-start(bf16[192,384]{1,0:T(8,128)(2,1)S(1)} %add_convert_fusion.refs_0_), channel_id=1, source_target_pairs={{0,16},{8,24},{16,0},{24,8},{1,17},{9,25},{17,1},{25,9},{2,18},{10... | collective-permute-start | bytes 442376 | tf_op jit(solution)/shard_map/ppermute | solution.py:43
  43.9 17.5 %collective-permute-start.10 = (bf16[192,384]{1,0:T(8,128)(2,1)S(1)}, bf16[192,384]{1,0:T(8,128)(2,1)S(1)}, u32[]{:S(2)}, u32[]{:S(2)}) collective-permute-start(bf16[192,384]{1,0:T(8,128)(2,1)S(1)} %add_convert_fusion.refs_0_), channel_id=1, source_target_pairs={{0,8},{8,16},{16,24},{24,0},{1,9},{9,17},{17,25},{25,1},{2,10},{10... | collective-permute-start | bytes 442376 | tf_op jit(solution)/shard_map/ppermute | solution.py:43
  45.8 1.8 %collective-permute-start.16 = (f32[3,4,8,128]{3,2,1,0:T(8,128)S(1)}, f32[3,4,8,128]{3,2,1,0:T(8,128)S(1)}, u32[]{:S(2)}, u32[]{:S(2)}) collective-permute-start(f32[3,4,8,128]{3,2,1,0:T(8,128)S(1)} %pad_maximum_fusion.refs_2_), channel_id=1, source_target_pairs={{2,0},{3,1},{4,2},{5,3},{6,4},{7,5},{0,6},{1,7},{10,8},{11,9},{12,... | collective-permute-start | bytes 147464 | tf_op jit(solution)/shard_map/ppermute | solution.py:722
  45.8 4.2 %collective-permute-start.15 = (f32[3,4,8,128]{3,2,1,0:T(8,128)S(1)}, f32[3,4,8,128]{3,2,1,0:T(8,128)S(1)}, u32[]{:S(2)}, u32[]{:S(2)}) collective-permute-start(f32[3,4,8,128]{3,2,1,0:T(8,128)S(1)} %pad_maximum_fusion.refs_2_), channel_id=1, source_target_pairs={{1,0},{0,1},{3,2},{2,3},{5,4},{4,5},{7,6},{6,7},{9,8},{8,9},{11,10... | collective-permute-start | bytes 147464 | tf_op jit(solution)/shard_map/ppermute | solution.py:722
  47.6 5.0 %collective-permute-start.14 = (f32[3,4,8,128]{3,2,1,0:T(8,128)S(1)}, f32[3,4,8,128]{3,2,1,0:T(8,128)S(1)}, u32[]{:S(2)}, u32[]{:S(2)}) collective-permute-start(f32[3,4,8,128]{3,2,1,0:T(8,128)S(1)} %pad_maximum_fusion.refs_2_), channel_id=1, source_target_pairs={{7,0},{6,1},{1,2},{0,3},{3,4},{2,5},{5,6},{4,7},{15,8},{14,9},{9,1... | collective-permute-start | bytes 147464 | tf_op jit(solution)/shard_map/ppermute | solution.py:722
  50.0 3.5 %collective-permute-start.13 = (f32[3,4,8,128]{3,2,1,0:T(8,128)S(1)}, f32[3,4,8,128]{3,2,1,0:T(8,128)S(1)}, u32[]{:S(2)}, u32[]{:S(2)}) collective-permute-start(f32[3,4,8,128]{3,2,1,0:T(8,128)S(1)} %pad_maximum_fusion.refs_2_), channel_id=1, source_target_pairs={{6,0},{7,1},{0,2},{1,3},{2,4},{3,5},{4,6},{5,7},{14,8},{15,9},{8,1... | collective-permute-start | bytes 147464 | tf_op jit(solution)/shard_map/ppermute | solution.py:722
  54.1 2.7 %copy-start = (f32[4,1,1,1,1024]{4,3,2,1,0:T(1,128)S(1)}, f32[4,1,1,1,1024]{4,3,2,1,0:T(1,128)}, u32[]{:S(2)}) copy-start(f32[4,1,1,1,1024]{4,3,2,1,0:T(1,128)} %param.13) | copy-start | bytes 49156
  62.3 5.2 %collective-permute-start.18 = (bf16[192,384]{1,0:T(8,128)(2,1)S(1)}, bf16[192,384]{1,0:T(8,128)(2,1)S(1)}, u32[]{:S(2)}, u32[]{:S(2)}) collective-permute-start(bf16[192,384]{1,0:T(8,128)(2,1)S(1)} %get-tuple-element.54), channel_id=1, source_target_pairs={{0,1},{1,0},{2,3},{3,2},{4,5},{5,4},{6,7},{7,6},{8,9},{9,8},{10,11... | collective-permute-start | bytes 442376 | tf_op jit(solution)/shard_map/ppermute | solution.py:775

commit v4 on v3

--- a/solution.py
+++ b/solution.py
@@ -429,18 +429,20 @@
 
 KEY_BITS = 8
 GROUP_BITS = 3
-BATCH = 8
+BATCH = 4
 CHUNK = 24
 
 
-def packing_kernel(inner, *refs):
+def packing_kernel(layers, inner, *refs):
     *near_refs, packed_ref, scale_ref = refs
-    picks = [(near_ref, i) for i in range(inner) for near_ref in near_refs]
+    picks = [
+        (near_ref, k, i) for i in range(inner) for near_ref in near_refs for k in range(layers)
+    ]
     domains = len(picks)
 
     def entry(d, c):
-        near_ref, i = picks[d]
-        return near_ref[i, c]
+        near_ref, k, i = picks[d]
+        return near_ref[k, i, c]
 
     low = [entry(0, c) for c in range(4)]
     high = list(low)
@@ -473,10 +475,11 @@
 
 
 def packing(near):
-    domains = len(near) * near[0].shape[0]
+    layers, inner = near[0].shape[:2]
+    domains = len(near) * layers * inner
     rows = domains * SUB + 2 * (SUB - 1) * domains + CHUNK
     return pl.pallas_call(
-        functools.partial(packing_kernel, near[0].shape[0]),
+        functools.partial(packing_kernel, layers, inner),
         out_shape=(
             jax.ShapeDtypeStruct((2, rows, LANES), jnp.int32),
             jax.ShapeDtypeStruct((8, SUB, LANES), jnp.float32),
@@ -704,23 +707,21 @@
     )(ranges, keys, own, packed, scale, start)
 
 
+def widened(value, axis):
+    count = lax.axis_size(axis)
+    steps = (-1, 0, 1) if count >= 3 else (0, 1) if count == 2 else (0,)
+    return [
+        lax.ppermute(value, axis, [((a + step) % count, a) for a in range(count)])
+        if step
+        else value
+        for step in steps
+    ]
+
+
 def neighbourhood(counts, along_rows):
-    reach = [(-1, 0, 1) if n >= 3 else (0, 1) if n == 2 else (0,) for n in counts]
-    mine = jnp.stack([along_rows[(-i) % counts[0]] for i in reach[0]])
-    columns, layers = counts[1:]
-    near = []
-    for j in reach[1]:
-        for k in reach[2]:
-            if (j, k) == (0, 0):
-                near.append(mine)
-                continue
-            pairs = [
-                (((c + j) % columns) * layers + (g + k) % layers, c * layers + g)
-                for c in range(columns)
-                for g in range(layers)
-            ]
-            near.append(lax.ppermute(mine, ("qc", "grp"), pairs))
-    return near
+    steps = (-1, 0, 1) if counts[0] >= 3 else (0, 1) if counts[0] == 2 else (0,)
+    mine = jnp.stack([along_rows[(-i) % counts[0]] for i in steps])
+    return widened(jnp.stack(widened(mine, "grp")), "qc")
 
 
 def crossed(value, axis):

time: 68.4 us -> 65.8 us (0.962)
  waiting for transfers between devices: 18.7 us -> 16.3 us
  starting transfers between devices: 31.9 us -> 30.7 us
    ppermute x5 -> x3, starting transfers between devices: 2.73 us -> 1.01 us  [widened(): lax.ppermute(value, axis, [((a + step) % count, a) for a in range(count)])]
    ppermute x5 -> x3, waiting for transfers between devices: 4.94 us -> 3.6 us  [widened(): lax.ppermute(value, axis, [((a + step) % count, a) for a in range(count)])]
    ppermute x2, waiting for transfers between devices: 4.92 us -> 3.91 us  [from_layers(): return lax.ppermute(send, 'grp', [(0, 1), (1, 0)])]
  transfers between devices with their start and end apart: 20 -> 18, of which waited for: 6 -> 5; matrix products, arithmetic and copies ran while one was open for 0% -> 0% of each run, Pallas kernels for 21% -> 22%
where the time goes in v4:
time: 65.8 us; the launch traced here: 65.1 us
  starting transfers between devices  30.7 us (47%)
  Pallas kernels  17.3 us (26%)
  waiting for transfers between devices  16.3 us (25%)
  between operations  0.8 us (1%)
    ppermute x9, starting transfers between devices, rotated(): lax.ppermute(of(k), axis, [(i, (i + k) % count) for i in range(count)])  18.7 us
    pallas_call x2, Pallas kernels, pair_forces(): pl.pallas_call(functools.partial(pair_kernel, (packed.shape[1] - CHUNK) /...  8.31 us
    ppermute x9, waiting for transfers between devices, rotated(): lax.ppermute(of(k), axis, [(i, (i + k) % count) for i in range(count)])  6.21 us
    all_to_all x1, starting transfers between devices, per_device(): lax.all_to_all(field, ALL, split_axis=0, concat_axis=0, tiled=True)  5.64 us
    pallas_call x7, Pallas kernels, in_vmem(): pl.pallas_call(kernel, out_shape=out_shape, in_specs=[pl.BlockSpec(memory...  4.93 us
    ppermute x2, waiting for transfers between devices, from_layers(): return lax.ppermute(send, 'grp', [(0, 1), (1, 0)])  3.91 us
    ppermute x3, waiting for transfers between devices, widened(): lax.ppermute(value, axis, [((a + step) % count, a) for a in range(count)])  3.6 us
    ppermute x2, starting transfers between devices, from_layers(): return lax.ppermute(send, 'grp', [(0, 1), (1, 0)])  3.5 us
  transfers between devices with their start and end apart: 18, of which 5 were waited for; matrix products, arithmetic and copies ran while one was open for 0% of the time, Pallas kernels for 22%

profile of v4, /device:TPU:0, one launch (start us, length us, event | category | flops | bytes accessed | tf_op | source)
XLA Modules:
  0.0 65.1 jit_solution(5159227692730598281)
XLA Ops:
  0.6 1.1 %prepare.1 = (bf16[384,192]{1,0:T(8,128)(2,1)S(1)}, bf16[192,384]{1,0:T(8,128)(2,1)S(1)}, f32[6,8,128]{2,1,0:T(8,128)S(1)}, f32[2,8,128]{2,1,0:T(8,128)S(1)}, s3...) custom-call(bf16[384,384]{1,0:T(8,128)(2,1)} %refs_0_.1, ...), custom_call_target="tpu_custom_call" | custom-call | flops 1000000 | bytes 1000000 | tf_op jit(solution)/shard_map/prepare/pallas_call | solution.py:106
  1.7 5.1 %collective-permute-start.8 = (f32[6,8,128]{2,1,0:T(8,128)S(1)}, f32[6,8,128]{2,1,0:T(8,128)S(1)}, u32[]{:S(2)}, u32[]{:S(2)}) collective-permute-start(f32[6,8,128]{2,1,0:T(8,128)S(1)} %get-tuple-element.36.refs_0_), channel_id=1, source_target_pairs={{0,24},{8,0},{16,8},{24,16},{1,25},{9,1},{17,9},{25,17},{2,26},{10... | collective-permute-start | bytes 73736 | tf_op jit(solution)/shard_map/ppermute | solution.py:43
  6.8 0.0 collective-permute-start.6
  6.8 3.8 %collective-permute-start.5 = (bf16[192,384]{1,0:T(8,128)(2,1)S(1)}, bf16[192,384]{1,0:T(8,128)(2,1)S(1)}, u32[]{:S(2)}, u32[]{:S(2)}) collective-permute-start(bf16[192,384]{1,0:T(8,128)(2,1)S(1)} %get-tuple-element.34.refs_4_.refs_0_.right_ref), channel_id=1, source_target_pairs={{0,24},{8,0},{16,8},{24,16},{1,25},{9,1},{17,9},{25,17},{2,26},{10... | collective-permute-start | bytes 442376 | tf_op jit(solution)/shard_map/ppermute | solution.py:43
  10.7 0.0 collective-permute-start.4
  10.7 2.9 %collective-permute-start.7 = (f32[2,8,128]{2,1,0:T(8,128)S(1)}, f32[2,8,128]{2,1,0:T(8,128)S(1)}, u32[]{:S(2)}, u32[]{:S(2)}) collective-permute-start(f32[2,8,128]{2,1,0:T(8,128)S(1)} %get-tuple-element.37), channel_id=1, source_target_pairs={{0,16},{8,24},{16,0},{24,8},{1,17},{9,25},{17,1},{25,9},{2,18},{10... | collective-permute-start | bytes 24584 | tf_op jit(solution)/shard_map/ppermute | solution.py:43
  13.6 6.2 %collective-permute-done.7.refs_2_ = f32[2,8,128]{2,1,0:T(8,128)S(1)} collective-permute-done((f32[2,8,128]{2,1,0:T(8,128)S(1)}, f32[2,8,128]{2,1,0:T(8,128)S(1)}, u32[]{:S(2)}, u32[]{:S(2)}) %collective-permute-start.7) | collective-permute-done | bytes 8224 | tf_op jit(solution)/shard_map/ppermute | solution.py:43
  19.8 1.2 %collective-permute-start.3 = (bf16[192,384]{1,0:T(8,128)(2,1)S(1)}, bf16[192,384]{1,0:T(8,128)(2,1)S(1)}, u32[]{:S(2)}, u32[]{:S(2)}) collective-permute-start(bf16[192,384]{1,0:T(8,128)(2,1)S(1)} %get-tuple-element.34.refs_4_.refs_0_.right_ref), channel_id=1, source_target_pairs={{0,8},{8,16},{16,24},{24,0},{1,9},{9,17},{17,25},{25,1},{2,10},{10... | collective-permute-start | bytes 442376 | tf_op jit(solution)/shard_map/ppermute | solution.py:43
  20.9 0.0 collective-permute-done.8.refs_3_
  20.9 0.0 collective-permute-start.2
  20.9 0.0 collective-permute-done.6.refs_1_
  20.9 1.6 %collective-permute-start.1 = (bf16[384,192]{1,0:T(8,128)(2,1)S(1)}, bf16[384,192]{1,0:T(8,128)(2,1)S(1)}, u32[]{:S(2)}, u32[]{:S(2)}) collective-permute-start(bf16[384,192]{1,0:T(8,128)(2,1)S(1)} %get-tuple-element.33.refs_0_), channel_id=1, source_target_pairs={{0,4},{2,6},{4,0},{6,2},{1,5},{3,7},{5,1},{7,3},{8,12},{10,14},{12... | collective-permute-start | bytes 442376 | tf_op jit(solution)/shard_map/ppermute | solution.py:733
  22.5 1.3 %shard_map.105 = (bf16[32,4,384]{2,1,0:T(4,128)(2,1)}, f32[3,8,128]{2,1,0:T(8,128)S(1)}) custom-call(f32[6,8,128]{2,1,0:T(8,128)S(1)} %get-tuple-element.36.refs_0_, f32[6,8,128]{2,1,0:T(8,128)S(1)} %collective-permute-done.6.refs_1_, f32[2,8,128]{2,1,0:T(8,128)S(1)} %collective-permute-done.7.refs_2_, f32[6,8,128]{2,1,0:T(8,128)S(1)} %collective-permute-done.8.refs_3_, ...), custom_call_target="tpu_custom_call" | custom-call | flops 1000000 | bytes 1000000 | tf_op jit(solution)/shard_map/pallas_call | solution.py:315
  23.8 5.6 %all-to-all-start = ((bf16[32,4,384]{2,1,0:T(4,128)(2,1)}), bf16[32,4,384]{2,1,0:T(4,128)(2,1)S(1)}, u32[]{:S(2)}, u32[]{:S(2)}) async-start(bf16[32,4,384]{2,1,0:T(4,128)(2,1)} %get-tuple-element.41), calls=%async_computation | async-start | bytes 196608 | tf_op jit(solution)/shard_map/all_to_all | solution.py:771
  29.5 0.0 collective-permute-done.5.refs_7_.refs_3_
  29.5 0.3 collective-permute-start
  29.8 0.0 collective-permute-done.4.refs_6_.refs_2_
  29.8 0.0 collective-permute-done.3.refs_5_.refs_1_
  29.8 0.0 collective-permute-done.2.refs_3_
  29.8 2.6 %collective-permute-done.1.refs_2_ = bf16[384,192]{1,0:T(8,128)(2,1)S(1)} collective-permute-done((bf16[384,192]{1,0:T(8,128)(2,1)S(1)}, bf16[384,192]{1,0:T(8,128)(2,1)S(1)}, u32[]{:S(2)}, u32[]{:S(2)}) %collective-permute-start.1) | collective-permute-done | bytes 147488 | tf_op jit(solution)/shard_map/ppermute | solution.py:733
  32.4 0.0 collective-permute-done.refs_1_
  32.4 0.6 shard_map.104
  33.0 1.7 %collective-permute-start.9 = (bf16[192,384]{1,0:T(8,128)(2,1)S(1)}, bf16[192,384]{1,0:T(8,128)(2,1)S(1)}, u32[]{:S(2)}, u32[]{:S(2)}) collective-permute-start(bf16[192,384]{1,0:T(8,128)(2,1)S(1)} %get-tuple-element.44), channel_id=1, source_target_pairs={{0,1},{1,0},{2,3},{3,2},{4,5},{5,4},{6,7},{7,6},{8,9},{9,8},{10,11... | collective-permute-start | bytes 442376 | tf_op jit(solution)/shard_map/ppermute | solution.py:776
  34.7 0.5 collective-permute-start.13
  35.2 0.5 shard_map.107
  35.7 3.9 %collective-permute-done.9 = bf16[192,384]{1,0:T(8,128)(2,1)S(1)} collective-permute-done((bf16[192,384]{1,0:T(8,128)(2,1)S(1)}, bf16[192,384]{1,0:T(8,128)(2,1)S(1)}, u32[]{:S(2)}, u32[]{:S(2)}) %collective-permute-start.9) | collective-permute-done | bytes 147488 | tf_op jit(solution)/shard_map/ppermute | solution.py:776
  39.7 2.6 %collective-permute-start.12 = (bf16[192,384]{1,0:T(8,128)(2,1)S(1)}, bf16[192,384]{1,0:T(8,128)(2,1)S(1)}, u32[]{:S(2)}, u32[]{:S(2)}) collective-permute-start(bf16[192,384]{1,0:T(8,128)(2,1)S(1)} %add_convert_fusion.refs_0_), channel_id=1, source_target_pairs={{0,24},{8,0},{16,8},{24,16},{1,25},{9,1},{17,9},{25,17},{2,26},{10... | collective-permute-start | bytes 442376 | tf_op jit(solution)/shard_map/ppermute | solution.py:43
  42.3 1.1 %collective-permute-start.11 = (bf16[192,384]{1,0:T(8,128)(2,1)S(1)}, bf16[192,384]{1,0:T(8,128)(2,1)S(1)}, u32[]{:S(2)}, u32[]{:S(2)}) collective-permute-start(bf16[192,384]{1,0:T(8,128)(2,1)S(1)} %add_convert_fusion.refs_0_), channel_id=1, source_target_pairs={{0,16},{8,24},{16,0},{24,8},{1,17},{9,25},{17,1},{25,9},{2,18},{10... | collective-permute-start | bytes 442376 | tf_op jit(solution)/shard_map/ppermute | solution.py:43
  43.4 1.9 %collective-permute-start.10 = (bf16[192,384]{1,0:T(8,128)(2,1)S(1)}, bf16[192,384]{1,0:T(8,128)(2,1)S(1)}, u32[]{:S(2)}, u32[]{:S(2)}) collective-permute-start(bf16[192,384]{1,0:T(8,128)(2,1)S(1)} %add_convert_fusion.refs_0_), channel_id=1, source_target_pairs={{0,8},{8,16},{16,24},{24,0},{1,9},{9,17},{17,25},{25,1},{2,10},{10... | collective-permute-start | bytes 442376 | tf_op jit(solution)/shard_map/ppermute | solution.py:43
  45.3 0.0 collective-permute-done.13
  45.3 0.1 collective-permute-start.15
  45.4 0.5 collective-permute-start.14
  45.9 2.5 %collective-permute-done.15.refs_2_ = f32[2,3,4,8,128]{4,3,2,1,0:T(8,128)S(1)} collective-permute-done((f32[2,3,4,8,128]{4,3,2,1,0:T(8,128)S(1)}, f32[2,3,4,8,128]{4,3,2,1,0:T(8,128)S(1)}, u32[]{:S(2)}, u32[]{:S(2)}) %collective-permute-start.15) | collective-permute-done | bytes 98336 | tf_op jit(solution)/shard_map/ppermute | solution.py:714
  48.4 1.1 %collective-permute-done.14.refs_0_ = f32[2,3,4,8,128]{4,3,2,1,0:T(8,128)S(1)} collective-permute-done((f32[2,3,4,8,128]{4,3,2,1,0:T(8,128)S(1)}, f32[2,3,4,8,128]{4,3,2,1,0:T(8,128)S(1)}, u32[]{:S(2)}, u32[]{:S(2)}) %collective-permute-start.14) | collective-permute-done | bytes 98336 | tf_op jit(solution)/shard_map/ppermute | solution.py:714
  49.5 0.2 packing.1
  49.7 0.0 all-to-all-done.parts_ref
  49.7 0.3 shard_map.106
  50.0 0.0 copy-start
  50.1 2.7 %sorting.1 = (s32[64,8,128]{2,1,0:T(8,128)S(1)}, s32[32,128]{1,0:T(8,128)S(1)}) custom-call(s32[2,64,1024]{2,1,0:T(8,128)} %bitcast.18), custom_call_target="tpu_custom_call" | custom-call | flops 10000000 | bytes 5000000 | tf_op jit(solution)/shard_map/sorting/pallas_call | solution.py:613
  52.8 0.0 copy-done
  52.8 4.6 %pairs.2.start_ref = f32[3,8,128]{2,1,0:T(8,128)S(1)} custom-call(s32[32,128]{1,0:T(8,128)S(1)} %get-tuple-element.46.range_ref, s32[64,8,128]{2,1,0:T(8,128)S(1)} %get-tuple-element.47.keys_ref, f32[4,8,128]{2,1,0:T(8,128)S(1)} %bitcast.16, s32[2,420,128]{2,1,0:T(8,128)S(1)} %get-tuple-element.48.packed_ref, f32[8,8,128]{2,1,0:T(8,128)S(1)} %get-tuple-element.49.scale_ref, ...), custom_call_target="tpu_custom_call" | custom-call | flops 10000000 | bytes 12000000 | tf_op jit(solution)/shard_map/pairs/pallas_call | solution.py:697
  57.4 0.0 collective-permute-done.12.refs_3_
  57.4 0.0 collective-permute-done.11.refs_2_
  57.4 0.0 collective-permute-done.10.refs_1_
  57.4 0.9 %shard_map.108 = (bf16[192,384]{1,0:T(8,128)(2,1)S(1)}, bf16[4,192,384]{2,1,0:T(8,128)(2,1)S(1)}) custom-call(s32[6,6]{1,0:T(8,128)S(1)} %get-tuple-element.32.pattern_ref, bf16[4,384,192]{2,1,0:T(8,128)(2,1)S(1)} %get-tuple-element.35.table_ref, f32[12,128]{1,0:T(8,128)S(1)} %get-tuple-element.42.rows_ref, f32[1536,128]{1,0:T(8,128)S(1)} %get-tuple-element.43.columns_ref, ...), custom_call_target="tpu_custom_call" | custom-call | flops 1000000 | bytes 1000000 | tf_op jit(solution)/shard_map/pallas_call | solution.py:315
  58.4 1.8 %collective-permute-start.16 = (bf16[192,384]{1,0:T(8,128)(2,1)S(1)}, bf16[192,384]{1,0:T(8,128)(2,1)S(1)}, u32[]{:S(2)}, u32[]{:S(2)}) collective-permute-start(bf16[192,384]{1,0:T(8,128)(2,1)S(1)} %get-tuple-element.54), channel_id=1, source_target_pairs={{0,1},{1,0},{2,3},{3,2},{4,5},{5,4},{6,7},{7,6},{8,9},{9,8},{10,11... | collective-permute-start | bytes 442376 | tf_op jit(solution)/shard_map/ppermute | solution.py:776
  60.2 0.5 shard_map.109.own_ref
  60.7 3.7 %pairs.3 = f32[3,8,128]{2,1,0:T(8,128)} custom-call(s32[32,128]{1,0:T(8,128)S(1)} %get-tuple-element.46.range_ref, s32[64,8,128]{2,1,0:T(8,128)S(1)} %get-tuple-element.47.keys_ref, f32[4,8,128]{2,1,0:T(8,128)S(1)} %bitcast.17, s32[2,420,128]{2,1,0:T(8,128)S(1)} %get-tuple-element.48.packed_ref, f32[8,8,128]{2,1,0:T(8,128)S(1)} %get-tuple-element.49.scale_ref, ...), custom_call_target="tpu_custom_call" | custom-call | flops 10000000 | bytes 7200000 | tf_op jit(solution)/shard_map/pairs/pallas_call | solution.py:697
  64.4 0.0 collective-permute-done.16.got_ref
  64.4 0.7 %shard_map.110 = bf16[192,384]{1,0:T(8,128)(2,1)} custom-call(f32[192,384]{1,0:T(8,128)S(1)} %shard_map.109.own_ref, bf16[192,384]{1,0:T(8,128)(2,1)S(1)} %collective-permute-done.16.got_ref), custom_call_target="tpu_custom_call" | custom-call | flops 1000000 | bytes 1000000 | tf_op jit(solution)/shard_map/pallas_call | solution.py:315
  (6 shorter events, 0.1 us)
Async XLA Ops:
  1.7 19.2 %collective-permute-start.8 = (f32[6,8,128]{2,1,0:T(8,128)S(1)}, f32[6,8,128]{2,1,0:T(8,128)S(1)}, u32[]{:S(2)}, u32[]{:S(2)}) collective-permute-start(f32[6,8,128]{2,1,0:T(8,128)S(1)} %get-tuple-element.36.refs_0_), channel_id=1, source_target_pairs={{0,24},{8,0},{16,8},{24,16},{1,25},{9,1},{17,9},{25,17},{2,26},{10... | collective-permute-start | bytes 73736 | tf_op jit(solution)/shard_map/ppermute | solution.py:43
  6.8 14.1 %collective-permute-start.6 = (f32[6,8,128]{2,1,0:T(8,128)S(1)}, f32[6,8,128]{2,1,0:T(8,128)S(1)}, u32[]{:S(2)}, u32[]{:S(2)}) collective-permute-start(f32[6,8,128]{2,1,0:T(8,128)S(1)} %get-tuple-element.36.refs_0_), channel_id=1, source_target_pairs={{0,8},{8,16},{16,24},{24,0},{1,9},{9,17},{17,25},{25,1},{2,10},{10... | collective-permute-start | bytes 73736 | tf_op jit(solution)/shard_map/ppermute | solution.py:43
  6.8 22.6 %collective-permute-start.5 = (bf16[192,384]{1,0:T(8,128)(2,1)S(1)}, bf16[192,384]{1,0:T(8,128)(2,1)S(1)}, u32[]{:S(2)}, u32[]{:S(2)}) collective-permute-start(bf16[192,384]{1,0:T(8,128)(2,1)S(1)} %get-tuple-element.34.refs_4_.refs_0_.right_ref), channel_id=1, source_target_pairs={{0,24},{8,0},{16,8},{24,16},{1,25},{9,1},{17,9},{25,17},{2,26},{10... | collective-permute-start | bytes 442376 | tf_op jit(solution)/shard_map/ppermute | solution.py:43
  10.7 19.1 %collective-permute-start.4 = (bf16[192,384]{1,0:T(8,128)(2,1)S(1)}, bf16[192,384]{1,0:T(8,128)(2,1)S(1)}, u32[]{:S(2)}, u32[]{:S(2)}) collective-permute-start(bf16[192,384]{1,0:T(8,128)(2,1)S(1)} %get-tuple-element.34.refs_4_.refs_0_.right_ref), channel_id=1, source_target_pairs={{0,16},{8,24},{16,0},{24,8},{1,17},{9,25},{17,1},{25,9},{2,18},{10... | collective-permute-start | bytes 442376 | tf_op jit(solution)/shard_map/ppermute | solution.py:43
  10.7 9.1 %collective-permute-start.7 = (f32[2,8,128]{2,1,0:T(8,128)S(1)}, f32[2,8,128]{2,1,0:T(8,128)S(1)}, u32[]{:S(2)}, u32[]{:S(2)}) collective-permute-start(f32[2,8,128]{2,1,0:T(8,128)S(1)} %get-tuple-element.37), channel_id=1, source_target_pairs={{0,16},{8,24},{16,0},{24,8},{1,17},{9,25},{17,1},{25,9},{2,18},{10... | collective-permute-start | bytes 24584 | tf_op jit(solution)/shard_map/ppermute | solution.py:43
  19.8 10.0 %collective-permute-start.3 = (bf16[192,384]{1,0:T(8,128)(2,1)S(1)}, bf16[192,384]{1,0:T(8,128)(2,1)S(1)}, u32[]{:S(2)}, u32[]{:S(2)}) collective-permute-start(bf16[192,384]{1,0:T(8,128)(2,1)S(1)} %get-tuple-element.34.refs_4_.refs_0_.right_ref), channel_id=1, source_target_pairs={{0,8},{8,16},{16,24},{24,0},{1,9},{9,17},{17,25},{25,1},{2,10},{10... | collective-permute-start | bytes 442376 | tf_op jit(solution)/shard_map/ppermute | solution.py:43
  20.9 8.9 %collective-permute-start.2 = (bf16[384,192]{1,0:T(8,128)(2,1)S(1)}, bf16[384,192]{1,0:T(8,128)(2,1)S(1)}, u32[]{:S(2)}, u32[]{:S(2)}) collective-permute-start(bf16[384,192]{1,0:T(8,128)(2,1)S(1)} %get-tuple-element.33.refs_0_), channel_id=1, source_target_pairs={{0,6},{2,4},{4,2},{6,0},{1,7},{3,5},{5,3},{7,1},{8,14},{10,12},{12... | collective-permute-start | bytes 442376 | tf_op jit(solution)/shard_map/ppermute | solution.py:733
  20.9 11.4 %collective-permute-start.1 = (bf16[384,192]{1,0:T(8,128)(2,1)S(1)}, bf16[384,192]{1,0:T(8,128)(2,1)S(1)}, u32[]{:S(2)}, u32[]{:S(2)}) collective-permute-start(bf16[384,192]{1,0:T(8,128)(2,1)S(1)} %get-tuple-element.33.refs_0_), channel_id=1, source_target_pairs={{0,4},{2,6},{4,0},{6,2},{1,5},{3,7},{5,1},{7,3},{8,12},{10,14},{12... | collective-permute-start | bytes 442376 | tf_op jit(solution)/shard_map/ppermute | solution.py:733
  23.8 25.9 %all-to-all-start = ((bf16[32,4,384]{2,1,0:T(4,128)(2,1)}), bf16[32,4,384]{2,1,0:T(4,128)(2,1)S(1)}, u32[]{:S(2)}, u32[]{:S(2)}) async-start(bf16[32,4,384]{2,1,0:T(4,128)(2,1)} %get-tuple-element.41), calls=%async_computation | async-start | bytes 196608 | tf_op jit(solution)/shard_map/all_to_all | solution.py:771
  29.5 2.9 %collective-permute-start = (bf16[384,192]{1,0:T(8,128)(2,1)S(1)}, bf16[384,192]{1,0:T(8,128)(2,1)S(1)}, u32[]{:S(2)}, u32[]{:S(2)}) collective-permute-start(bf16[384,192]{1,0:T(8,128)(2,1)S(1)} %get-tuple-element.33.refs_0_), channel_id=1, source_target_pairs={{0,2},{2,0},{4,6},{6,4},{1,3},{3,1},{5,7},{7,5},{8,10},{10,8},{12,... | collective-permute-start | bytes 442376 | tf_op jit(solution)/shard_map/ppermute | solution.py:733
  33.0 6.6 %collective-permute-start.9 = (bf16[192,384]{1,0:T(8,128)(2,1)S(1)}, bf16[192,384]{1,0:T(8,128)(2,1)S(1)}, u32[]{:S(2)}, u32[]{:S(2)}) collective-permute-start(bf16[192,384]{1,0:T(8,128)(2,1)S(1)} %get-tuple-element.44), channel_id=1, source_target_pairs={{0,1},{1,0},{2,3},{3,2},{4,5},{5,4},{6,7},{7,6},{8,9},{9,8},{10,11... | collective-permute-start | bytes 442376 | tf_op jit(solution)/shard_map/ppermute | solution.py:776
  34.7 10.6 %collective-permute-start.13 = (f32[3,4,8,128]{3,2,1,0:T(8,128)S(1)}, f32[3,4,8,128]{3,2,1,0:T(8,128)S(1)}, u32[]{:S(2)}, u32[]{:S(2)}) collective-permute-start(f32[3,4,8,128]{3,2,1,0:T(8,128)S(1)} %get-tuple-element.67), channel_id=1, source_target_pairs={{1,0},{0,1},{3,2},{2,3},{5,4},{4,5},{7,6},{6,7},{9,8},{8,9},{11,10... | collective-permute-start | bytes 147464 | tf_op jit(solution)/shard_map/ppermute | solution.py:714
  39.7 17.7 %collective-permute-start.12 = (bf16[192,384]{1,0:T(8,128)(2,1)S(1)}, bf16[192,384]{1,0:T(8,128)(2,1)S(1)}, u32[]{:S(2)}, u32[]{:S(2)}) collective-permute-start(bf16[192,384]{1,0:T(8,128)(2,1)S(1)} %add_convert_fusion.refs_0_), channel_id=1, source_target_pairs={{0,24},{8,0},{16,8},{24,16},{1,25},{9,1},{17,9},{25,17},{2,26},{10... | collective-permute-start | bytes 442376 | tf_op jit(solution)/shard_map/ppermute | solution.py:43
  42.3 15.1 %collective-permute-start.11 = (bf16[192,384]{1,0:T(8,128)(2,1)S(1)}, bf16[192,384]{1,0:T(8,128)(2,1)S(1)}, u32[]{:S(2)}, u32[]{:S(2)}) collective-permute-start(bf16[192,384]{1,0:T(8,128)(2,1)S(1)} %add_convert_fusion.refs_0_), channel_id=1, source_target_pairs={{0,16},{8,24},{16,0},{24,8},{1,17},{9,25},{17,1},{25,9},{2,18},{10... | collective-permute-start | bytes 442376 | tf_op jit(solution)/shard_map/ppermute | solution.py:43
  43.4 14.1 %collective-permute-start.10 = (bf16[192,384]{1,0:T(8,128)(2,1)S(1)}, bf16[192,384]{1,0:T(8,128)(2,1)S(1)}, u32[]{:S(2)}, u32[]{:S(2)}) collective-permute-start(bf16[192,384]{1,0:T(8,128)(2,1)S(1)} %add_convert_fusion.refs_0_), channel_id=1, source_target_pairs={{0,8},{8,16},{16,24},{24,0},{1,9},{9,17},{17,25},{25,1},{2,10},{10... | collective-permute-start | bytes 442376 | tf_op jit(solution)/shard_map/ppermute | solution.py:43
  45.3 3.1 %collective-permute-start.15 = (f32[2,3,4,8,128]{4,3,2,1,0:T(8,128)S(1)}, f32[2,3,4,8,128]{4,3,2,1,0:T(8,128)S(1)}, u32[]{:S(2)}, u32[]{:S(2)}) collective-permute-start(f32[2,3,4,8,128]{4,3,2,1,0:T(8,128)S(1)} %pad_maximum_fusion.refs_1_), channel_id=1, source_target_pairs={{2,0},{4,2},{6,4},{0,6},{3,1},{5,3},{7,5},{1,7},{10,8},{12,10},{14... | collective-permute-start | bytes 294920 | tf_op jit(solution)/shard_map/ppermute | solution.py:714
  45.4 4.1 %collective-permute-start.14 = (f32[2,3,4,8,128]{4,3,2,1,0:T(8,128)S(1)}, f32[2,3,4,8,128]{4,3,2,1,0:T(8,128)S(1)}, u32[]{:S(2)}, u32[]{:S(2)}) collective-permute-start(f32[2,3,4,8,128]{4,3,2,1,0:T(8,128)S(1)} %pad_maximum_fusion.refs_1_), channel_id=1, source_target_pairs={{6,0},{0,2},{2,4},{4,6},{7,1},{1,3},{3,5},{5,7},{14,8},{8,10},{10,... | collective-permute-start | bytes 294920 | tf_op jit(solution)/shard_map/ppermute | solution.py:714
  50.0 2.7 %copy-start = (f32[4,1,1,1,1024]{4,3,2,1,0:T(1,128)S(1)}, f32[4,1,1,1,1024]{4,3,2,1,0:T(1,128)}, u32[]{:S(2)}) copy-start(f32[4,1,1,1,1024]{4,3,2,1,0:T(1,128)} %param.13) | copy-start | bytes 49156
  58.4 6.1 %collective-permute-start.16 = (bf16[192,384]{1,0:T(8,128)(2,1)S(1)}, bf16[192,384]{1,0:T(8,128)(2,1)S(1)}, u32[]{:S(2)}, u32[]{:S(2)}) collective-permute-start(bf16[192,384]{1,0:T(8,128)(2,1)S(1)} %get-tuple-element.54), channel_id=1, source_target_pairs={{0,1},{1,0},{2,3},{3,2},{4,5},{5,4},{6,7},{7,6},{8,9},{9,8},{10,11... | collective-permute-start | bytes 442376 | tf_op jit(solution)/shard_map/ppermute | solution.py:776
